TPU v7x, 128 devices: a whole 4x4x4 slice. The times are simulated.
128 devices in a mesh: slab: 16 (over x, y), grp: 8 (over z, core).
Axes of the slice: x: 4, y: 4, z: 4, core: 2. Of those that a mesh axis runs over, the one named last changes fastest.
Arguments:
- reference_bricks: bfloat16 [8, 8192, 512], P('grp', 'slab'), may hold values from -6 to 6
- deformed: bfloat16 [32, 16, 128, 512], P('slab', 'grp'), may hold values from -6 to 6
- tap_weights: bfloat16 [8, 32, 16, 128, 512], P(None, 'slab', 'grp')
- valid_voxels: int32 [32, 16, 128, 512], P('slab', 'grp'), may hold values from 0 to 1
- sources: int32 [32, 16, 128], P('slab', 'grp'), may hold values from 0 to 8191, as said below
Outputs:
- coefficients: float32 [3, 32, 16, 128], P(None, 'slab', 'grp')
- residual: float32 [32, 16, 128, 512], P('slab', 'grp')
Inputs may be any that keep to these rules, and one draw needn't show every extreme that they name: The cells of one band (equal y // 2) name each of the band's 8192 reference bricks exactly once; the 512 cells of one block of 2 z-cells of a band take exactly 32 sources from each run of 512 consecutive reference bricks of the band.
All inputs are finite; a program needn't handle non-finite values.
Results may differ from a plain program's by a relative error of at most 0.00035.
Values may be sent and summed in bfloat16 or wider, within the bound.
No kernel may reach another device: no remote copies, remote signals or barrier semaphores. Data moves between devices by JAX's collectives and lax.ppermute only.
A program may use at most 128 MiB of HBM per device.

v0:
```python
import jax
import jax.numpy as jnp
from jax import lax
from jax.sharding import PartitionSpec as P

ITERS = 2


def shifted(block, axis, distance):
    devices = range(lax.axis_size(axis))
    route = [(i - distance, i) for i in devices if i - distance in devices]
    return lax.ppermute(block, axis, route)


def voxel_place():
    place = jnp.arange(512, dtype=jnp.int32)
    return (place // 64, place // 8 % 8, place % 8)


def spline_rows():
    fractions = [(coord.astype(jnp.float32) + 0.5) / 8.0 for coord in voxel_place()]
    basis = []
    for corner in range(8):
        corner_bits = (corner // 4, corner // 2 % 2, corner % 2)
        product = jnp.ones((512,), jnp.float32)
        for bit_value, fraction in zip(corner_bits, fractions):
            product = product * (fraction if bit_value else 1.0 - fraction)
        basis.append(product)
    return jnp.stack(basis)


def shift_ahead(field, stride, at_edge):
    return jnp.where(at_edge, field, jnp.roll(field, -stride, axis=-1))


def shift_behind(field, stride, at_edge):
    return jnp.where(at_edge, field, jnp.roll(field, stride, axis=-1))


def warp_fields(source, weights, image, valid_voxels):
    coords = voxel_place()
    strides = (64, 8, 1)
    warped = jnp.zeros(source.shape, jnp.float32)
    for corner in range(8):
        corner_bits = (corner // 4, corner // 2 % 2, corner % 2)
        tapped = source
        for bit_value, stride, coord in zip(corner_bits, strides, coords):
            if bit_value:
                tapped = shift_ahead(tapped, stride, coord == 7)
        warped = warped + weights[corner].astype(jnp.float32) * tapped
    gradients = jnp.stack(
        [
            0.5
            * (shift_ahead(warped, stride, coord == 7) - shift_behind(warped, stride, coord == 0))
            for stride, coord in zip(strides, coords)
        ]
    )
    valid_mask = valid_voxels.astype(jnp.float32)
    misfit = valid_mask * (warped - image.astype(jnp.float32))
    return (gradients, valid_mask, misfit)


def interpolate(extended, basis):
    z_cells = extended.shape[1] - 1
    y_cells = extended.shape[2] - 1
    terms = []
    for corner in range(8):
        along_z, along_y, along_x = (corner // 4, corner // 2 % 2, corner % 2)
        portion = extended[:, along_z : along_z + z_cells, along_y : along_y + y_cells]
        if along_x:
            portion = jnp.pad(portion[..., 1:], ((0, 0), (0, 0), (0, 0), (0, 1)))
        terms.append(portion)
    return jnp.einsum("tczyx,tv->czyxv", jnp.stack(terms), basis, precision=lax.Precision.HIGHEST)


def corner_terms(force, basis):
    portions = jnp.einsum("czyxv,tv->tczyx", force, basis, precision=lax.Precision.HIGHEST)
    comps, z_cells, y_cells, x_cells = portions.shape[1:]
    summed = jnp.zeros((comps, z_cells + 1, y_cells + 1, x_cells), jnp.float32)
    for corner in range(8):
        along_z, along_y, along_x = (corner // 4, corner // 2 % 2, corner % 2)
        portion = portions[corner]
        if along_x:
            portion = jnp.pad(portion[..., :-1], ((0, 0), (0, 0), (0, 0), (1, 0)))
        summed = summed + jnp.pad(
            portion, ((0, 0), (along_z, 1 - along_z), (along_y, 1 - along_y), (0, 0))
        )
    return summed


def node_values(step_dir, basis):
    above = shifted(step_dir[:, :1], "slab", -1)
    extended = jnp.concatenate([step_dir, above], axis=1)
    beside = shifted(extended[:, :, :1], "grp", -1)
    extended = jnp.concatenate([extended, beside], axis=2)
    return interpolate(extended, basis)


def node_sums(force, basis):
    summed = corner_terms(force, basis)
    z_cells = summed.shape[1] - 1
    y_cells = summed.shape[2] - 1
    from_below = shifted(summed[:, z_cells:], "slab", 1)
    summed = summed[:, :z_cells] + jnp.pad(from_below, ((0, 0), (0, z_cells - 1), (0, 0), (0, 0)))
    from_side = shifted(summed[:, :, y_cells:], "grp", 1)
    return summed[:, :, :y_cells] + jnp.pad(from_side, ((0, 0), (0, 0), (0, y_cells - 1), (0, 0)))


def shards(reference_bricks, deformed, tap_weights, valid_voxels, sources):
    z_cells, y_cells, x_cells = sources.shape
    cell_count = z_cells * y_cells * x_cells
    wanted = sources.reshape(cell_count)
    own_bricks = reference_bricks[0]
    part_rows = lax.all_gather(own_bricks, "slab", axis=0, tiled=True)
    row_count = part_rows.shape[0]
    inside = (wanted >= 0) & (wanted < row_count)
    taken = jnp.take(part_rows, jnp.clip(wanted, 0, row_count - 1), axis=0)
    fetched = jnp.where(inside[:, None], taken, jnp.zeros_like(taken))
    source = fetched.reshape(z_cells, y_cells, x_cells, 512).astype(jnp.float32)
    gradients, valid_mask, misfit = warp_fields(source, tap_weights, deformed, valid_voxels)
    basis = spline_rows()
    counted, square_sum = lax.psum((jnp.sum(valid_mask), jnp.sum(misfit * misfit)), ("slab", "grp"))
    coefficients = jnp.zeros((3, z_cells, y_cells, x_cells), jnp.float32)
    for sweep in range(ITERS):
        if sweep > 0:
            square_sum = lax.psum(jnp.sum(misfit * misfit), ("slab", "grp"))
        spread = square_sum / counted + 1e-06
        robust = 1.0 / (1.0 + misfit * misfit / spread)
        force = (robust * misfit)[None] * gradients
        gradient_nodes = node_sums(force, basis)
        step_dir = -gradient_nodes
        moved = valid_mask * jnp.sum(gradients * node_values(step_dir, basis), axis=0)
        steep_sum = lax.psum(jnp.sum(gradient_nodes * gradient_nodes), ("slab", "grp"))
        curve_sum = lax.psum(jnp.sum(robust * moved * moved), ("slab", "grp"))
        step_size = steep_sum / curve_sum
        coefficients = coefficients + step_size * step_dir
        misfit = misfit + step_size * moved
    return (coefficients, misfit)


def solution(mesh):
    in_specs = (
        P("grp", "slab", None),
        P("slab", "grp", None, None),
        P(None, "slab", "grp", None, None),
        P("slab", "grp", None, None),
        P("slab", "grp", None),
    )
    out_specs = (P(None, "slab", "grp", None), P("slab", "grp", None, None))
    return jax.shard_map(shards, mesh=mesh, in_specs=in_specs, out_specs=out_specs, check_vma=False)
```

profile of v0, /device:TPU:1, one launch (start us, length us, event | category | flops | bytes accessed | tf_op | source)
XLA Modules:
  0.0 454.7 jit_solution(7930035067122343308)
XLA Ops:
  8.8 2.1 convert_reduce_fusion
  11.6 72.2 %all-gather.3.cloned.1.call-done = bf16[1,8192,512]{2,1,0:T(8,128)(2,1)} async-done(((bf16[1,512,512]{2,1,0:T(8,128)(2,1)}), bf16[1,8192,512]{2,1,0:T(8,128)(2,1)}) %all-gather.3.cloned.1.call-update) | async-done | bytes 8388624 | tf_op jit(solution)/shard_map/all_gather | solution.py:114
  83.8 6.4 %gather_fusion = bf16[512,512]{1,0:T(8,128)(2,1)S(1)} fusion(bf16[8192,512]{1,0:T(8,128)(2,1)} %bitcast.242, s32[1024]{0:T(1024)S(1)} %pad_clamp_fusion), kind=kCustom, calls=%fused_computation | custom fusion | bytes 1050624 | tf_op jit(solution)/shard_map/jit(_take)/gather | solution.py:117
  91.8 1.4 slice_bitcast_fusion.26
  93.7 1.3 slice_bitcast_fusion.24
  95.3 2.1 slice_bitcast_fusion.23
  98.3 2.1 slice_bitcast_fusion.25
  101.8 2.6 multiply_reduce_fusion.3
  104.4 1.7 slice_bitcast_fusion.4
  107.0 1.7 slice_bitcast_fusion.2
  108.7 1.7 slice_bitcast_fusion
  112.2 65.2 %all-reduce.38 = (f32[]{:T(128)}, f32[]{:T(128)}) all-reduce(f32[]{:T(128)} %get-tuple-element.16, f32[]{:T(128)} %convert_reduce_fusion), channel_id=1, replica_groups=mesh['slab'=16,'grp'=8] {'slab','grp'}, use_global_device_ids=true, to_apply=%region_1.2 | all-reduce | flops 2 | bytes 16 | tf_op jit(solution)/shard_map/psum | solution.py:122
  179.0 6.7 %fusion.31 = (f32[1,2,2,128,512]{4,3,2,1,0:T(8,128)S(1)}, f32[1,2,2,128,512]{4,3,2,1,0:T(8,128)S(1)}) fusion(f32[1,2,2,128,64]{4,3,2,1,0:T(8,128)} %get-tuple-element.58, f32[1,2,2,128,448]{4,3,2,1,0:T(8,128)} %get-tuple-element.60, f32[1,2,2,128,448]{4,3,2,1,0:T(8,128)} %get-tuple-element.59, f32[1,2,2,128,64]{4,3,2,1,0:T(8,128)} %get-tuple-element.57, ...), kind=kLoop, calls=%fused_computation.74 | loop fusion | flops 12058624 | bytes 16256000 | tf_op jit(solution)/shard_map/mul | solution.py:53
  186.8 2.7 fusion.2
  189.7 2.6 collective-permute-start
  193.2 3.5 collective-permute-start.1
  199.4 3.0 collective-permute-done.2
  202.4 2.3 collective-permute-start.3
  204.7 3.9 collective-permute-done.3
  208.9 2.9 multiply_reduce_fusion.1
  213.8 66.4 %all-reduce.37 = (f32[]{:T(128)}, f32[]{:T(128)}) all-reduce(f32[]{:T(128)} %multiply_reduce_fusion.5, f32[]{:T(128)} %fusion.28), channel_id=1, replica_groups=mesh['slab'=16,'grp'=8] {'slab','grp'}, use_global_device_ids=true, to_apply=%region_5.6 | all-reduce | flops 2 | bytes 16 | tf_op jit(solution)/shard_map/psum | solution.py:133
  281.5 2.2 multiply_reduce_fusion.2
  283.7 63.0 %psum.53 = f32[]{:T(128)} all-reduce(f32[]{:T(128)} %get-tuple-element.10), channel_id=1, replica_groups=mesh['slab'=16,'grp'=8] {'slab','grp'}, use_global_device_ids=true, to_apply=%region_10.11 | all-reduce | flops 1 | bytes 8 | tf_op jit(solution)/shard_map/psum | solution.py:126
  348.2 4.8 %fusion = f32[8,3,2,2,128]{4,0,3,2,1:T(8,128)S(1)} fusion(f32[2,2,128,512]{3,2,1,0:T(8,128)S(1)} %fusion.37, f32[1,2,2,128,512]{4,3,2,1,0:T(8,128)} %copy-done.6, f32[1,2,2,128,512]{4,3,2,1,0:T(8,128)} %copy-done.4, f32[1,2,2,128,512]{4,3,2,1,0:T(8,128)} %copy-done.2, f32[8,512]{1,0:T(8,128)S(1)} %stack.71), kind=kOutput, calls=%fused_computation.3 | convolution fusion | flops 77856768 | bytes 4259840 | tf_op jit(solution)/shard_map/czyxv,tv->tczyx/dot_general | solution.py:77
  353.2 2.3 collective-permute-start.4
  356.3 3.4 collective-permute-start.5
  362.4 3.1 collective-permute-done.6
  365.5 2.3 collective-permute-start.7
  367.8 3.9 collective-permute-done.7
  371.9 2.9 multiply_reduce_fusion
  376.9 66.5 %all-reduce.36 = (f32[]{:T(128)}, f32[]{:T(128)}) all-reduce(f32[]{:T(128)} %multiply_reduce_fusion.4, f32[]{:T(128)} %fusion.29), channel_id=1, replica_groups=mesh['slab'=16,'grp'=8] {'slab','grp'}, use_global_device_ids=true, to_apply=%region_12.13 | all-reduce | flops 2 | bytes 16 | tf_op jit(solution)/shard_map/psum | solution.py:133
  444.7 2.6 multiply_add_fusion
  (115 shorter events, 23.3 us)
Async XLA Ops:
  7.2 76.7 %all-gather.3.cloned.1.call-start = ((), (), s32[]{:S(2)}) async-start(), calls=%async_computation | async-start | bytes 8912896 | tf_op jit(solution)/shard_map/all_gather | solution.py:114
  98.3 3.0 copy-start
  98.3 3.5 copy-start.1
  98.3 3.5 copy-start.18
  178.9 6.8 %copy-start.10 = (f32[1,2,2,128,504]{4,3,2,1,0:T(8,128)S(1)}, f32[1,2,2,128,504]{4,3,2,1,0:T(8,128)}, u32[]{:S(2)}) copy-start(f32[1,2,2,128,504]{4,3,2,1,0:T(8,128)} %get-tuple-element.23) | copy-start | bytes 3096580
  178.9 6.8 %copy-start.11 = (f32[1,2,2,128,504]{4,3,2,1,0:T(8,128)S(1)}, f32[1,2,2,128,504]{4,3,2,1,0:T(8,128)}, u32[]{:S(2)}) copy-start(f32[1,2,2,128,504]{4,3,2,1,0:T(8,128)} %get-tuple-element.24) | copy-start | bytes 3096580
  178.9 6.8 %copy-start.12 = (f32[1,2,2,128,511]{4,3,2,1,0:T(8,128)S(1)}, f32[1,2,2,128,511]{4,3,2,1,0:T(8,128)}, u32[]{:S(2)}) copy-start(f32[1,2,2,128,511]{4,3,2,1,0:T(8,128)} %get-tuple-element.27) | copy-start | bytes 3139588
  178.9 6.8 %copy-start.13 = (f32[1,2,2,128,511]{4,3,2,1,0:T(8,128)S(1)}, f32[1,2,2,128,511]{4,3,2,1,0:T(8,128)}, u32[]{:S(2)}) copy-start(f32[1,2,2,128,511]{4,3,2,1,0:T(8,128)} %get-tuple-element.28) | copy-start | bytes 3139588
  179.0 6.8 %copy-start.14 = (f32[1,2,2,128,8]{4,3,2,1,0:T(8,128)S(1)}, f32[1,2,2,128,8]{4,3,2,1,0:T(8,128)}, u32[]{:S(2)}) copy-start(f32[1,2,2,128,8]{4,3,2,1,0:T(8,128)} %get-tuple-element.21) | copy-start | bytes 49156
  179.0 6.8 %copy-start.15 = (f32[1,2,2,128,8]{4,3,2,1,0:T(8,128)S(1)}, f32[1,2,2,128,8]{4,3,2,1,0:T(8,128)}, u32[]{:S(2)}) copy-start(f32[1,2,2,128,8]{4,3,2,1,0:T(8,128)} %get-tuple-element.22) | copy-start | bytes 49156
  179.0 6.8 %copy-start.16 = (f32[1,2,2,128,1]{4,3,2,1,0:T(8,128)S(1)}, f32[1,2,2,128,1]{4,3,2,1,0:T(8,128)}, u32[]{:S(2)}) copy-start(f32[1,2,2,128,1]{4,3,2,1,0:T(8,128)} %get-tuple-element.25) | copy-start | bytes 6148
  179.0 6.8 %copy-start.17 = (f32[1,2,2,128,1]{4,3,2,1,0:T(8,128)S(1)}, f32[1,2,2,128,1]{4,3,2,1,0:T(8,128)}, u32[]{:S(2)}) copy-start(f32[1,2,2,128,1]{4,3,2,1,0:T(8,128)} %get-tuple-element.26) | copy-start | bytes 6148
  185.7 23.2 %copy-start.2 = (f32[1,2,2,128,512]{4,3,2,1,0:T(8,128)}, f32[1,2,2,128,512]{4,3,2,1,0:T(8,128)S(1)}, u32[]{:S(2)}) copy-start(f32[1,2,2,128,512]{4,3,2,1,0:T(8,128)S(1)} %get-tuple-element.14) | copy-start | bytes 3145732
  186.8 22.1 %copy-start.4 = (f32[1,2,2,128,512]{4,3,2,1,0:T(8,128)}, f32[1,2,2,128,512]{4,3,2,1,0:T(8,128)S(1)}, u32[]{:S(2)}) copy-start(f32[1,2,2,128,512]{4,3,2,1,0:T(8,128)S(1)} %get-tuple-element.19) | copy-start | bytes 3145732
  186.8 22.1 %copy-start.6 = (f32[1,2,2,128,512]{4,3,2,1,0:T(8,128)}, f32[1,2,2,128,512]{4,3,2,1,0:T(8,128)S(1)}, u32[]{:S(2)}) copy-start(f32[1,2,2,128,512]{4,3,2,1,0:T(8,128)S(1)} %get-tuple-element.20) | copy-start | bytes 3145732
  189.7 3.4 collective-permute-start
  193.2 4.2 collective-permute-start.1
  197.4 5.0 %collective-permute-start.2 = (f32[3,1,2,128]{3,2,1,0:T(2,128)S(1)}, f32[3,1,2,128]{3,2,1,0:T(2,128)S(1)}, u32[]{:S(2)}, u32[]{:S(2)}) collective-permute-start(f32[3,1,2,128]{3,2,1,0:T(2,128)S(1)} %slice.415), channel_id=1, source_target_pairs={{8,0},{16,8},{24,16},{32,24},{40,32},{48,40},{56,48},{64,56},{72,6... | collective-permute-start | bytes 9224 | tf_op jit(solution)/shard_map/ppermute | solution.py:12
  202.4 6.2 %collective-permute-start.3 = (f32[3,3,1,128]{3,2,1,0:T(1,128)S(1)}, f32[3,3,1,128]{3,2,1,0:T(1,128)S(1)}, u32[]{:S(2)}, u32[]{:S(2)}) collective-permute-start(f32[3,3,1,128]{3,2,1,0:T(1,128)S(1)} %fusion.58), channel_id=1, source_target_pairs={{1,0},{2,1},{3,2},{4,3},{5,4},{6,5},{7,6},{9,8},{10,9},{11,10},{12... | collective-permute-start | bytes 13832 | tf_op jit(solution)/shard_map/ppermute | solution.py:12
  211.8 1.0 copy-start.9
  348.2 23.7 %copy-start.3 = (f32[1,2,2,128,512]{4,3,2,1,0:T(8,128)S(1)}, f32[1,2,2,128,512]{4,3,2,1,0:T(8,128)}, u32[]{:S(2)}) copy-start(f32[1,2,2,128,512]{4,3,2,1,0:T(8,128)} %copy-done.2) | copy-start | bytes 3145732
  348.2 23.7 %copy-start.5 = (f32[1,2,2,128,512]{4,3,2,1,0:T(8,128)S(1)}, f32[1,2,2,128,512]{4,3,2,1,0:T(8,128)}, u32[]{:S(2)}) copy-start(f32[1,2,2,128,512]{4,3,2,1,0:T(8,128)} %copy-done.4) | copy-start | bytes 3145732
  348.2 23.7 %copy-start.7 = (f32[1,2,2,128,512]{4,3,2,1,0:T(8,128)S(1)}, f32[1,2,2,128,512]{4,3,2,1,0:T(8,128)}, u32[]{:S(2)}) copy-start(f32[1,2,2,128,512]{4,3,2,1,0:T(8,128)} %copy-done.6) | copy-start | bytes 3145732
  353.2 3.1 collective-permute-start.4
  356.3 4.1 collective-permute-start.5
  360.4 5.1 %collective-permute-start.6 = (f32[3,1,2,128]{3,2,1,0:T(2,128)S(1)}, f32[3,1,2,128]{3,2,1,0:T(2,128)S(1)}, u32[]{:S(2)}, u32[]{:S(2)}) collective-permute-start(f32[3,1,2,128]{3,2,1,0:T(2,128)S(1)} %slice.441), channel_id=1, source_target_pairs={{8,0},{16,8},{24,16},{32,24},{40,32},{48,40},{56,48},{64,56},{72,6... | collective-permute-start | bytes 9224 | tf_op jit(solution)/shard_map/ppermute | solution.py:12
  365.5 6.2 %collective-permute-start.7 = (f32[3,3,1,128]{3,2,1,0:T(1,128)S(1)}, f32[3,3,1,128]{3,2,1,0:T(1,128)S(1)}, u32[]{:S(2)}, u32[]{:S(2)}) collective-permute-start(f32[3,3,1,128]{3,2,1,0:T(1,128)S(1)} %fusion.57), channel_id=1, source_target_pairs={{1,0},{2,1},{3,2},{4,3},{5,4},{6,5},{7,6},{9,8},{10,9},{11,10},{12... | collective-permute-start | bytes 13832 | tf_op jit(solution)/shard_map/ppermute | solution.py:12
  374.8 1.0 copy-start.8
Sparse Core Ops, SparseCore 0:
  10.1 73.6 all-gather.2
where the time goes:
time: 456 us; the launch traced here: 455 us
  blocking collectives  261 us (57%)
  waiting for transfers between devices  89.7 us (20%)
  local copies, waits for them, and re-layouts  27.4 us (6%)
  other arithmetic  24.2 us (5%)
  between operations  19.9 us (4%)
  starting transfers between devices  19 us (4%)
  matrix products  13.4 us (3%)
    psum x2, blocking collectives, shards(): lax.psum(jnp.sum(gradient_nodes * gradient_nodes), ('slab', 'grp'))  133 us
    all_gather x1, waiting for transfers between devices, shards(): part_rows = lax.all_gather(own_bricks, 'slab', axis=0, tiled=True)  72.2 us
    psum x1, blocking collectives, shards(): lax.psum((jnp.sum(valid_mask), jnp.sum(misfit * misfit)), ('slab', 'grp'))  65.2 us
    psum x1, blocking collectives, shards(): square_sum = lax.psum(jnp.sum(misfit * misfit), ('slab', 'grp'))  63 us
    ppermute x8, starting transfers between devices, shifted(): return lax.ppermute(block, axis, route)  19 us
    ppermute x8, waiting for transfers between devices, shifted(): return lax.ppermute(block, axis, route)  16.8 us
    concatenate x10, local copies, waits for them, and re-layouts, shift_ahead(): return jnp.where(at_edge, field, jnp.roll(field, -stride, axis=-1))  10.1 us
  transfers between devices with their start and end apart: 9, of which 9 were waited for; matrix products, arithmetic and copies ran while one was open for 1% of the time, Pallas kernels for 0%

commit v1 on v0

v1 whole, which is shorter than its diff:
```python
import jax
import jax.numpy as jnp
from jax import lax
from jax.experimental import pallas as pl
from jax.experimental.pallas import tpu as pltpu
from jax.sharding import PartitionSpec as P

F32 = jnp.float32
BF16 = jnp.bfloat16
I32 = jnp.int32
EVERY = ("slab", "grp")
CELLS = 512
ROWS = 16
BLOCKS = CELLS // ROWS
CHUNKS = 4
NT = (((1,), (1,)), ((), ()))
TN = (((0,), (0,)), ((), ()))
VMEM = pl.BlockSpec(memory_space=pltpu.VMEM)


def iota(shape, axis):
    return lax.broadcasted_iota(I32, shape, axis)


def dot(a, b, dims):
    return lax.dot_general(a, b, dims, preferred_element_type=F32)


def call(body, outs, ins, name, scratch=(), limit=16):
    return pl.pallas_call(
        body,
        out_shape=[jax.ShapeDtypeStruct(s, d) for s, d in outs],
        in_specs=[VMEM] * len(ins),
        out_specs=[VMEM] * len(outs),
        scratch_shapes=list(scratch),
        compiler_params=pltpu.CompilerParams(vmem_limit_bytes=limit << 20),
        name=name,
    )(*ins)


def wanted_body(src_ref, pos_ref, want_ref):
    place = 32 * (lax.axis_index("slab") % 4)
    earlier = (iota((128, 128), 0) < iota((128, 128), 1)).astype(F32).astype(BF16)
    owners = iota((16, 128), 0)
    lanes = iota((128, 128), 0)
    before = jnp.zeros((16, 1), F32)
    want = jnp.zeros((32, 128), F32)
    for r in range(4):
        src = src_ref[r // 2, pl.ds(r % 2, 1), :]
        owner = src >> 9
        row = src & 511
        mine = jnp.where(owners == owner, 1.0, 0.0)
        count = dot(mine.astype(BF16), earlier, (((1,), (0,)), ((), ()))) + before
        before = before + jnp.sum(mine, axis=1, keepdims=True)
        rank = jnp.sum(mine * count, axis=0, keepdims=True).astype(I32)
        pos_ref[pl.ds(r, 1), :] = owner * 32 + rank
        slot = jnp.where(lanes == rank + place, 1.0, 0.0).astype(BF16)
        low = (row & 255).astype(F32)
        high = (row >> 8).astype(F32)
        parts = jnp.concatenate([mine * low, mine * high], axis=0).astype(BF16)
        want = want + dot(parts, slot, NT)
    want_ref[...] = (want[:16] + 256.0 * want[16:]).astype(I32)


def pick_body(want_ref, bricks_ref, out_ref):
    bricks = bricks_ref[0]
    rows = iota((CELLS, 128), 0)
    for r in range(4):
        index = jnp.sum(want_ref[pl.ds(4 * r, 4), :], axis=0, keepdims=True)
        chosen = jnp.where(rows == index, 1.0, 0.0).astype(BF16)
        out_ref[pl.ds(128 * r, 128), :] = dot(chosen, bricks, TN).astype(BF16)


def ahead(field, amount, at_edge):
    return jnp.where(at_edge, field, pltpu.roll(field, 128 - amount, 1))


def behind(field, amount, at_edge):
    return jnp.where(at_edge, field, pltpu.roll(field, amount, 1))


def ahead_z(chunks, swapped, low):
    return [
        jnp.where(low, swapped[j], swapped[j + 1] if j + 1 < CHUNKS else chunks[j])
        for j in range(CHUNKS)
    ]


def behind_z(chunks, swapped, low):
    return [
        jnp.where(low, swapped[j - 1] if j else chunks[j], swapped[j]) for j in range(CHUNKS)
    ]


def swap_halves(chunks):
    return [pltpu.roll(c, 64, 1) for c in chunks]


def columns(j):
    return pl.ds(128 * j, 128)


def spread_sums(values):
    lane = iota((128, 128), 1)
    out = jnp.zeros((128, 128), F32)
    for n, value in enumerate(values):
        total = jnp.sum(jnp.sum(value, axis=0, keepdims=True), axis=1, keepdims=True)
        out = jnp.where(lane == n, total, out)
    return out


def gathered_sums(ref, count):
    sums = jnp.sum(ref[...], axis=0, keepdims=True)
    lane = iota((1, 128), 1)
    return [
        jnp.sum(jnp.where(lane == n, sums, 0.0), axis=1, keepdims=True) for n in range(count)
    ]


def warp_body(pos_ref, recv_ref, image_ref, taps_ref, valid_ref, grad_ref, misfit_ref, sums_ref, source_ref):
    recv = recv_ref[...]
    rows = iota((CELLS, 128), 0)
    for r in range(4):
        chosen = jnp.where(rows == pos_ref[pl.ds(r, 1), :], 1.0, 0.0).astype(BF16)
        source_ref[pl.ds(128 * r, 128), :] = dot(chosen, recv, TN)
    lane = iota((ROWS, 128), 1)
    low = lane < 64
    x_last = (lane & 7) == 7
    x_first = (lane & 7) == 0
    y_last = (lane & 56) == 56
    y_first = (lane & 56) == 0

    def block(i, carry):
        squares, counted = carry
        at = pl.ds(pl.multiple_of(i * ROWS, ROWS), ROWS)
        base = [source_ref[at, columns(j)] for j in range(CHUNKS)]
        along_x = [ahead(c, 1, x_last) for c in base]
        plane = [
            base,
            along_x,
            [ahead(c, 8, y_last) for c in base],
            [ahead(c, 8, y_last) for c in along_x],
        ]
        warped = None
        for tap in range(8):
            chunks = plane[tap % 4]
            if tap >= 4:
                chunks = ahead_z(chunks, swap_halves(chunks), low)
            terms = [
                taps_ref[tap, at, columns(j)].astype(F32) * chunks[j] for j in range(CHUNKS)
            ]
            warped = terms if warped is None else [w + t for w, t in zip(warped, terms)]
        swapped = swap_halves(warped)
        front = ahead_z(warped, swapped, low)
        back = behind_z(warped, swapped, low)
        for j in range(CHUNKS):
            field = warped[j]
            mask = valid_ref[at, columns(j)].astype(F32)
            half = 0.5 * mask
            grad_ref[0, at, columns(j)] = half * (front[j] - back[j])
            grad_ref[1, at, columns(j)] = half * (
                ahead(field, 8, y_last) - behind(field, 8, y_first)
            )
            grad_ref[2, at, columns(j)] = half * (
                ahead(field, 1, x_last) - behind(field, 1, x_first)
            )
            misfit = mask * (field - image_ref[at, columns(j)].astype(F32))
            misfit_ref[at, columns(j)] = misfit
            squares = squares + misfit * misfit
            counted = counted + mask
        return squares, counted

    zero = jnp.zeros((ROWS, 128), F32)
    squares, counted = lax.fori_loop(0, BLOCKS, block, (zero, zero))
    sums_ref[...] = spread_sums([squares, counted])


def high_z(j, shape):
    vz = 2 * j + (iota(shape, 1) >> 6)
    return (vz.astype(F32) + 0.5) * 0.125


def plane_basis(corner, lane):
    vy = (((lane >> 3) & 7).astype(F32) + 0.5) * 0.125
    vx = ((lane & 7).astype(F32) + 0.5) * 0.125
    along_y = (corner & 2) == 2
    along_x = (corner & 1) == 1
    return jnp.where(along_y, vy, 1.0 - vy) * jnp.where(along_x, vx, 1.0 - vx)


def force_nodes(misfit_at, inverse, grad_ref, near_ref, mid_ref, far_ref, parts_ref):
    high = [high_z(j, (1, 128)) for j in range(CHUNKS)]

    def block(i, carry):
        at = pl.ds(pl.multiple_of(i * ROWS, ROWS), ROWS)
        pull = []
        for j in range(CHUNKS):
            misfit = misfit_at(at, j)
            pull.append(misfit / (1.0 + misfit * misfit * inverse))
        for k in range(3):
            force = [pull[j] * grad_ref[k, at, columns(j)] for j in range(CHUNKS)]
            total = (force[0] + force[1]) + (force[2] + force[3])
            upper = (force[0] * high[0] + force[1] * high[1]) + (
                force[2] * high[2] + force[3] * high[3]
            )
            for a, value in enumerate((total - upper, upper)):
                coarse = value.astype(BF16)
                parts_ref[2 * k + a, at, pl.ds(0, 128)] = coarse
                parts_ref[2 * k + a, at, pl.ds(128, 128)] = (value - coarse.astype(F32)).astype(BF16)
        return carry

    lax.fori_loop(0, BLOCKS, block, 0)
    corner = iota((16, 256), 0)
    basis = jnp.where(corner < 4, plane_basis(corner, iota((16, 256), 1)), 0.0).astype(BF16)
    first = iota((16, 128), 1) == 0
    nodes = {}
    for k in range(3):
        for a in range(2):
            parts = dot(basis, parts_ref[2 * k + a], NT)
            for r in range(4):
                own = parts[:, 128 * r : 128 * r + 128]
                moved = jnp.where(first, 0.0, pltpu.roll(own, 1, 1))
                for b in range(2):
                    value = own[2 * b : 2 * b + 1] + moved[2 * b + 1 : 2 * b + 2]
                    key = (r % 2 + b, (r // 2 + a) * 3 + k)
                    nodes[key] = nodes[key] + value if key in nodes else value
    for y, ref in enumerate((near_ref, mid_ref, far_ref)):
        for row in range(9):
            ref[pl.ds(row, 1), :] = nodes[(y, row)]


def first_force_body(sums_ref, misfit_ref, grad_ref, near_ref, mid_ref, far_ref, parts_ref):
    square_sum, counted = gathered_sums(sums_ref, 2)
    inverse = 1.0 / (square_sum / counted + 1e-06)
    force_nodes(
        lambda at, j: misfit_ref[at, columns(j)],
        inverse,
        grad_ref,
        near_ref,
        mid_ref,
        far_ref,
        parts_ref,
    )


def second_spread(sums_ref, steps_ref):
    square_sum, counted = gathered_sums(sums_ref, 2)
    steep, curve, cross, moved_sum = gathered_sums(steps_ref, 4)
    step = steep / curve
    updated = jnp.maximum(square_sum + step * (2.0 * cross + step * moved_sum), 0.0)
    return step, 1.0 / (updated / counted + 1e-06)


def second_force_body(
    sums_ref, steps_ref, misfit_ref, change_ref, grad_ref, near_ref, mid_ref, far_ref, out_ref, parts_ref
):
    step, inverse = second_spread(sums_ref, steps_ref)

    def misfit_at(at, j):
        misfit = misfit_ref[at, columns(j)] + step * change_ref[at, columns(j)]
        out_ref[at, columns(j)] = misfit
        return misfit

    force_nodes(misfit_at, inverse, grad_ref, near_ref, mid_ref, far_ref, parts_ref)


def band_sums(near_ref, mid_ref, far_ref, below_ref, above_ref):
    band = lax.axis_index("grp")
    last = lax.axis_size("grp") - 1
    near = near_ref[...] + jnp.where(band > 0, below_ref[...], 0.0)
    far = jnp.where(band < last, far_ref[...] + above_ref[...], 0.0)
    return near, mid_ref[...], far


def edge_body(near_ref, mid_ref, far_ref, below_ref, above_ref, down_ref, up_ref):
    for y, part in enumerate(band_sums(near_ref, mid_ref, far_ref, below_ref, above_ref)):
        down_ref[pl.ds(3 * y, 3), :] = part[0:3]
        up_ref[pl.ds(3 * y, 3), :] = part[6:9]


def move_body(
    near_ref, mid_ref, far_ref, below_ref, above_ref, under_ref, over_ref,
    sums_ref, steps_ref, misfit_ref, grad_ref, change_ref, out_ref, dir_ref, fields_ref, second,
):
    slab = lax.axis_index("slab")
    last = lax.axis_size("slab") - 1
    bands = band_sums(near_ref, mid_ref, far_ref, below_ref, above_ref)
    steep = jnp.zeros((1, 128), F32)
    nodes = {}
    for y in range(3):
        under = jnp.where(slab > 0, under_ref[pl.ds(3 * y, 3), :], 0.0)
        over = over_ref[pl.ds(3 * y, 3), :]
        layers = (
            bands[y][0:3] + under,
            bands[y][3:6],
            jnp.where(slab < last, bands[y][6:9] + over, 0.0),
        )
        for z, layer in enumerate(layers):
            direction = -layer
            if z < 2 and y < 2:
                for k in range(3):
                    dir_ref[k, z, pl.ds(y, 1), :] = direction[k : k + 1]
                steep = steep + jnp.sum(direction * direction, axis=0, keepdims=True)
            nodes[(z, y)] = jnp.concatenate([direction[k : k + 1] for k in range(3)], axis=1)
    end = (iota((1, 384), 1) & 127) == 127
    shifted = {key: jnp.where(end, 0.0, pltpu.roll(value, 383, 1)) for key, value in nodes.items()}
    rank = iota((24, 256), 0)
    lane = iota((24, 256), 1)
    basis = jnp.where(((rank >> 2) & 1) == (lane >> 7), plane_basis(rank & 3, lane), 0.0).astype(BF16)
    for r in range(4):
        rows = []
        for corner in range(8):
            key = (r // 2 + corner // 4, r % 2 + corner // 2 % 2)
            rows.append(shifted[key] if corner % 2 else nodes[key])
        full = jnp.concatenate(rows, axis=0)
        coarse = full.astype(BF16).astype(F32)
        rest = full - coarse
        middle = rest.astype(BF16).astype(F32)
        split = jnp.concatenate([coarse, middle, rest - middle], axis=0)
        fields_ref[r] = dot(split.astype(BF16), basis, TN)
    if second:
        _, inverse = second_spread(sums_ref, steps_ref)
    else:
        square_sum, counted = gathered_sums(sums_ref, 2)
        inverse = 1.0 / (square_sum / counted + 1e-06)
    high = [high_z(j, (1, 128)) for j in range(CHUNKS)]

    def block(i, carry):
        curve, cross, moved_sum = carry
        at = pl.ds(pl.multiple_of(i * ROWS, ROWS), ROWS)
        r = i // (128 // ROWS)
        x = (i % (128 // ROWS)) * ROWS
        change = [None] * CHUNKS
        for k in range(3):
            cells = pl.ds(pl.multiple_of(128 * k + x, ROWS), ROWS)
            lower = fields_ref[r, cells, pl.ds(0, 128)]
            slope = fields_ref[r, cells, pl.ds(128, 128)] - lower
            for j in range(CHUNKS):
                term = grad_ref[k, at, columns(j)] * (lower + high[j] * slope)
                change[j] = term if k == 0 else change[j] + term
        for j in range(CHUNKS):
            misfit = misfit_ref[at, columns(j)]
            change_ref[at, columns(j)] = change[j]
            square = change[j] * change[j]
            curve = curve + square / (1.0 + misfit * misfit * inverse)
            if not second:
                cross = cross + misfit * change[j]
                moved_sum = moved_sum + square
        return curve, cross, moved_sum

    zero = jnp.zeros((ROWS, 128), F32)
    curve, cross, moved_sum = lax.fori_loop(0, BLOCKS, block, (zero, zero, zero))
    out_ref[...] = spread_sums([steep, curve] + ([] if second else [cross, moved_sum]))


def first_move_body(
    near_ref, mid_ref, far_ref, below_ref, above_ref, under_ref, over_ref,
    sums_ref, misfit_ref, grad_ref, change_ref, out_ref, dir_ref, fields_ref,
):
    move_body(
        near_ref, mid_ref, far_ref, below_ref, above_ref, under_ref, over_ref,
        sums_ref, None, misfit_ref, grad_ref, change_ref, out_ref, dir_ref, fields_ref, False,
    )


def second_move_body(
    near_ref, mid_ref, far_ref, below_ref, above_ref, under_ref, over_ref,
    sums_ref, steps_ref, misfit_ref, grad_ref, change_ref, out_ref, dir_ref, fields_ref,
):
    move_body(
        near_ref, mid_ref, far_ref, below_ref, above_ref, under_ref, over_ref,
        sums_ref, steps_ref, misfit_ref, grad_ref, change_ref, out_ref, dir_ref, fields_ref, True,
    )


def finish_body(first_ref, second_ref, dir0_ref, dir1_ref, misfit_ref, change_ref, coef_ref, out_ref):
    steep, curve = gathered_sums(first_ref, 2)
    step0 = steep / curve
    steep, curve = gathered_sums(second_ref, 2)
    step1 = steep / curve
    coef_ref[...] = step0.reshape(1, 1, 1, 1) * dir0_ref[...] + step1.reshape(1, 1, 1, 1) * dir1_ref[...]
    out_ref[...] = misfit_ref[...] + step1 * change_ref[...]


def around(block, axis, distance):
    size = lax.axis_size(axis)
    return lax.ppermute(block, axis, [(i, (i + distance) % size) for i in range(size)])


def to_all(sums):
    return lax.all_to_all(sums, EVERY, 0, 0, tiled=True)


def halo(near, mid, far):
    below = around(far, "grp", 1)
    above = around(near, "grp", -1)
    down, up = call(edge_body, [((9, 128), F32)] * 2, (near, mid, far, below, above), "edges")
    under = around(up, "slab", 1)
    over = around(down, "slab", -1)
    return below, above, under, over


def shards(reference_bricks, deformed, tap_weights, valid_voxels, sources):
    big = ((CELLS, 512), F32)
    sums_shape = ((128, 128), F32)
    nodes_shape = [((9, 128), F32)] * 3
    dir_shape = ((3, 2, 2, 128), F32)
    grad_shape = ((3, CELLS, 512), F32)
    parts = [pltpu.VMEM((6, CELLS, 256), BF16)]
    fields = [pltpu.VMEM((4, 384, 256), F32)]
    taps = tap_weights.reshape(8, CELLS, 512)
    image = deformed.reshape(CELLS, 512)
    valid = valid_voxels.reshape(CELLS, 512)

    pos, want = call(wanted_body, [((4, 128), I32), ((16, 128), I32)], (sources,), "wanted")
    asked = lax.all_to_all(want, "slab", 0, 0, tiled=True)
    (sent,) = call(pick_body, [((CELLS, 512), BF16)], (asked, reference_bricks), "pick")
    recv = lax.all_to_all(sent, "slab", 0, 0, tiled=True)
    grads, misfit, sums = call(
        warp_body,
        [grad_shape, big, sums_shape],
        (pos, recv, image, taps, valid),
        "warp",
        [pltpu.VMEM((CELLS, 512), F32)],
    )
    sums = to_all(sums)
    near, mid, far = call(first_force_body, nodes_shape, (sums, misfit, grads), "force_first", parts)
    below, above, under, over = halo(near, mid, far)
    change, steps, dir0 = call(
        first_move_body,
        [big, sums_shape, dir_shape],
        (near, mid, far, below, above, under, over, sums, misfit, grads),
        "move_first",
        fields,
    )
    first = to_all(steps)
    near, mid, far, misfit = call(
        second_force_body,
        nodes_shape + [big],
        (sums, first, misfit, change, grads),
        "force_second",
        parts,
    )
    below, above, under, over = halo(near, mid, far)
    change, steps, dir1 = call(
        second_move_body,
        [big, sums_shape, dir_shape],
        (near, mid, far, below, above, under, over, sums, first, misfit, grads),
        "move_second",
        fields,
    )
    second = to_all(steps)
    coefficients, residual = call(
        finish_body, [dir_shape, big], (first, second, dir0, dir1, misfit, change), "finish"
    )
    return (coefficients, residual.reshape(2, 2, 128, 512))


def solution(mesh):
    in_specs = (
        P("grp", "slab", None),
        P("slab", "grp", None, None),
        P(None, "slab", "grp", None, None),
        P("slab", "grp", None, None),
        P("slab", "grp", None),
    )
    out_specs = (P(None, "slab", "grp", None), P("slab", "grp", None, None))
    return jax.shard_map(shards, mesh=mesh, in_specs=in_specs, out_specs=out_specs, check_vma=False)
```

time: 456 us -> 129 us (0.28)
  blocking collectives: 261 us -> 83 us
  waiting for transfers between devices: 89.7 us -> 4.74 us
  other arithmetic: 24.2 us -> 0 us
  local copies, waits for them, and re-layouts: 27.4 us -> 6.17 us
  Pallas kernels: 0 us -> 20.6 us
  between operations: 19.9 us -> 0.67 us
  matrix products: 13.4 us -> 0 us
  starting transfers between devices: 19 us -> 13.2 us
    psum x4 -> x0, blocking collectives: 261 us -> none  [the longest x2 133 us: shards(): lax.psum(jnp.sum(gradient_nodes * gradient_nodes), ('slab', 'grp'))]
    all_to_all x0 -> x5, blocking collectives: none -> 83 us  [the longest x3 57.2 us: to_all(): return lax.all_to_all(sums, EVERY, 0, 0, tiled=True)]
    all_gather x1 -> x0, waiting for transfers between devices: 72.2 us -> none  [shards(): part_rows = lax.all_gather(own_bricks, 'slab', axis=0, tiled=True)]
    pallas_call x0 -> x10, Pallas kernels: none -> 20.6 us  [call(): pl.pallas_call(body, out_shape=[jax.ShapeDtypeStruct(s, d) for s, d in ou...]
    concatenate x16 -> x0, local copies, waits for them, and re-layouts: 17.9 us -> none  [the longest x10 10.1 us: shift_ahead(): return jnp.where(at_edge, field, jnp.roll(field, -stride, axis=-1))]
    dot_general x4 -> x0, matrix products: 13.4 us -> none  [the longest x2 7.55 us: corner_terms(): jnp.einsum('czyxv,tv->tczyx', force, basis, precision=lax.Precision.HIGHEST)]
    ppermute x8, waiting for transfers between devices: 16.8 us -> 4.74 us  [around(): lax.ppermute(block, axis, [(i, (i + distance) % size) for i in range(size)])]
    reduce_sum x7 -> x0, other arithmetic: 10.1 us -> none  [the longest x1 2.57 us: shards(): jnp.sum(misfit * misfit)]
  transfers between devices with their start and end apart: 9 -> 8, of which waited for: 9 -> 4; matrix products, arithmetic and copies ran while one was open for 1% -> 0% of each run, Pallas kernels for 0% -> 0%
where the time goes in v1:
time: 129 us; the launch traced here: 128 us
  blocking collectives  83 us (64%)
  Pallas kernels  20.6 us (16%)
  starting transfers between devices  13.2 us (10%)
  local copies, waits for them, and re-layouts  6.17 us (5%)
  waiting for transfers between devices  4.74 us (4%)
    all_to_all x3, blocking collectives, to_all(): return lax.all_to_all(sums, EVERY, 0, 0, tiled=True)  57.2 us
    pallas_call x10, Pallas kernels, call(): pl.pallas_call(body, out_shape=[jax.ShapeDtypeStruct(s, d) for s, d in ou...  20.6 us
    all_to_all x1, blocking collectives, shards(): asked = lax.all_to_all(want, 'slab', 0, 0, tiled=True)  13.8 us
    ppermute x8, starting transfers between devices, around(): lax.ppermute(block, axis, [(i, (i + distance) % size) for i in range(size)])  13.2 us
    all_to_all x1, blocking collectives, shards(): recv = lax.all_to_all(sent, 'slab', 0, 0, tiled=True)  11.9 us
    unnamed x10, local copies, waits for them, and re-layouts  6.17 us
    ppermute x8, waiting for transfers between devices, around(): lax.ppermute(block, axis, [(i, (i + distance) % size) for i in range(size)])  4.74 us
  transfers between devices with their start and end apart: 8, of which 4 were waited for; matrix products, arithmetic and copies ran while one was open for 0% of the time, Pallas kernels for 0%

profile of v1, /device:TPU:1, one launch (start us, length us, event | category | flops | bytes accessed | tf_op | source)
XLA Modules:
  0.0 128.4 jit_solution(9589157378395721676)
XLA Ops:
  0.6 0.7 copy-done.4
  1.3 0.5 wanted.1
  1.8 13.8 %all_to_all.55 = s32[16,1,128]{2,1,0:T(1,128)S(1)} all-to-all(s32[16,1,128]{2,1,0:T(1,128)S(1)} %bitcast.39), channel_id=1, replica_groups=mesh['slab'=16,'grp'=8] {'slab'}, dimensions={0} | all-to-all | bytes 16384 | tf_op jit(solution)/shard_map/all_to_all | solution.py:416
  15.6 1.0 copy-done.3
  16.7 0.5 pick.1
  17.2 11.9 %all_to_all.56 = bf16[16,32,512]{2,1,0:T(8,128)(2,1)S(1)} all-to-all(bf16[16,32,512]{2,1,0:T(8,128)(2,1)S(1)} %bitcast.24), channel_id=1, replica_groups=mesh['slab'=16,'grp'=8] {'slab'}, dimensions={0} | all-to-all | bytes 1048576 | tf_op jit(solution)/shard_map/all_to_all | solution.py:418
  29.1 2.2 %copy-done = bf16[8,2,2,128,512]{4,3,2,1,0:T(8,128)(2,1)S(1)} copy-done((bf16[8,2,2,128,512]{4,3,2,1,0:T(8,128)(2,1)S(1)}, bf16[8,2,2,128,512]{4,3,2,1,0:T(8,128)(2,1)}, u32[]{:S(2)}) %copy-start) | copy-done | bytes 4194328
  31.3 1.2 copy-done.1
  32.5 1.0 copy-done.2
  33.6 10.9 %warp.1 = (f32[3,512,512]{2,1,0:T(8,128)S(1)}, f32[512,512]{1,0:T(8,128)S(1)}, f32[128,128]{1,0:T(8,128)S(1)}) custom-call(s32[4,128]{1,0:T(4,128)S(1)} %get-tuple-element.26.pos_ref, bf16[512,512]{1,0:T(8,128)(2,1)S(1)} %bitcast.23, bf16[512,512]{1,0:T(8,128)(2,1)S(1)} %bitcast.33, bf16[8,512,512]{2,1,0:T(8,128)(2,1)S(1)} %bitcast.22, s32[512,512]{1,0:T(8,128)S(1)} %bitcast.32), custom_call_target="tpu_custom_call" | custom-call | tf_op jit(solution)/shard_map/warp/pallas_call | solution.py:30
  44.4 18.8 %all_to_all.57 = f32[128,1,128]{2,1,0:T(1,128)S(1)} all-to-all(f32[128,1,128]{2,1,0:T(1,128)S(1)} %bitcast.37), channel_id=1, replica_groups=mesh['slab'=16,'grp'=8] {'slab','grp'}, dimensions={0} | all-to-all | bytes 131072 | tf_op jit(solution)/shard_map/all_to_all | solution.py:391
  63.3 1.9 %force_first.1 = (f32[9,128]{1,0:T(8,128)S(1)}, f32[9,128]{1,0:T(8,128)S(1)}, f32[9,128]{1,0:T(8,128)S(1)}) custom-call(f32[128,128]{1,0:T(8,128)S(1)} %bitcast.25, f32[512,512]{1,0:T(8,128)S(1)} %get-tuple-element.29.misfit_ref, f32[3,512,512]{2,1,0:T(8,128)S(1)} %get-tuple-element.30.grad_ref), custom_call_target="tpu_custom_call" | custom-call | tf_op jit(solution)/shard_map/force_first/pallas_call | solution.py:30
  65.2 1.2 collective-permute-start.1
  66.4 0.5 collective-permute-start
  66.9 1.3 %collective-permute-done.1.above_ref = f32[9,128]{1,0:T(8,128)S(1)} collective-permute-done((f32[9,128]{1,0:T(8,128)S(1)}, f32[9,128]{1,0:T(8,128)S(1)}, u32[]{:S(2)}, u32[]{:S(2)}) %collective-permute-start.1) | collective-permute-done | bytes 4640 | tf_op jit(solution)/shard_map/ppermute | solution.py:387
  68.2 0.0 collective-permute-done.below_ref
  68.3 0.4 collective-permute-start.2
  68.7 4.4 %collective-permute-start.3 = (f32[9,128]{1,0:T(8,128)S(1)}, f32[9,128]{1,0:T(8,128)S(1)}, u32[]{:S(2)}, u32[]{:S(2)}) collective-permute-start(f32[9,128]{1,0:T(8,128)S(1)} %get-tuple-element.35), channel_id=1, source_target_pairs={{0,120},{8,0},{16,8},{24,16},{32,24},{40,32},{48,40},{56,48},{64,5... | collective-permute-start | bytes 13832 | tf_op jit(solution)/shard_map/ppermute | solution.py:387
  73.1 1.0 collective-permute-done.2.under_ref
  74.1 0.0 collective-permute-done.3.over_ref
  74.2 1.9 %move_first.1 = (f32[512,512]{1,0:T(8,128)S(1)}, f32[128,128]{1,0:T(8,128)S(1)}, f32[3,2,2,128]{3,2,1,0:T(2,128)S(1)}) custom-call(f32[9,128]{1,0:T(8,128)S(1)} %get-tuple-element.31.near_ref, f32[9,128]{1,0:T(8,128)S(1)} %get-tuple-element.32.mid_ref, f32[9,128]{1,0:T(8,128)S(1)} %get-tuple-element.33.far_ref, f32[9,128]{1,0:T(8,128)S(1)} %collective-permute-done.below_ref, ...), custom_call_target="tpu_custom_call" | custom-call | tf_op jit(solution)/shard_map/move_first/pallas_call | solution.py:30
  76.0 19.2 %all_to_all.58 = f32[128,1,128]{2,1,0:T(1,128)S(1)} all-to-all(f32[128,1,128]{2,1,0:T(1,128)S(1)} %bitcast.36), channel_id=1, replica_groups=mesh['slab'=16,'grp'=8] {'slab','grp'}, dimensions={0} | all-to-all | bytes 131072 | tf_op jit(solution)/shard_map/all_to_all | solution.py:391
  95.2 2.0 %force_second.1 = (f32[9,128]{1,0:T(8,128)S(1)}, f32[9,128]{1,0:T(8,128)S(1)}, f32[9,128]{1,0:T(8,128)S(1)}, f32[512,512]{1,0:T(8,128)S(1)}) custom-call(f32[128,128]{1,0:T(8,128)S(1)} %bitcast.27, f32[128,128]{1,0:T(8,128)S(1)} %bitcast.29, f32[512,512]{1,0:T(8,128)S(1)} %get-tuple-element.29.misfit_ref, f32[512,512]{1,0:T(8,128)S(1)} %get-tuple-element.37.change_ref, ...), custom_call_target="tpu_custom_call" | custom-call | tf_op jit(solution)/shard_map/force_second/pallas_call | solution.py:30
  97.2 1.2 collective-permute-start.5
  98.5 0.5 collective-permute-start.4
  99.0 1.3 %collective-permute-done.5.above_ref = f32[9,128]{1,0:T(8,128)S(1)} collective-permute-done((f32[9,128]{1,0:T(8,128)S(1)}, f32[9,128]{1,0:T(8,128)S(1)}, u32[]{:S(2)}, u32[]{:S(2)}) %collective-permute-start.5) | collective-permute-done | bytes 4640 | tf_op jit(solution)/shard_map/ppermute | solution.py:387
  100.3 0.4 collective-permute-start.6
  100.7 4.4 %collective-permute-start.7 = (f32[9,128]{1,0:T(8,128)S(1)}, f32[9,128]{1,0:T(8,128)S(1)}, u32[]{:S(2)}, u32[]{:S(2)}) collective-permute-start(f32[9,128]{1,0:T(8,128)S(1)} %get-tuple-element.42), channel_id=1, source_target_pairs={{0,120},{8,0},{16,8},{24,16},{32,24},{40,32},{48,40},{56,48},{64,5... | collective-permute-start | bytes 13832 | tf_op jit(solution)/shard_map/ppermute | solution.py:387
  105.2 1.0 collective-permute-done.6.under_ref
  106.2 1.7 %move_second.1 = (f32[512,512]{1,0:T(8,128)S(1)}, f32[128,128]{1,0:T(8,128)S(1)}, f32[3,2,2,128]{3,2,1,0:T(2,128)S(1)}) custom-call(f32[9,128]{1,0:T(8,128)S(1)} %get-tuple-element.38.near_ref, f32[9,128]{1,0:T(8,128)S(1)} %get-tuple-element.39.mid_ref, f32[9,128]{1,0:T(8,128)S(1)} %get-tuple-element.40.far_ref, ...), custom_call_target="tpu_custom_call" | custom-call | tf_op jit(solution)/shard_map/move_second/pallas_call | solution.py:30
  108.0 19.2 %all_to_all.59 = f32[128,1,128]{2,1,0:T(1,128)S(1)} all-to-all(f32[128,1,128]{2,1,0:T(1,128)S(1)} %bitcast.35), channel_id=1, replica_groups=mesh['slab'=16,'grp'=8] {'slab','grp'}, dimensions={0} | all-to-all | bytes 131072 | tf_op jit(solution)/shard_map/all_to_all | solution.py:391
  127.1 1.3 finish.1
  (9 shorter events, 0.0 us)
Async XLA Ops:
  0.6 0.7 copy-start.4
  15.6 1.0 copy-start.3
  29.1 2.2 %copy-start = (bf16[8,2,2,128,512]{4,3,2,1,0:T(8,128)(2,1)S(1)}, bf16[8,2,2,128,512]{4,3,2,1,0:T(8,128)(2,1)}, u32[]{:S(2)}) copy-start(bf16[8,2,2,128,512]{4,3,2,1,0:T(8,128)(2,1)} %param.7) | copy-start | bytes 12582916
  31.3 1.2 copy-start.1
  32.5 1.0 copy-start.2
  65.2 3.1 %collective-permute-start.1 = (f32[9,128]{1,0:T(8,128)S(1)}, f32[9,128]{1,0:T(8,128)S(1)}, u32[]{:S(2)}, u32[]{:S(2)}) collective-permute-start(f32[9,128]{1,0:T(8,128)S(1)} %get-tuple-element.31.near_ref), channel_id=1, source_target_pairs={{0,7},{1,0},{2,1},{3,2},{4,3},{5,4},{6,5},{7,6},{8,15},{9,8},{10,9... | collective-permute-start | bytes 13832 | tf_op jit(solution)/shard_map/ppermute | solution.py:387
  66.4 1.9 %collective-permute-start = (f32[9,128]{1,0:T(8,128)S(1)}, f32[9,128]{1,0:T(8,128)S(1)}, u32[]{:S(2)}, u32[]{:S(2)}) collective-permute-start(f32[9,128]{1,0:T(8,128)S(1)} %get-tuple-element.33.far_ref), channel_id=1, source_target_pairs={{0,1},{1,2},{2,3},{3,4},{4,5},{5,6},{6,7},{7,0},{8,9},{9,10},{10,1... | collective-permute-start | bytes 13832 | tf_op jit(solution)/shard_map/ppermute | solution.py:387
  68.3 5.9 %collective-permute-start.2 = (f32[9,128]{1,0:T(8,128)S(1)}, f32[9,128]{1,0:T(8,128)S(1)}, u32[]{:S(2)}, u32[]{:S(2)}) collective-permute-start(f32[9,128]{1,0:T(8,128)S(1)} %get-tuple-element.34), channel_id=1, source_target_pairs={{0,8},{8,16},{16,24},{24,32},{32,40},{40,48},{48,56},{56,64},{64,7... | collective-permute-start | bytes 13832 | tf_op jit(solution)/shard_map/ppermute | solution.py:387
  68.7 5.5 %collective-permute-start.3 = (f32[9,128]{1,0:T(8,128)S(1)}, f32[9,128]{1,0:T(8,128)S(1)}, u32[]{:S(2)}, u32[]{:S(2)}) collective-permute-start(f32[9,128]{1,0:T(8,128)S(1)} %get-tuple-element.35), channel_id=1, source_target_pairs={{0,120},{8,0},{16,8},{24,16},{32,24},{40,32},{48,40},{56,48},{64,5... | collective-permute-start | bytes 13832 | tf_op jit(solution)/shard_map/ppermute | solution.py:387
  97.2 3.1 %collective-permute-start.5 = (f32[9,128]{1,0:T(8,128)S(1)}, f32[9,128]{1,0:T(8,128)S(1)}, u32[]{:S(2)}, u32[]{:S(2)}) collective-permute-start(f32[9,128]{1,0:T(8,128)S(1)} %get-tuple-element.38.near_ref), channel_id=1, source_target_pairs={{0,7},{1,0},{2,1},{3,2},{4,3},{5,4},{6,5},{7,6},{8,15},{9,8},{10,9... | collective-permute-start | bytes 13832 | tf_op jit(solution)/shard_map/ppermute | solution.py:387
  98.5 1.9 %collective-permute-start.4 = (f32[9,128]{1,0:T(8,128)S(1)}, f32[9,128]{1,0:T(8,128)S(1)}, u32[]{:S(2)}, u32[]{:S(2)}) collective-permute-start(f32[9,128]{1,0:T(8,128)S(1)} %get-tuple-element.40.far_ref), channel_id=1, source_target_pairs={{0,1},{1,2},{2,3},{3,4},{4,5},{5,6},{6,7},{7,0},{8,9},{9,10},{10,1... | collective-permute-start | bytes 13832 | tf_op jit(solution)/shard_map/ppermute | solution.py:387
  100.3 5.9 %collective-permute-start.6 = (f32[9,128]{1,0:T(8,128)S(1)}, f32[9,128]{1,0:T(8,128)S(1)}, u32[]{:S(2)}, u32[]{:S(2)}) collective-permute-start(f32[9,128]{1,0:T(8,128)S(1)} %get-tuple-element.41), channel_id=1, source_target_pairs={{0,8},{8,16},{16,24},{24,32},{32,40},{40,48},{48,56},{56,64},{64,7... | collective-permute-start | bytes 13832 | tf_op jit(solution)/shard_map/ppermute | solution.py:387
  100.7 5.5 %collective-permute-start.7 = (f32[9,128]{1,0:T(8,128)S(1)}, f32[9,128]{1,0:T(8,128)S(1)}, u32[]{:S(2)}, u32[]{:S(2)}) collective-permute-start(f32[9,128]{1,0:T(8,128)S(1)} %get-tuple-element.42), channel_id=1, source_target_pairs={{0,120},{8,0},{16,8},{24,16},{32,24},{40,32},{48,40},{56,48},{64,5... | collective-permute-start | bytes 13832 | tf_op jit(solution)/shard_map/ppermute | solution.py:387

commit v2 on v1

--- a/solution.py
+++ b/solution.py
@@ -16,6 +16,7 @@
 NT = (((1,), (1,)), ((), ()))
 TN = (((0,), (0,)), ((), ()))
 VMEM = pl.BlockSpec(memory_space=pltpu.VMEM)
+HBM = pl.BlockSpec(memory_space=pltpu.HBM)
 
 
 def iota(shape, axis):
@@ -26,25 +27,30 @@
     return lax.dot_general(a, b, dims, preferred_element_type=F32)
 
 
-def call(body, outs, ins, name, scratch=(), limit=16):
+def call(body, outs, ins, name, scratch=(), limit=16, far=()):
     return pl.pallas_call(
         body,
         out_shape=[jax.ShapeDtypeStruct(s, d) for s, d in outs],
-        in_specs=[VMEM] * len(ins),
+        in_specs=[HBM if n in far else VMEM for n in range(len(ins))],
         out_specs=[VMEM] * len(outs),
         scratch_shapes=list(scratch),
         compiler_params=pltpu.CompilerParams(vmem_limit_bytes=limit << 20),
         name=name,
-    )(*ins)
-
-
-def wanted_body(src_ref, pos_ref, want_ref):
+    )(*[pltpu.with_memory_space_constraint(x, pltpu.HBM) if n in far else x for n, x in enumerate(ins)])
+
+
+def wanted_body(src_hbm, bricks_hbm, pos_ref, want_ref, bricks_ref, src_ref, sems):
+    first = pltpu.make_async_copy(src_hbm, src_ref, sems.at[0])
+    fetch = pltpu.make_async_copy(bricks_hbm, bricks_ref, sems.at[1])
+    first.start()
+    fetch.start()
     place = 32 * (lax.axis_index("slab") % 4)
     earlier = (iota((128, 128), 0) < iota((128, 128), 1)).astype(F32).astype(BF16)
     owners = iota((16, 128), 0)
     lanes = iota((128, 128), 0)
     before = jnp.zeros((16, 1), F32)
     want = jnp.zeros((32, 128), F32)
+    first.wait()
     for r in range(4):
         src = src_ref[r // 2, pl.ds(r % 2, 1), :]
         owner = src >> 9
@@ -60,40 +66,16 @@
         parts = jnp.concatenate([mine * low, mine * high], axis=0).astype(BF16)
         want = want + dot(parts, slot, NT)
     want_ref[...] = (want[:16] + 256.0 * want[16:]).astype(I32)
+    fetch.wait()
 
 
 def pick_body(want_ref, bricks_ref, out_ref):
-    bricks = bricks_ref[0]
+    bricks = bricks_ref[...]
     rows = iota((CELLS, 128), 0)
     for r in range(4):
         index = jnp.sum(want_ref[pl.ds(4 * r, 4), :], axis=0, keepdims=True)
         chosen = jnp.where(rows == index, 1.0, 0.0).astype(BF16)
         out_ref[pl.ds(128 * r, 128), :] = dot(chosen, bricks, TN).astype(BF16)
-
-
-def ahead(field, amount, at_edge):
-    return jnp.where(at_edge, field, pltpu.roll(field, 128 - amount, 1))
-
-
-def behind(field, amount, at_edge):
-    return jnp.where(at_edge, field, pltpu.roll(field, amount, 1))
-
-
-def ahead_z(chunks, swapped, low):
-    return [
-        jnp.where(low, swapped[j], swapped[j + 1] if j + 1 < CHUNKS else chunks[j])
-        for j in range(CHUNKS)
-    ]
-
-
-def behind_z(chunks, swapped, low):
-    return [
-        jnp.where(low, swapped[j - 1] if j else chunks[j], swapped[j]) for j in range(CHUNKS)
-    ]
-
-
-def swap_halves(chunks):
-    return [pltpu.roll(c, 64, 1) for c in chunks]
 
 
 def columns(j):
@@ -117,53 +99,91 @@
     ]
 
 
-def warp_body(pos_ref, recv_ref, image_ref, taps_ref, valid_ref, grad_ref, misfit_ref, sums_ref, source_ref):
+def shift_table(width, last):
+    at = iota((1, 896), 1)
+    tap = (at >> 7) + 1
+    lane = at & 127
+    step_x = jnp.where(((tap & 1) == 1) & ((lane & 7) < 7), 1, 0)
+    step_y = jnp.where(((tap & 2) == 2) & ((lane & 56) < 56), 8, 0)
+    rise = (tap & 4) == 4
+    if last:
+        rise = rise & (lane < 64)
+    target = lane + step_x + step_y + jnp.where(rise, 64, 0)
+    return jnp.where(iota((width, 896), 0) == target, 1.0, 0.0).astype(BF16)
+
+
+def slope_table():
+    at = iota((1, 256), 1)
+    lane = at & 127
+    along_x = at >= 128
+    place = jnp.where(along_x, lane & 7, (lane >> 3) & 7)
+    stride = jnp.where(along_x, 1, 8)
+    front = lane + jnp.where(place < 7, stride, 0)
+    back = lane - jnp.where(place > 0, stride, 0)
+    row = iota((256, 256), 0) & 127
+    return (jnp.where(row == front, 0.5, 0.0) - jnp.where(row == back, 0.5, 0.0)).astype(BF16)
+
+
+def warp_body(
+    pos_ref, recv_ref, image_hbm, taps_hbm, valid_hbm, grad_ref, misfit_ref, sums_ref,
+    source_ref, planes_ref, split_ref, mask_ref, image_ref, taps_ref, valid_ref, sems,
+):
+    copies = []
+    for r in range(4):
+        at = pl.ds(128 * r, 128)
+        copies.append(
+            [
+                pltpu.make_async_copy(taps_hbm.at[:, at], taps_ref.at[:, at], sems.at[0, r]),
+                pltpu.make_async_copy(valid_hbm.at[at], valid_ref.at[at], sems.at[1, r]),
+                pltpu.make_async_copy(image_hbm.at[at], image_ref.at[at], sems.at[2, r]),
+            ]
+        )
+    for group in copies:
+        for copy in group:
+            copy.start()
     recv = recv_ref[...]
     rows = iota((CELLS, 128), 0)
     for r in range(4):
+        at = pl.ds(128 * r, 128)
         chosen = jnp.where(rows == pos_ref[pl.ds(r, 1), :], 1.0, 0.0).astype(BF16)
-        source_ref[pl.ds(128 * r, 128), :] = dot(chosen, recv, TN)
-    lane = iota((ROWS, 128), 1)
-    low = lane < 64
-    x_last = (lane & 7) == 7
-    x_first = (lane & 7) == 0
-    y_last = (lane & 56) == 56
-    y_first = (lane & 56) == 0
+        picked = dot(chosen, recv, TN)
+        planes_ref[0, at, :] = picked
+        source_ref[at, :] = picked.astype(BF16)
+    inner = shift_table(256, False)
+    outer = shift_table(128, True)
+    for j in range(CHUNKS):
+        if j + 1 < CHUNKS:
+            shifted = dot(source_ref[:, pl.ds(128 * j, 256)], inner, (((1,), (0,)), ((), ())))
+        else:
+            shifted = dot(source_ref[:, columns(j)], outer, (((1,), (0,)), ((), ())))
+        for tap in range(7):
+            planes_ref[tap + 1, :, columns(j)] = shifted[:, 128 * tap : 128 * tap + 128]
+    low = iota((ROWS, 128), 1) < 64
 
     def block(i, carry):
         squares, counted = carry
         at = pl.ds(pl.multiple_of(i * ROWS, ROWS), ROWS)
-        base = [source_ref[at, columns(j)] for j in range(CHUNKS)]
-        along_x = [ahead(c, 1, x_last) for c in base]
-        plane = [
-            base,
-            along_x,
-            [ahead(c, 8, y_last) for c in base],
-            [ahead(c, 8, y_last) for c in along_x],
-        ]
-        warped = None
-        for tap in range(8):
-            chunks = plane[tap % 4]
-            if tap >= 4:
-                chunks = ahead_z(chunks, swap_halves(chunks), low)
+        warped = []
+        for j in range(CHUNKS):
             terms = [
-                taps_ref[tap, at, columns(j)].astype(F32) * chunks[j] for j in range(CHUNKS)
+                taps_ref[tap, at, columns(j)].astype(F32) * planes_ref[tap, at, columns(j)]
+                for tap in range(8)
             ]
-            warped = terms if warped is None else [w + t for w, t in zip(warped, terms)]
-        swapped = swap_halves(warped)
-        front = ahead_z(warped, swapped, low)
-        back = behind_z(warped, swapped, low)
+            warped.append(
+                ((terms[0] + terms[1]) + (terms[2] + terms[3]))
+                + ((terms[4] + terms[5]) + (terms[6] + terms[7]))
+            )
+        swapped = [pltpu.roll(c, 64, 1) for c in warped]
         for j in range(CHUNKS):
             field = warped[j]
             mask = valid_ref[at, columns(j)].astype(F32)
-            half = 0.5 * mask
-            grad_ref[0, at, columns(j)] = half * (front[j] - back[j])
-            grad_ref[1, at, columns(j)] = half * (
-                ahead(field, 8, y_last) - behind(field, 8, y_first)
-            )
-            grad_ref[2, at, columns(j)] = half * (
-                ahead(field, 1, x_last) - behind(field, 1, x_first)
-            )
+            mask_ref[at, columns(j)] = mask
+            front = jnp.where(low, swapped[j], swapped[j + 1] if j + 1 < CHUNKS else field)
+            back = jnp.where(low, swapped[j - 1] if j else field, swapped[j])
+            grad_ref[0, at, columns(j)] = (0.5 * mask) * (front - back)
+            coarse = field.astype(BF16)
+            split_ref[at, pl.ds(256 * j, 128)] = coarse
+            split_ref[at, pl.ds(256 * j + 128, 128)] = (field - coarse.astype(F32)).astype(BF16)
             misfit = mask * (field - image_ref[at, columns(j)].astype(F32))
             misfit_ref[at, columns(j)] = misfit
             squares = squares + misfit * misfit
@@ -171,8 +191,18 @@
         return squares, counted
 
     zero = jnp.zeros((ROWS, 128), F32)
-    squares, counted = lax.fori_loop(0, BLOCKS, block, (zero, zero))
-    sums_ref[...] = spread_sums([squares, counted])
+    carry = (zero, zero)
+    for r in range(4):
+        for copy in copies[r]:
+            copy.wait()
+        carry = lax.fori_loop(128 * r // ROWS, 128 * (r + 1) // ROWS, block, carry)
+    sums_ref[...] = spread_sums(list(carry))
+    table = slope_table()
+    for j in range(CHUNKS):
+        slopes = dot(split_ref[:, pl.ds(256 * j, 256)], table, (((1,), (0,)), ((), ())))
+        mask = mask_ref[:, columns(j)]
+        grad_ref[1, :, columns(j)] = mask * slopes[:, :128]
+        grad_ref[2, :, columns(j)] = mask * slopes[:, 128:]
 
 
 def high_z(j, shape):
@@ -412,16 +442,34 @@
     image = deformed.reshape(CELLS, 512)
     valid = valid_voxels.reshape(CELLS, 512)
 
-    pos, want = call(wanted_body, [((4, 128), I32), ((16, 128), I32)], (sources,), "wanted")
+    pos, want, bricks = call(
+        wanted_body,
+        [((4, 128), I32), ((16, 128), I32), ((CELLS, 512), BF16)],
+        (sources, reference_bricks.reshape(CELLS, 512)),
+        "wanted",
+        [pltpu.VMEM((2, 2, 128), I32), pltpu.SemaphoreType.DMA((2,))],
+        far=(0, 1),
+    )
     asked = lax.all_to_all(want, "slab", 0, 0, tiled=True)
-    (sent,) = call(pick_body, [((CELLS, 512), BF16)], (asked, reference_bricks), "pick")
+    (sent,) = call(pick_body, [((CELLS, 512), BF16)], (asked, bricks), "pick")
     recv = lax.all_to_all(sent, "slab", 0, 0, tiled=True)
     grads, misfit, sums = call(
         warp_body,
         [grad_shape, big, sums_shape],
         (pos, recv, image, taps, valid),
         "warp",
-        [pltpu.VMEM((CELLS, 512), F32)],
+        [
+            pltpu.VMEM((CELLS, 512), BF16),
+            pltpu.VMEM((8, CELLS, 512), F32),
+            pltpu.VMEM((CELLS, 1024), BF16),
+            pltpu.VMEM((CELLS, 512), F32),
+            pltpu.VMEM((CELLS, 512), BF16),
+            pltpu.VMEM((8, CELLS, 512), BF16),
+            pltpu.VMEM((CELLS, 512), I32),
+            pltpu.SemaphoreType.DMA((3, 4)),
+        ],
+        40,
+        (2, 3, 4),
     )
     sums = to_all(sums)
     near, mid, far = call(first_force_body, nodes_shape, (sums, misfit, grads), "force_first", parts)

time: 129 us -> 118 us (0.915)
  local copies, waits for them, and re-layouts: 6.17 us -> 0 us
  Pallas kernels: 20.6 us -> 16.1 us
    unnamed x10 -> x0, local copies, waits for them, and re-layouts: 6.17 us -> none
    pallas_call x10, Pallas kernels: 20.6 us -> 16.1 us  [call(): pl.pallas_call(body, out_shape=[jax.ShapeDtypeStruct(s, d) for s, d in ou...]
where the time goes in v2:
time: 118 us
  blocking collectives  83 us (70%)
  Pallas kernels  16.1 us (14%)
  starting transfers between devices  13.2 us (11%)
  waiting for transfers between devices  4.74 us (4%)
    all_to_all x3, blocking collectives, to_all(): return lax.all_to_all(sums, EVERY, 0, 0, tiled=True)  57.2 us
    pallas_call x10, Pallas kernels, call(): pl.pallas_call(body, out_shape=[jax.ShapeDtypeStruct(s, d) for s, d in ou...  16.1 us
    all_to_all x1, blocking collectives, shards(): asked = lax.all_to_all(want, 'slab', 0, 0, tiled=True)  13.8 us
    ppermute x8, starting transfers between devices, around(): lax.ppermute(block, axis, [(i, (i + distance) % size) for i in range(size)])  13.2 us
    all_to_all x1, blocking collectives, shards(): recv = lax.all_to_all(sent, 'slab', 0, 0, tiled=True)  11.9 us
    ppermute x8, waiting for transfers between devices, around(): lax.ppermute(block, axis, [(i, (i + distance) % size) for i in range(size)])  4.74 us
  transfers between devices with their start and end apart: 8, of which 4 were waited for; matrix products, arithmetic and copies ran while one was open for 0% of the time, Pallas kernels for 0%

profile of v2, /device:TPU:1, one launch (start us, length us, event | category | flops | bytes accessed | tf_op | source)
XLA Modules:
  0.0 117.7 jit_solution(1741346959798141989)
XLA Ops:
  0.6 1.2 %wanted.1 = (s32[4,128]{1,0:T(4,128)S(1)}, s32[16,128]{1,0:T(8,128)S(1)}, bf16[512,512]{1,0:T(8,128)(2,1)S(1)}) custom-call(s32[2,2,128]{2,1,0:T(2,128)} %src_hbm.1, bf16[512,512]{1,0:T(8,128)(2,1)} %bitcast.41), custom_call_target="tpu_custom_call" | custom-call | tf_op jit(solution)/shard_map/wanted/pallas_call | solution.py:31
  1.9 13.8 %all_to_all.55 = s32[16,1,128]{2,1,0:T(1,128)S(1)} all-to-all(s32[16,1,128]{2,1,0:T(1,128)S(1)} %bitcast.37), channel_id=1, replica_groups=mesh['slab'=16,'grp'=8] {'slab'}, dimensions={0} | all-to-all | bytes 16384 | tf_op jit(solution)/shard_map/all_to_all | solution.py:453
  15.7 0.5 pick.1
  16.2 11.9 %all_to_all.56 = bf16[16,32,512]{2,1,0:T(8,128)(2,1)S(1)} all-to-all(bf16[16,32,512]{2,1,0:T(8,128)(2,1)S(1)} %bitcast.24), channel_id=1, replica_groups=mesh['slab'=16,'grp'=8] {'slab'}, dimensions={0} | all-to-all | bytes 1048576 | tf_op jit(solution)/shard_map/all_to_all | solution.py:455
  28.1 5.7 %warp.1 = (f32[3,512,512]{2,1,0:T(8,128)S(1)}, f32[512,512]{1,0:T(8,128)S(1)}, f32[128,128]{1,0:T(8,128)S(1)}) custom-call(s32[4,128]{1,0:T(4,128)S(1)} %get-tuple-element.27.pos_ref, bf16[512,512]{1,0:T(8,128)(2,1)S(1)} %bitcast.23, bf16[512,512]{1,0:T(8,128)(2,1)} %bitcast.40, bf16[8,512,512]{2,1,0:T(8,128)(2,1)} %bitcast.38, s32[512,512]{1,0:T(8,128)} %bitcast.39), custom_call_target="tpu_custom_call" | custom-call | tf_op jit(solution)/shard_map/warp/pallas_call | solution.py:31
  33.8 18.8 %all_to_all.57 = f32[128,1,128]{2,1,0:T(1,128)S(1)} all-to-all(f32[128,1,128]{2,1,0:T(1,128)S(1)} %bitcast.35), channel_id=1, replica_groups=mesh['slab'=16,'grp'=8] {'slab','grp'}, dimensions={0} | all-to-all | bytes 131072 | tf_op jit(solution)/shard_map/all_to_all | solution.py:421
  52.6 1.9 %force_first.1 = (f32[9,128]{1,0:T(8,128)S(1)}, f32[9,128]{1,0:T(8,128)S(1)}, f32[9,128]{1,0:T(8,128)S(1)}) custom-call(f32[128,128]{1,0:T(8,128)S(1)} %bitcast.25, f32[512,512]{1,0:T(8,128)S(1)} %get-tuple-element.31.misfit_ref, f32[3,512,512]{2,1,0:T(8,128)S(1)} %get-tuple-element.32.grad_ref), custom_call_target="tpu_custom_call" | custom-call | tf_op jit(solution)/shard_map/force_first/pallas_call | solution.py:31
  54.5 1.2 %collective-permute-start.1 = (f32[9,128]{1,0:T(8,128)S(1)}, f32[9,128]{1,0:T(8,128)S(1)}, u32[]{:S(2)}, u32[]{:S(2)}) collective-permute-start(f32[9,128]{1,0:T(8,128)S(1)} %get-tuple-element.33.near_ref), channel_id=1, source_target_pairs={{0,7},{1,0},{2,1},{3,2},{4,3},{5,4},{6,5},{7,6},{8,15},{9,8},{10,9... | collective-permute-start | bytes 13832 | tf_op jit(solution)/shard_map/ppermute | solution.py:417
  55.7 0.5 collective-permute-start
  56.2 1.3 %collective-permute-done.1.above_ref = f32[9,128]{1,0:T(8,128)S(1)} collective-permute-done((f32[9,128]{1,0:T(8,128)S(1)}, f32[9,128]{1,0:T(8,128)S(1)}, u32[]{:S(2)}, u32[]{:S(2)}) %collective-permute-start.1) | collective-permute-done | bytes 4640 | tf_op jit(solution)/shard_map/ppermute | solution.py:417
  57.6 0.0 collective-permute-done.below_ref
  57.6 0.4 collective-permute-start.2
  58.0 4.4 %collective-permute-start.3 = (f32[9,128]{1,0:T(8,128)S(1)}, f32[9,128]{1,0:T(8,128)S(1)}, u32[]{:S(2)}, u32[]{:S(2)}) collective-permute-start(f32[9,128]{1,0:T(8,128)S(1)} %get-tuple-element.37), channel_id=1, source_target_pairs={{0,120},{8,0},{16,8},{24,16},{32,24},{40,32},{48,40},{56,48},{64,5... | collective-permute-start | bytes 13832 | tf_op jit(solution)/shard_map/ppermute | solution.py:417
  62.4 1.0 collective-permute-done.2.under_ref
  63.5 0.0 collective-permute-done.3.over_ref
  63.5 1.8 %move_first.1 = (f32[512,512]{1,0:T(8,128)S(1)}, f32[128,128]{1,0:T(8,128)S(1)}, f32[3,2,2,128]{3,2,1,0:T(2,128)S(1)}) custom-call(f32[9,128]{1,0:T(8,128)S(1)} %get-tuple-element.33.near_ref, f32[9,128]{1,0:T(8,128)S(1)} %get-tuple-element.34.mid_ref, f32[9,128]{1,0:T(8,128)S(1)} %get-tuple-element.35.far_ref, f32[9,128]{1,0:T(8,128)S(1)} %collective-permute-done.below_ref, ...), custom_call_target="tpu_custom_call" | custom-call | tf_op jit(solution)/shard_map/move_first/pallas_call | solution.py:31
  65.3 19.2 %all_to_all.58 = f32[128,1,128]{2,1,0:T(1,128)S(1)} all-to-all(f32[128,1,128]{2,1,0:T(1,128)S(1)} %bitcast.34), channel_id=1, replica_groups=mesh['slab'=16,'grp'=8] {'slab','grp'}, dimensions={0} | all-to-all | bytes 131072 | tf_op jit(solution)/shard_map/all_to_all | solution.py:421
  84.5 2.0 %force_second.1 = (f32[9,128]{1,0:T(8,128)S(1)}, f32[9,128]{1,0:T(8,128)S(1)}, f32[9,128]{1,0:T(8,128)S(1)}, f32[512,512]{1,0:T(8,128)S(1)}) custom-call(f32[128,128]{1,0:T(8,128)S(1)} %bitcast.27, f32[128,128]{1,0:T(8,128)S(1)} %bitcast.29, f32[512,512]{1,0:T(8,128)S(1)} %get-tuple-element.31.misfit_ref, f32[512,512]{1,0:T(8,128)S(1)} %get-tuple-element.39.change_ref, ...), custom_call_target="tpu_custom_call" | custom-call | tf_op jit(solution)/shard_map/force_second/pallas_call | solution.py:31
  86.5 1.2 %collective-permute-start.5 = (f32[9,128]{1,0:T(8,128)S(1)}, f32[9,128]{1,0:T(8,128)S(1)}, u32[]{:S(2)}, u32[]{:S(2)}) collective-permute-start(f32[9,128]{1,0:T(8,128)S(1)} %get-tuple-element.40.near_ref), channel_id=1, source_target_pairs={{0,7},{1,0},{2,1},{3,2},{4,3},{5,4},{6,5},{7,6},{8,15},{9,8},{10,9... | collective-permute-start | bytes 13832 | tf_op jit(solution)/shard_map/ppermute | solution.py:417
  87.8 0.5 collective-permute-start.4
  88.3 1.3 %collective-permute-done.5.above_ref = f32[9,128]{1,0:T(8,128)S(1)} collective-permute-done((f32[9,128]{1,0:T(8,128)S(1)}, f32[9,128]{1,0:T(8,128)S(1)}, u32[]{:S(2)}, u32[]{:S(2)}) %collective-permute-start.5) | collective-permute-done | bytes 4640 | tf_op jit(solution)/shard_map/ppermute | solution.py:417
  89.6 0.0 collective-permute-done.4.below_ref
  89.6 0.4 collective-permute-start.6
  90.0 4.4 %collective-permute-start.7 = (f32[9,128]{1,0:T(8,128)S(1)}, f32[9,128]{1,0:T(8,128)S(1)}, u32[]{:S(2)}, u32[]{:S(2)}) collective-permute-start(f32[9,128]{1,0:T(8,128)S(1)} %get-tuple-element.44), channel_id=1, source_target_pairs={{0,120},{8,0},{16,8},{24,16},{32,24},{40,32},{48,40},{56,48},{64,5... | collective-permute-start | bytes 13832 | tf_op jit(solution)/shard_map/ppermute | solution.py:417
  94.5 1.0 collective-permute-done.6.under_ref
  95.5 0.0 collective-permute-done.7.over_ref
  95.5 1.7 %move_second.1 = (f32[512,512]{1,0:T(8,128)S(1)}, f32[128,128]{1,0:T(8,128)S(1)}, f32[3,2,2,128]{3,2,1,0:T(2,128)S(1)}) custom-call(f32[9,128]{1,0:T(8,128)S(1)} %get-tuple-element.40.near_ref, f32[9,128]{1,0:T(8,128)S(1)} %get-tuple-element.41.mid_ref, f32[9,128]{1,0:T(8,128)S(1)} %get-tuple-element.42.far_ref, ...), custom_call_target="tpu_custom_call" | custom-call | tf_op jit(solution)/shard_map/move_second/pallas_call | solution.py:31
  97.3 19.2 %all_to_all.59 = f32[128,1,128]{2,1,0:T(1,128)S(1)} all-to-all(f32[128,1,128]{2,1,0:T(1,128)S(1)} %bitcast.33), channel_id=1, replica_groups=mesh['slab'=16,'grp'=8] {'slab','grp'}, dimensions={0} | all-to-all | bytes 131072 | tf_op jit(solution)/shard_map/all_to_all | solution.py:421
  116.4 1.2 %finish.1 = (f32[3,2,2,128]{3,2,1,0:T(2,128)}, f32[512,512]{1,0:T(8,128)}) custom-call(f32[128,128]{1,0:T(8,128)S(1)} %bitcast.31, f32[128,128]{1,0:T(8,128)S(1)} %bitcast.32, f32[3,2,2,128]{3,2,1,0:T(2,128)S(1)} %get-tuple-element.47.dir0_ref, f32[3,2,2,128]{3,2,1,0:T(2,128)S(1)} %get-tuple-element.48.dir1_ref, ...), custom_call_target="tpu_custom_call" | custom-call | tf_op jit(solution)/shard_map/finish/pallas_call | solution.py:31
  (2 shorter events, 0.0 us)
Async XLA Ops:
  54.5 3.1 %collective-permute-start.1 = (f32[9,128]{1,0:T(8,128)S(1)}, f32[9,128]{1,0:T(8,128)S(1)}, u32[]{:S(2)}, u32[]{:S(2)}) collective-permute-start(f32[9,128]{1,0:T(8,128)S(1)} %get-tuple-element.33.near_ref), channel_id=1, source_target_pairs={{0,7},{1,0},{2,1},{3,2},{4,3},{5,4},{6,5},{7,6},{8,15},{9,8},{10,9... | collective-permute-start | bytes 13832 | tf_op jit(solution)/shard_map/ppermute | solution.py:417
  55.7 1.9 %collective-permute-start = (f32[9,128]{1,0:T(8,128)S(1)}, f32[9,128]{1,0:T(8,128)S(1)}, u32[]{:S(2)}, u32[]{:S(2)}) collective-permute-start(f32[9,128]{1,0:T(8,128)S(1)} %get-tuple-element.35.far_ref), channel_id=1, source_target_pairs={{0,1},{1,2},{2,3},{3,4},{4,5},{5,6},{6,7},{7,0},{8,9},{9,10},{10,1... | collective-permute-start | bytes 13832 | tf_op jit(solution)/shard_map/ppermute | solution.py:417
  57.6 5.9 %collective-permute-start.2 = (f32[9,128]{1,0:T(8,128)S(1)}, f32[9,128]{1,0:T(8,128)S(1)}, u32[]{:S(2)}, u32[]{:S(2)}) collective-permute-start(f32[9,128]{1,0:T(8,128)S(1)} %get-tuple-element.36), channel_id=1, source_target_pairs={{0,8},{8,16},{16,24},{24,32},{32,40},{40,48},{48,56},{56,64},{64,7... | collective-permute-start | bytes 13832 | tf_op jit(solution)/shard_map/ppermute | solution.py:417
  58.0 5.5 %collective-permute-start.3 = (f32[9,128]{1,0:T(8,128)S(1)}, f32[9,128]{1,0:T(8,128)S(1)}, u32[]{:S(2)}, u32[]{:S(2)}) collective-permute-start(f32[9,128]{1,0:T(8,128)S(1)} %get-tuple-element.37), channel_id=1, source_target_pairs={{0,120},{8,0},{16,8},{24,16},{32,24},{40,32},{48,40},{56,48},{64,5... | collective-permute-start | bytes 13832 | tf_op jit(solution)/shard_map/ppermute | solution.py:417
  86.5 3.1 %collective-permute-start.5 = (f32[9,128]{1,0:T(8,128)S(1)}, f32[9,128]{1,0:T(8,128)S(1)}, u32[]{:S(2)}, u32[]{:S(2)}) collective-permute-start(f32[9,128]{1,0:T(8,128)S(1)} %get-tuple-element.40.near_ref), channel_id=1, source_target_pairs={{0,7},{1,0},{2,1},{3,2},{4,3},{5,4},{6,5},{7,6},{8,15},{9,8},{10,9... | collective-permute-start | bytes 13832 | tf_op jit(solution)/shard_map/ppermute | solution.py:417
  87.8 1.9 %collective-permute-start.4 = (f32[9,128]{1,0:T(8,128)S(1)}, f32[9,128]{1,0:T(8,128)S(1)}, u32[]{:S(2)}, u32[]{:S(2)}) collective-permute-start(f32[9,128]{1,0:T(8,128)S(1)} %get-tuple-element.42.far_ref), channel_id=1, source_target_pairs={{0,1},{1,2},{2,3},{3,4},{4,5},{5,6},{6,7},{7,0},{8,9},{9,10},{10,1... | collective-permute-start | bytes 13832 | tf_op jit(solution)/shard_map/ppermute | solution.py:417
  89.6 5.9 %collective-permute-start.6 = (f32[9,128]{1,0:T(8,128)S(1)}, f32[9,128]{1,0:T(8,128)S(1)}, u32[]{:S(2)}, u32[]{:S(2)}) collective-permute-start(f32[9,128]{1,0:T(8,128)S(1)} %get-tuple-element.43), channel_id=1, source_target_pairs={{0,8},{8,16},{16,24},{24,32},{32,40},{40,48},{48,56},{56,64},{64,7... | collective-permute-start | bytes 13832 | tf_op jit(solution)/shard_map/ppermute | solution.py:417
  90.0 5.5 %collective-permute-start.7 = (f32[9,128]{1,0:T(8,128)S(1)}, f32[9,128]{1,0:T(8,128)S(1)}, u32[]{:S(2)}, u32[]{:S(2)}) collective-permute-start(f32[9,128]{1,0:T(8,128)S(1)} %get-tuple-element.44), channel_id=1, source_target_pairs={{0,120},{8,0},{16,8},{24,16},{32,24},{40,32},{48,40},{56,48},{64,5... | collective-permute-start | bytes 13832 | tf_op jit(solution)/shard_map/ppermute | solution.py:417

commit v3 on v2

--- a/solution.py
+++ b/solution.py
@@ -254,9 +254,12 @@
                     value = own[2 * b : 2 * b + 1] + moved[2 * b + 1 : 2 * b + 2]
                     key = (r % 2 + b, (r // 2 + a) * 3 + k)
                     nodes[key] = nodes[key] + value if key in nodes else value
-    for y, ref in enumerate((near_ref, mid_ref, far_ref)):
-        for row in range(9):
-            ref[pl.ds(row, 1), :] = nodes[(y, row)]
+    upward = is_even("grp")
+    for row in range(9):
+        near, far = nodes[(0, row)], nodes[(2, row)]
+        near_ref[pl.ds(row, 1), :] = jnp.where(upward, far, near)
+        mid_ref[pl.ds(row, 1), :] = nodes[(1, row)]
+        far_ref[pl.ds(row, 1), :] = jnp.where(upward, near, far)
 
 
 def first_force_body(sums_ref, misfit_ref, grad_ref, near_ref, mid_ref, far_ref, parts_ref):
@@ -294,18 +297,28 @@
     force_nodes(misfit_at, inverse, grad_ref, near_ref, mid_ref, far_ref, parts_ref)
 
 
-def band_sums(near_ref, mid_ref, far_ref, below_ref, above_ref):
+def is_even(axis):
+    return lax.axis_index(axis) % 2 == 0
+
+
+def band_sums(pair_ref, mid_ref, cross_ref, from_pair_ref, from_cross_ref):
     band = lax.axis_index("grp")
     last = lax.axis_size("grp") - 1
-    near = near_ref[...] + jnp.where(band > 0, below_ref[...], 0.0)
-    far = jnp.where(band < last, far_ref[...] + above_ref[...], 0.0)
+    upward = is_even("grp")
+    pair, cross = pair_ref[...], cross_ref[...]
+    from_pair, from_cross = from_pair_ref[...], from_cross_ref[...]
+    below = jnp.where(upward, from_cross, from_pair)
+    above = jnp.where(upward, from_pair, from_cross)
+    near = jnp.where(upward, cross, pair) + jnp.where(band > 0, below, 0.0)
+    far = jnp.where(band < last, jnp.where(upward, pair, cross) + above, 0.0)
     return near, mid_ref[...], far
 
 
-def edge_body(near_ref, mid_ref, far_ref, below_ref, above_ref, down_ref, up_ref):
+def edge_body(near_ref, mid_ref, far_ref, below_ref, above_ref, pair_ref, cross_ref):
+    upward = is_even("slab")
     for y, part in enumerate(band_sums(near_ref, mid_ref, far_ref, below_ref, above_ref)):
-        down_ref[pl.ds(3 * y, 3), :] = part[0:3]
-        up_ref[pl.ds(3 * y, 3), :] = part[6:9]
+        pair_ref[pl.ds(3 * y, 3), :] = jnp.where(upward, part[6:9], part[0:3])
+        cross_ref[pl.ds(3 * y, 3), :] = jnp.where(upward, part[0:3], part[6:9])
 
 
 def move_body(
@@ -315,11 +328,13 @@
     slab = lax.axis_index("slab")
     last = lax.axis_size("slab") - 1
     bands = band_sums(near_ref, mid_ref, far_ref, below_ref, above_ref)
+    upward = is_even("slab")
     steep = jnp.zeros((1, 128), F32)
     nodes = {}
     for y in range(3):
-        under = jnp.where(slab > 0, under_ref[pl.ds(3 * y, 3), :], 0.0)
-        over = over_ref[pl.ds(3 * y, 3), :]
+        from_pair, from_cross = under_ref[pl.ds(3 * y, 3), :], over_ref[pl.ds(3 * y, 3), :]
+        under = jnp.where(slab > 0, jnp.where(upward, from_cross, from_pair), 0.0)
+        over = jnp.where(upward, from_pair, from_cross)
         layers = (
             bands[y][0:3] + under,
             bands[y][3:6],
@@ -412,9 +427,12 @@
     out_ref[...] = misfit_ref[...] + step1 * change_ref[...]
 
 
-def around(block, axis, distance):
+def swap(block, axis, offset):
     size = lax.axis_size(axis)
-    return lax.ppermute(block, axis, [(i, (i + distance) % size) for i in range(size)])
+    route = []
+    for i in range(offset, size + offset, 2):
+        route += [(i % size, (i + 1) % size), ((i + 1) % size, i % size)]
+    return lax.ppermute(block, axis, route)
 
 
 def to_all(sums):
@@ -422,11 +440,11 @@
 
 
 def halo(near, mid, far):
-    below = around(far, "grp", 1)
-    above = around(near, "grp", -1)
-    down, up = call(edge_body, [((9, 128), F32)] * 2, (near, mid, far, below, above), "edges")
-    under = around(up, "slab", 1)
-    over = around(down, "slab", -1)
+    below = swap(near, "grp", 0)
+    above = swap(far, "grp", 1)
+    pair, cross = call(edge_body, [((9, 128), F32)] * 2, (near, mid, far, below, above), "edges")
+    under = swap(pair, "slab", 0)
+    over = swap(cross, "slab", 1)
     return below, above, under, over
 
 

time: 118 us -> 113 us (0.958)
  waiting for transfers between devices: 4.74 us -> 15.1 us
  blocking collectives: 83 us -> 74.6 us
  starting transfers between devices: 13.2 us -> 6.17 us
    ppermute x8, waiting for transfers between devices: 4.74 us -> 15.1 us  [swap(): return lax.ppermute(block, axis, route)]
    all_to_all x3, blocking collectives: 57.2 us -> 48.8 us  [to_all(): return lax.all_to_all(sums, EVERY, 0, 0, tiled=True)]
    ppermute x8, starting transfers between devices: 13.2 us -> 6.17 us  [swap(): return lax.ppermute(block, axis, route)]
  transfers between devices with their start and end apart: 8 -> 8, of which waited for: 4 -> 8; matrix products, arithmetic and copies ran while one was open for 0% -> 0% of each run, Pallas kernels for 0% -> 0%
where the time goes in v3:
time: 113 us
  blocking collectives  74.6 us (66%)
  Pallas kernels  16.1 us (14%)
  waiting for transfers between devices  15.1 us (13%)
  starting transfers between devices  6.17 us (5%)
    all_to_all x3, blocking collectives, to_all(): return lax.all_to_all(sums, EVERY, 0, 0, tiled=True)  48.8 us
    pallas_call x10, Pallas kernels, call(): pl.pallas_call(body, out_shape=[jax.ShapeDtypeStruct(s, d) for s, d in ou...  16.1 us
    ppermute x8, waiting for transfers between devices, swap(): return lax.ppermute(block, axis, route)  15.1 us
    all_to_all x1, blocking collectives, shards(): asked = lax.all_to_all(want, 'slab', 0, 0, tiled=True)  13.8 us
    all_to_all x1, blocking collectives, shards(): recv = lax.all_to_all(sent, 'slab', 0, 0, tiled=True)  11.9 us
    ppermute x8, starting transfers between devices, swap(): return lax.ppermute(block, axis, route)  6.17 us
  transfers between devices with their start and end apart: 8, of which 8 were waited for; matrix products, arithmetic and copies ran while one was open for 0% of the time, Pallas kernels for 0%

profile of v3, /device:TPU:1, one launch (start us, length us, event | category | flops | bytes accessed | tf_op | source)
XLA Modules:
  0.0 112.7 jit_solution(17058099494342879835)
XLA Ops:
  0.6 1.2 %wanted.1 = (s32[4,128]{1,0:T(4,128)S(1)}, s32[16,128]{1,0:T(8,128)S(1)}, bf16[512,512]{1,0:T(8,128)(2,1)S(1)}) custom-call(s32[2,2,128]{2,1,0:T(2,128)} %src_hbm.1, bf16[512,512]{1,0:T(8,128)(2,1)} %bitcast.41), custom_call_target="tpu_custom_call" | custom-call | tf_op jit(solution)/shard_map/wanted/pallas_call | solution.py:31
  1.9 13.8 %all_to_all.55 = s32[16,1,128]{2,1,0:T(1,128)S(1)} all-to-all(s32[16,1,128]{2,1,0:T(1,128)S(1)} %bitcast.37), channel_id=1, replica_groups=mesh['slab'=16,'grp'=8] {'slab'}, dimensions={0} | all-to-all | bytes 16384 | tf_op jit(solution)/shard_map/all_to_all | solution.py:471
  15.7 0.5 pick.1
  16.2 11.9 %all_to_all.56 = bf16[16,32,512]{2,1,0:T(8,128)(2,1)S(1)} all-to-all(bf16[16,32,512]{2,1,0:T(8,128)(2,1)S(1)} %bitcast.24), channel_id=1, replica_groups=mesh['slab'=16,'grp'=8] {'slab'}, dimensions={0} | all-to-all | bytes 1048576 | tf_op jit(solution)/shard_map/all_to_all | solution.py:473
  28.1 5.7 %warp.1 = (f32[3,512,512]{2,1,0:T(8,128)S(1)}, f32[512,512]{1,0:T(8,128)S(1)}, f32[128,128]{1,0:T(8,128)S(1)}) custom-call(s32[4,128]{1,0:T(4,128)S(1)} %get-tuple-element.27.pos_ref, bf16[512,512]{1,0:T(8,128)(2,1)S(1)} %bitcast.23, bf16[512,512]{1,0:T(8,128)(2,1)} %bitcast.40, bf16[8,512,512]{2,1,0:T(8,128)(2,1)} %bitcast.38, s32[512,512]{1,0:T(8,128)} %bitcast.39), custom_call_target="tpu_custom_call" | custom-call | tf_op jit(solution)/shard_map/warp/pallas_call | solution.py:31
  33.8 18.8 %all_to_all.57 = f32[128,1,128]{2,1,0:T(1,128)S(1)} all-to-all(f32[128,1,128]{2,1,0:T(1,128)S(1)} %bitcast.35), channel_id=1, replica_groups=mesh['slab'=16,'grp'=8] {'slab','grp'}, dimensions={0} | all-to-all | bytes 131072 | tf_op jit(solution)/shard_map/all_to_all | solution.py:439
  52.6 1.9 %force_first.1 = (f32[9,128]{1,0:T(8,128)S(1)}, f32[9,128]{1,0:T(8,128)S(1)}, f32[9,128]{1,0:T(8,128)S(1)}) custom-call(f32[128,128]{1,0:T(8,128)S(1)} %bitcast.25, f32[512,512]{1,0:T(8,128)S(1)} %get-tuple-element.31.misfit_ref, f32[3,512,512]{2,1,0:T(8,128)S(1)} %get-tuple-element.32.grad_ref), custom_call_target="tpu_custom_call" | custom-call | tf_op jit(solution)/shard_map/force_first/pallas_call | solution.py:31
  54.5 1.3 %collective-permute-start = (f32[9,128]{1,0:T(8,128)S(1)}, f32[9,128]{1,0:T(8,128)S(1)}, u32[]{:S(2)}, u32[]{:S(2)}) collective-permute-start(f32[9,128]{1,0:T(8,128)S(1)} %get-tuple-element.33.near_ref), channel_id=1, source_target_pairs={{0,1},{1,0},{2,3},{3,2},{4,5},{5,4},{6,7},{7,6},{8,9},{9,8},{10,11... | collective-permute-start | bytes 13832 | tf_op jit(solution)/shard_map/ppermute | solution.py:435
  55.8 0.1 collective-permute-start.1
  55.9 0.8 collective-permute-done.below_ref
  56.6 2.2 %collective-permute-done.1.above_ref = f32[9,128]{1,0:T(8,128)S(1)} collective-permute-done((f32[9,128]{1,0:T(8,128)S(1)}, f32[9,128]{1,0:T(8,128)S(1)}, u32[]{:S(2)}, u32[]{:S(2)}) %collective-permute-start.1) | collective-permute-done | bytes 4640 | tf_op jit(solution)/shard_map/ppermute | solution.py:435
  58.9 0.4 collective-permute-start.2
  59.3 1.3 %collective-permute-start.3 = (f32[9,128]{1,0:T(8,128)S(1)}, f32[9,128]{1,0:T(8,128)S(1)}, u32[]{:S(2)}, u32[]{:S(2)}) collective-permute-start(f32[9,128]{1,0:T(8,128)S(1)} %get-tuple-element.37), channel_id=1, source_target_pairs={{8,16},{16,8},{24,32},{32,24},{40,48},{48,40},{56,64},{64,56},{72,... | collective-permute-start | bytes 13832 | tf_op jit(solution)/shard_map/ppermute | solution.py:435
  60.6 0.9 collective-permute-done.2.under_ref
  61.5 3.7 %collective-permute-done.3.over_ref = f32[9,128]{1,0:T(8,128)S(1)} collective-permute-done((f32[9,128]{1,0:T(8,128)S(1)}, f32[9,128]{1,0:T(8,128)S(1)}, u32[]{:S(2)}, u32[]{:S(2)}) %collective-permute-start.3) | collective-permute-done | bytes 4640 | tf_op jit(solution)/shard_map/ppermute | solution.py:435
  65.2 1.8 %move_first.1 = (f32[512,512]{1,0:T(8,128)S(1)}, f32[128,128]{1,0:T(8,128)S(1)}, f32[3,2,2,128]{3,2,1,0:T(2,128)S(1)}) custom-call(f32[9,128]{1,0:T(8,128)S(1)} %get-tuple-element.33.near_ref, f32[9,128]{1,0:T(8,128)S(1)} %get-tuple-element.34.mid_ref, f32[9,128]{1,0:T(8,128)S(1)} %get-tuple-element.35.far_ref, f32[9,128]{1,0:T(8,128)S(1)} %collective-permute-done.below_ref, ...), custom_call_target="tpu_custom_call" | custom-call | tf_op jit(solution)/shard_map/move_first/pallas_call | solution.py:31
  67.0 15.0 %all_to_all.58 = f32[128,1,128]{2,1,0:T(1,128)S(1)} all-to-all(f32[128,1,128]{2,1,0:T(1,128)S(1)} %bitcast.34), channel_id=1, replica_groups=mesh['slab'=16,'grp'=8] {'slab','grp'}, dimensions={0} | all-to-all | bytes 131072 | tf_op jit(solution)/shard_map/all_to_all | solution.py:439
  82.0 2.0 %force_second.1 = (f32[9,128]{1,0:T(8,128)S(1)}, f32[9,128]{1,0:T(8,128)S(1)}, f32[9,128]{1,0:T(8,128)S(1)}, f32[512,512]{1,0:T(8,128)S(1)}) custom-call(f32[128,128]{1,0:T(8,128)S(1)} %bitcast.27, f32[128,128]{1,0:T(8,128)S(1)} %bitcast.29, f32[512,512]{1,0:T(8,128)S(1)} %get-tuple-element.31.misfit_ref, f32[512,512]{1,0:T(8,128)S(1)} %get-tuple-element.39.change_ref, ...), custom_call_target="tpu_custom_call" | custom-call | tf_op jit(solution)/shard_map/force_second/pallas_call | solution.py:31
  84.0 1.3 %collective-permute-start.4 = (f32[9,128]{1,0:T(8,128)S(1)}, f32[9,128]{1,0:T(8,128)S(1)}, u32[]{:S(2)}, u32[]{:S(2)}) collective-permute-start(f32[9,128]{1,0:T(8,128)S(1)} %get-tuple-element.40.near_ref), channel_id=1, source_target_pairs={{0,1},{1,0},{2,3},{3,2},{4,5},{5,4},{6,7},{7,6},{8,9},{9,8},{10,11... | collective-permute-start | bytes 13832 | tf_op jit(solution)/shard_map/ppermute | solution.py:435
  85.3 0.1 collective-permute-start.5
  85.4 0.8 collective-permute-done.4.below_ref
  86.2 2.2 %collective-permute-done.5.above_ref = f32[9,128]{1,0:T(8,128)S(1)} collective-permute-done((f32[9,128]{1,0:T(8,128)S(1)}, f32[9,128]{1,0:T(8,128)S(1)}, u32[]{:S(2)}, u32[]{:S(2)}) %collective-permute-start.5) | collective-permute-done | bytes 4640 | tf_op jit(solution)/shard_map/ppermute | solution.py:435
  88.4 0.4 collective-permute-start.6
  88.9 1.3 %collective-permute-start.7 = (f32[9,128]{1,0:T(8,128)S(1)}, f32[9,128]{1,0:T(8,128)S(1)}, u32[]{:S(2)}, u32[]{:S(2)}) collective-permute-start(f32[9,128]{1,0:T(8,128)S(1)} %get-tuple-element.44), channel_id=1, source_target_pairs={{8,16},{16,8},{24,32},{32,24},{40,48},{48,40},{56,64},{64,56},{72,... | collective-permute-start | bytes 13832 | tf_op jit(solution)/shard_map/ppermute | solution.py:435
  90.2 0.9 collective-permute-done.6.under_ref
  91.0 3.7 %collective-permute-done.7.over_ref = f32[9,128]{1,0:T(8,128)S(1)} collective-permute-done((f32[9,128]{1,0:T(8,128)S(1)}, f32[9,128]{1,0:T(8,128)S(1)}, u32[]{:S(2)}, u32[]{:S(2)}) %collective-permute-start.7) | collective-permute-done | bytes 4640 | tf_op jit(solution)/shard_map/ppermute | solution.py:435
  94.7 1.7 %move_second.1 = (f32[512,512]{1,0:T(8,128)S(1)}, f32[128,128]{1,0:T(8,128)S(1)}, f32[3,2,2,128]{3,2,1,0:T(2,128)S(1)}) custom-call(f32[9,128]{1,0:T(8,128)S(1)} %get-tuple-element.40.near_ref, f32[9,128]{1,0:T(8,128)S(1)} %get-tuple-element.41.mid_ref, f32[9,128]{1,0:T(8,128)S(1)} %get-tuple-element.42.far_ref, ...), custom_call_target="tpu_custom_call" | custom-call | tf_op jit(solution)/shard_map/move_second/pallas_call | solution.py:31
  96.4 15.0 %all_to_all.59 = f32[128,1,128]{2,1,0:T(1,128)S(1)} all-to-all(f32[128,1,128]{2,1,0:T(1,128)S(1)} %bitcast.33), channel_id=1, replica_groups=mesh['slab'=16,'grp'=8] {'slab','grp'}, dimensions={0} | all-to-all | bytes 131072 | tf_op jit(solution)/shard_map/all_to_all | solution.py:439
  111.4 1.2 %finish.1 = (f32[3,2,2,128]{3,2,1,0:T(2,128)}, f32[512,512]{1,0:T(8,128)}) custom-call(f32[128,128]{1,0:T(8,128)S(1)} %bitcast.31, f32[128,128]{1,0:T(8,128)S(1)} %bitcast.32, f32[3,2,2,128]{3,2,1,0:T(2,128)S(1)} %get-tuple-element.47.dir0_ref, f32[3,2,2,128]{3,2,1,0:T(2,128)S(1)} %get-tuple-element.48.dir1_ref, ...), custom_call_target="tpu_custom_call" | custom-call | tf_op jit(solution)/shard_map/finish/pallas_call | solution.py:31
  (2 shorter events, 0.0 us)
Async XLA Ops:
  54.5 2.1 %collective-permute-start = (f32[9,128]{1,0:T(8,128)S(1)}, f32[9,128]{1,0:T(8,128)S(1)}, u32[]{:S(2)}, u32[]{:S(2)}) collective-permute-start(f32[9,128]{1,0:T(8,128)S(1)} %get-tuple-element.33.near_ref), channel_id=1, source_target_pairs={{0,1},{1,0},{2,3},{3,2},{4,5},{5,4},{6,7},{7,6},{8,9},{9,8},{10,11... | collective-permute-start | bytes 13832 | tf_op jit(solution)/shard_map/ppermute | solution.py:435
  55.8 3.1 %collective-permute-start.1 = (f32[9,128]{1,0:T(8,128)S(1)}, f32[9,128]{1,0:T(8,128)S(1)}, u32[]{:S(2)}, u32[]{:S(2)}) collective-permute-start(f32[9,128]{1,0:T(8,128)S(1)} %get-tuple-element.35.far_ref), channel_id=1, source_target_pairs={{1,2},{2,1},{3,4},{4,3},{5,6},{6,5},{7,0},{0,7},{9,10},{10,9},{11,... | collective-permute-start | bytes 13832 | tf_op jit(solution)/shard_map/ppermute | solution.py:435
  58.9 2.6 %collective-permute-start.2 = (f32[9,128]{1,0:T(8,128)S(1)}, f32[9,128]{1,0:T(8,128)S(1)}, u32[]{:S(2)}, u32[]{:S(2)}) collective-permute-start(f32[9,128]{1,0:T(8,128)S(1)} %get-tuple-element.36), channel_id=1, source_target_pairs={{0,8},{8,0},{16,24},{24,16},{32,40},{40,32},{48,56},{56,48},{64,72... | collective-permute-start | bytes 13832 | tf_op jit(solution)/shard_map/ppermute | solution.py:435
  59.3 5.8 %collective-permute-start.3 = (f32[9,128]{1,0:T(8,128)S(1)}, f32[9,128]{1,0:T(8,128)S(1)}, u32[]{:S(2)}, u32[]{:S(2)}) collective-permute-start(f32[9,128]{1,0:T(8,128)S(1)} %get-tuple-element.37), channel_id=1, source_target_pairs={{8,16},{16,8},{24,32},{32,24},{40,48},{48,40},{56,64},{64,56},{72,... | collective-permute-start | bytes 13832 | tf_op jit(solution)/shard_map/ppermute | solution.py:435
  84.0 2.1 %collective-permute-start.4 = (f32[9,128]{1,0:T(8,128)S(1)}, f32[9,128]{1,0:T(8,128)S(1)}, u32[]{:S(2)}, u32[]{:S(2)}) collective-permute-start(f32[9,128]{1,0:T(8,128)S(1)} %get-tuple-element.40.near_ref), channel_id=1, source_target_pairs={{0,1},{1,0},{2,3},{3,2},{4,5},{5,4},{6,7},{7,6},{8,9},{9,8},{10,11... | collective-permute-start | bytes 13832 | tf_op jit(solution)/shard_map/ppermute | solution.py:435
  85.3 3.1 %collective-permute-start.5 = (f32[9,128]{1,0:T(8,128)S(1)}, f32[9,128]{1,0:T(8,128)S(1)}, u32[]{:S(2)}, u32[]{:S(2)}) collective-permute-start(f32[9,128]{1,0:T(8,128)S(1)} %get-tuple-element.42.far_ref), channel_id=1, source_target_pairs={{1,2},{2,1},{3,4},{4,3},{5,6},{6,5},{7,0},{0,7},{9,10},{10,9},{11,... | collective-permute-start | bytes 13832 | tf_op jit(solution)/shard_map/ppermute | solution.py:435
  88.4 2.6 %collective-permute-start.6 = (f32[9,128]{1,0:T(8,128)S(1)}, f32[9,128]{1,0:T(8,128)S(1)}, u32[]{:S(2)}, u32[]{:S(2)}) collective-permute-start(f32[9,128]{1,0:T(8,128)S(1)} %get-tuple-element.43), channel_id=1, source_target_pairs={{0,8},{8,0},{16,24},{24,16},{32,40},{40,32},{48,56},{56,48},{64,72... | collective-permute-start | bytes 13832 | tf_op jit(solution)/shard_map/ppermute | solution.py:435
  88.9 5.8 %collective-permute-start.7 = (f32[9,128]{1,0:T(8,128)S(1)}, f32[9,128]{1,0:T(8,128)S(1)}, u32[]{:S(2)}, u32[]{:S(2)}) collective-permute-start(f32[9,128]{1,0:T(8,128)S(1)} %get-tuple-element.44), channel_id=1, source_target_pairs={{8,16},{16,8},{24,32},{32,24},{40,48},{48,40},{56,64},{64,56},{72,... | collective-permute-start | bytes 13832 | tf_op jit(solution)/shard_map/ppermute | solution.py:435

commit v4 on v3

--- a/solution.py
+++ b/solution.py
@@ -13,6 +13,7 @@
 ROWS = 16
 BLOCKS = CELLS // ROWS
 CHUNKS = 4
+NN = (((1,), (0,)), ((), ()))
 NT = (((1,), (1,)), ((), ()))
 TN = (((0,), (0,)), ((), ()))
 VMEM = pl.BlockSpec(memory_space=pltpu.VMEM)
@@ -27,46 +28,59 @@
     return lax.dot_general(a, b, dims, preferred_element_type=F32)
 
 
-def call(body, outs, ins, name, scratch=(), limit=16, far=()):
+def call(body, outs, ins, name, scratch=(), limit=16, far=(), stored=False):
     return pl.pallas_call(
         body,
         out_shape=[jax.ShapeDtypeStruct(s, d) for s, d in outs],
         in_specs=[HBM if n in far else VMEM for n in range(len(ins))],
-        out_specs=[VMEM] * len(outs),
+        out_specs=[HBM if stored else VMEM] * len(outs),
         scratch_shapes=list(scratch),
         compiler_params=pltpu.CompilerParams(vmem_limit_bytes=limit << 20),
         name=name,
     )(*[pltpu.with_memory_space_constraint(x, pltpu.HBM) if n in far else x for n, x in enumerate(ins)])
 
 
-def wanted_body(src_hbm, bricks_hbm, pos_ref, want_ref, bricks_ref, src_ref, sems):
+def wanted_body(
+    src_hbm, bricks_hbm, pos_ref, want_ref, bricks_ref, level_ref, inner_ref, outer_ref, slope_ref,
+    src_ref, sems,
+):
     first = pltpu.make_async_copy(src_hbm, src_ref, sems.at[0])
-    fetch = pltpu.make_async_copy(bricks_hbm, bricks_ref, sems.at[1])
+    fetches = []
+    for r in range(4):
+        at = pl.ds(128 * r, 128)
+        fetches.append(pltpu.make_async_copy(bricks_hbm.at[at], bricks_ref.at[at], sems.at[r + 1]))
     first.start()
-    fetch.start()
+    for fetch in fetches:
+        fetch.start()
     place = 32 * (lax.axis_index("slab") % 4)
     earlier = (iota((128, 128), 0) < iota((128, 128), 1)).astype(F32).astype(BF16)
     owners = iota((16, 128), 0)
     lanes = iota((128, 128), 0)
     before = jnp.zeros((16, 1), F32)
     want = jnp.zeros((32, 128), F32)
+    level_ref[...] = level_table()
+    inner_ref[...] = rise_table(256)
+    outer_ref[...] = rise_table(128)
+    slope_ref[...] = slope_table()
     first.wait()
     for r in range(4):
         src = src_ref[r // 2, pl.ds(r % 2, 1), :]
         owner = src >> 9
         row = src & 511
         mine = jnp.where(owners == owner, 1.0, 0.0)
-        count = dot(mine.astype(BF16), earlier, (((1,), (0,)), ((), ()))) + before
+        count = dot(mine.astype(BF16), earlier, NN) + before
         before = before + jnp.sum(mine, axis=1, keepdims=True)
         rank = jnp.sum(mine * count, axis=0, keepdims=True).astype(I32)
-        pos_ref[pl.ds(r, 1), :] = owner * 32 + rank
+        pos = (owner * 32 + rank).astype(F32)
+        pos_ref[pl.ds(128 * r, 128), :] = jnp.transpose(jnp.broadcast_to(pos, (128, 128)))
         slot = jnp.where(lanes == rank + place, 1.0, 0.0).astype(BF16)
         low = (row & 255).astype(F32)
         high = (row >> 8).astype(F32)
         parts = jnp.concatenate([mine * low, mine * high], axis=0).astype(BF16)
         want = want + dot(parts, slot, NT)
     want_ref[...] = (want[:16] + 256.0 * want[16:]).astype(I32)
-    fetch.wait()
+    for fetch in fetches:
+        fetch.wait()
 
 
 def pick_body(want_ref, bricks_ref, out_ref):
@@ -99,17 +113,26 @@
     ]
 
 
-def shift_table(width, last):
-    at = iota((1, 896), 1)
-    tap = (at >> 7) + 1
-    lane = at & 127
+def plane_step(tap, lane):
     step_x = jnp.where(((tap & 1) == 1) & ((lane & 7) < 7), 1, 0)
     step_y = jnp.where(((tap & 2) == 2) & ((lane & 56) < 56), 8, 0)
-    rise = (tap & 4) == 4
-    if last:
-        rise = rise & (lane < 64)
-    target = lane + step_x + step_y + jnp.where(rise, 64, 0)
-    return jnp.where(iota((width, 896), 0) == target, 1.0, 0.0).astype(BF16)
+    return lane + step_x + step_y
+
+
+def shift_table(shape, target):
+    return jnp.where(iota(shape, 0) == target, 1.0, 0.0).astype(BF16)
+
+
+def level_table():
+    at = iota((1, 384), 1)
+    return shift_table((128, 384), plane_step((at >> 7) + 1, at & 127))
+
+
+def rise_table(width):
+    at = iota((1, 512), 1)
+    lane = at & 127
+    rise = jnp.where(lane < 64, 64, 64 if width == 256 else 0)
+    return shift_table((width, 512), plane_step(at >> 7, lane) + rise)
 
 
 def slope_table():
@@ -125,8 +148,9 @@
 
 
 def warp_body(
-    pos_ref, recv_ref, image_hbm, taps_hbm, valid_hbm, grad_ref, misfit_ref, sums_ref,
-    source_ref, planes_ref, split_ref, mask_ref, image_ref, taps_ref, valid_ref, sems,
+    pos_ref, recv_ref, level_ref, inner_ref, outer_ref, slope_ref, image_hbm, taps_hbm, valid_hbm,
+    grad_ref, misfit_ref, sums_ref,
+    planes_ref, split_ref, mask_ref, image_ref, taps_ref, valid_ref, sems,
 ):
     copies = []
     for r in range(4):
@@ -141,28 +165,34 @@
     for group in copies:
         for copy in group:
             copy.start()
-    recv = recv_ref[...]
-    rows = iota((CELLS, 128), 0)
-    for r in range(4):
+    lane = iota((128, 128), 1).astype(F32)
+    low = iota((ROWS, 128), 1) < 64
+    table = slope_ref[...]
+
+    def planes(r):
         at = pl.ds(128 * r, 128)
-        chosen = jnp.where(rows == pos_ref[pl.ds(r, 1), :], 1.0, 0.0).astype(BF16)
-        picked = dot(chosen, recv, TN)
+        pos = pos_ref[at, :]
+        chosen = jnp.concatenate(
+            [jnp.where(pos == lane + 128.0 * q, 1.0, 0.0).astype(BF16) for q in range(4)], axis=1
+        )
+        picked = dot(chosen, recv_ref[...], NN)
         planes_ref[0, at, :] = picked
-        source_ref[at, :] = picked.astype(BF16)
-    inner = shift_table(256, False)
-    outer = shift_table(128, True)
-    for j in range(CHUNKS):
-        if j + 1 < CHUNKS:
-            shifted = dot(source_ref[:, pl.ds(128 * j, 256)], inner, (((1,), (0,)), ((), ())))
-        else:
-            shifted = dot(source_ref[:, columns(j)], outer, (((1,), (0,)), ((), ())))
-        for tap in range(7):
-            planes_ref[tap + 1, :, columns(j)] = shifted[:, 128 * tap : 128 * tap + 128]
-    low = iota((ROWS, 128), 1) < 64
-
-    def block(i, carry):
-        squares, counted = carry
-        at = pl.ds(pl.multiple_of(i * ROWS, ROWS), ROWS)
+        source = picked.astype(BF16)
+        parts = [source[:, 128 * j : 128 * j + 128] for j in range(CHUNKS)]
+        shifted = dot(jnp.concatenate(parts, axis=0), level_ref[...], NN)
+        for j in range(CHUNKS):
+            for tap in range(3):
+                planes_ref[tap + 1, at, columns(j)] = shifted[
+                    128 * j : 128 * (j + 1), 128 * tap : 128 * tap + 128
+                ]
+        pairs = jnp.concatenate([source[:, 128 * j : 128 * j + 256] for j in range(3)], axis=0)
+        raised = dot(pairs, inner_ref[...], NN)
+        for j in range(CHUNKS):
+            found = dot(parts[3], outer_ref[...], NN) if j == 3 else raised[128 * j : 128 * (j + 1)]
+            for tap in range(4):
+                planes_ref[tap + 4, at, columns(j)] = found[:, 128 * tap : 128 * tap + 128]
+
+    def block(at, squares, counted):
         warped = []
         for j in range(CHUNKS):
             terms = [
@@ -190,19 +220,28 @@
             counted = counted + mask
         return squares, counted
 
-    zero = jnp.zeros((ROWS, 128), F32)
-    carry = (zero, zero)
+    def slopes(r):
+        at = pl.ds(128 * r, 128)
+        for j in range(CHUNKS):
+            both = dot(split_ref[at, pl.ds(256 * j, 256)], table, NN)
+            mask = mask_ref[at, columns(j)]
+            grad_ref[1, at, columns(j)] = mask * both[:, :128]
+            grad_ref[2, at, columns(j)] = mask * both[:, 128:]
+
+    squares = counted = jnp.zeros((ROWS, 128), F32)
+    for r in range(3):
+        planes(r)
     for r in range(4):
         for copy in copies[r]:
             copy.wait()
-        carry = lax.fori_loop(128 * r // ROWS, 128 * (r + 1) // ROWS, block, carry)
-    sums_ref[...] = spread_sums(list(carry))
-    table = slope_table()
-    for j in range(CHUNKS):
-        slopes = dot(split_ref[:, pl.ds(256 * j, 256)], table, (((1,), (0,)), ((), ())))
-        mask = mask_ref[:, columns(j)]
-        grad_ref[1, :, columns(j)] = mask * slopes[:, :128]
-        grad_ref[2, :, columns(j)] = mask * slopes[:, 128:]
+        if r + 3 < 4:
+            planes(r + 3)
+        for i in range(128 // ROWS):
+            squares, counted = block(pl.ds(128 * r + ROWS * i, ROWS), squares, counted)
+        if r > 0:
+            slopes(r - 1)
+    slopes(3)
+    sums_ref[...] = spread_sums([squares, counted])
 
 
 def high_z(j, shape):
@@ -239,7 +278,7 @@
                 parts_ref[2 * k + a, at, pl.ds(128, 128)] = (value - coarse.astype(F32)).astype(BF16)
         return carry
 
-    lax.fori_loop(0, BLOCKS, block, 0)
+    lax.fori_loop(0, BLOCKS, block, 0, unroll=4)
     corner = iota((16, 256), 0)
     basis = jnp.where(corner < 4, plane_basis(corner, iota((16, 256), 1)), 0.0).astype(BF16)
     first = iota((16, 128), 1) == 0
@@ -394,7 +433,7 @@
         return curve, cross, moved_sum
 
     zero = jnp.zeros((ROWS, 128), F32)
-    curve, cross, moved_sum = lax.fori_loop(0, BLOCKS, block, (zero, zero, zero))
+    curve, cross, moved_sum = lax.fori_loop(0, BLOCKS, block, (zero, zero, zero), unroll=4)
     out_ref[...] = spread_sums([steep, curve] + ([] if second else [cross, moved_sum]))
 
 
@@ -418,13 +457,24 @@
     )
 
 
-def finish_body(first_ref, second_ref, dir0_ref, dir1_ref, misfit_ref, change_ref, coef_ref, out_ref):
+def finish_body(
+    first_ref, second_ref, dir0_ref, dir1_ref, misfit_ref, change_ref, coef_hbm, out_hbm,
+    coef_ref, out_ref, sems,
+):
     steep, curve = gathered_sums(first_ref, 2)
     step0 = steep / curve
     steep, curve = gathered_sums(second_ref, 2)
     step1 = steep / curve
     coef_ref[...] = step0.reshape(1, 1, 1, 1) * dir0_ref[...] + step1.reshape(1, 1, 1, 1) * dir1_ref[...]
-    out_ref[...] = misfit_ref[...] + step1 * change_ref[...]
+    copies = [pltpu.make_async_copy(coef_ref, coef_hbm, sems.at[4])]
+    copies[0].start()
+    for r in range(4):
+        at = pl.ds(128 * r, 128)
+        out_ref[at, :] = misfit_ref[at, :] + step1 * change_ref[at, :]
+        copies.append(pltpu.make_async_copy(out_ref.at[at], out_hbm.at[at], sems.at[r]))
+        copies[-1].start()
+    for copy in copies:
+        copy.wait()
 
 
 def swap(block, axis, offset):
@@ -460,12 +510,20 @@
     image = deformed.reshape(CELLS, 512)
     valid = valid_voxels.reshape(CELLS, 512)
 
-    pos, want, bricks = call(
+    pos, want, bricks, level, inner, outer, slope = call(
         wanted_body,
-        [((4, 128), I32), ((16, 128), I32), ((CELLS, 512), BF16)],
+        [
+            ((CELLS, 128), F32),
+            ((16, 128), I32),
+            ((CELLS, 512), BF16),
+            ((128, 384), BF16),
+            ((256, 512), BF16),
+            ((128, 512), BF16),
+            ((256, 256), BF16),
+        ],
         (sources, reference_bricks.reshape(CELLS, 512)),
         "wanted",
-        [pltpu.VMEM((2, 2, 128), I32), pltpu.SemaphoreType.DMA((2,))],
+        [pltpu.VMEM((2, 2, 128), I32), pltpu.SemaphoreType.DMA((5,))],
         far=(0, 1),
     )
     asked = lax.all_to_all(want, "slab", 0, 0, tiled=True)
@@ -474,10 +532,9 @@
     grads, misfit, sums = call(
         warp_body,
         [grad_shape, big, sums_shape],
-        (pos, recv, image, taps, valid),
+        (pos, recv, level, inner, outer, slope, image, taps, valid),
         "warp",
         [
-            pltpu.VMEM((CELLS, 512), BF16),
             pltpu.VMEM((8, CELLS, 512), F32),
             pltpu.VMEM((CELLS, 1024), BF16),
             pltpu.VMEM((CELLS, 512), F32),
@@ -487,7 +544,7 @@
             pltpu.SemaphoreType.DMA((3, 4)),
         ],
         40,
-        (2, 3, 4),
+        (6, 7, 8),
     )
     sums = to_all(sums)
     near, mid, far = call(first_force_body, nodes_shape, (sums, misfit, grads), "force_first", parts)
@@ -517,7 +574,16 @@
     )
     second = to_all(steps)
     coefficients, residual = call(
-        finish_body, [dir_shape, big], (first, second, dir0, dir1, misfit, change), "finish"
+        finish_body,
+        [dir_shape, big],
+        (first, second, dir0, dir1, misfit, change),
+        "finish",
+        [
+            pltpu.VMEM((3, 2, 2, 128), F32),
+            pltpu.VMEM((CELLS, 512), F32),
+            pltpu.SemaphoreType.DMA((5,)),
+        ],
+        stored=True,
     )
     return (coefficients, residual.reshape(2, 2, 128, 512))
 

time: 113 us -> 110 us (0.973)
  Pallas kernels: 16.1 us -> 12.9 us
    pallas_call x10, Pallas kernels: 16.1 us -> 12.9 us  [call(): pl.pallas_call(body, out_shape=[jax.ShapeDtypeStruct(s, d) for s, d in ou...]
where the time goes in v4:
time: 110 us; the launch traced here: 109 us
  blocking collectives  74.6 us (68%)
  waiting for transfers between devices  15.1 us (14%)
  Pallas kernels  12.9 us (12%)
  starting transfers between devices  6.17 us (6%)
    all_to_all x3, blocking collectives, to_all(): return lax.all_to_all(sums, EVERY, 0, 0, tiled=True)  48.9 us
    ppermute x8, waiting for transfers between devices, swap(): return lax.ppermute(block, axis, route)  15.1 us
    all_to_all x1, blocking collectives, shards(): asked = lax.all_to_all(want, 'slab', 0, 0, tiled=True)  13.8 us
    pallas_call x10, Pallas kernels, call(): pl.pallas_call(body, out_shape=[jax.ShapeDtypeStruct(s, d) for s, d in ou...  12.9 us
    all_to_all x1, blocking collectives, shards(): recv = lax.all_to_all(sent, 'slab', 0, 0, tiled=True)  11.9 us
    ppermute x8, starting transfers between devices, swap(): return lax.ppermute(block, axis, route)  6.17 us
  transfers between devices with their start and end apart: 8, of which 8 were waited for; matrix products, arithmetic and copies ran while one was open for 0% of the time, Pallas kernels for 0%

profile of v4, /device:TPU:1, one launch (start us, length us, event | category | flops | bytes accessed | tf_op | source)
XLA Modules:
  0.0 109.5 jit_solution(17548439520332852737)
XLA Ops:
  0.6 1.3 %wanted.1 = (f32[512,128]{1,0:T(8,128)S(1)}, s32[16,128]{1,0:T(8,128)S(1)}, bf16[512,512]{1,0:T(8,128)(2,1)S(1)}, bf16[128,384]{1,0:T(8,128)(2,1)S(1)}, bf16[256...) custom-call(s32[2,2,128]{2,1,0:T(2,128)} %src_hbm.1, bf16[512,512]{1,0:T(8,128)(2,1)} %bitcast.41), custom_call_target="tpu_custom_call" | custom-call | tf_op jit(solution)/shard_map/wanted/pallas_call | solution.py:32
  1.9 13.8 %all_to_all.55 = s32[16,1,128]{2,1,0:T(1,128)S(1)} all-to-all(s32[16,1,128]{2,1,0:T(1,128)S(1)} %bitcast.37), channel_id=1, replica_groups=mesh['slab'=16,'grp'=8] {'slab'}, dimensions={0} | all-to-all | bytes 16384 | tf_op jit(solution)/shard_map/all_to_all | solution.py:529
  15.7 0.5 pick.1
  16.2 11.9 %all_to_all.56 = bf16[16,32,512]{2,1,0:T(8,128)(2,1)S(1)} all-to-all(bf16[16,32,512]{2,1,0:T(8,128)(2,1)S(1)} %bitcast.24), channel_id=1, replica_groups=mesh['slab'=16,'grp'=8] {'slab'}, dimensions={0} | all-to-all | bytes 1048576 | tf_op jit(solution)/shard_map/all_to_all | solution.py:531
  28.1 3.6 %warp.1 = (f32[3,512,512]{2,1,0:T(8,128)S(1)}, f32[512,512]{1,0:T(8,128)S(1)}, f32[128,128]{1,0:T(8,128)S(1)}) custom-call(f32[512,128]{1,0:T(8,128)S(1)} %get-tuple-element.31.pos_ref, bf16[512,512]{1,0:T(8,128)(2,1)S(1)} %bitcast.23, bf16[128,384]{1,0:T(8,128)(2,1)S(1)} %get-tuple-element.34.level_ref, bf16[256,512]{1,0:T(8,128)(2,1)S(1)} %get-tuple-element.35.inner_ref, ...), custom_call_target="tpu_custom_call" | custom-call | tf_op jit(solution)/shard_map/warp/pallas_call | solution.py:32
  31.8 18.9 %all_to_all.57 = f32[128,1,128]{2,1,0:T(1,128)S(1)} all-to-all(f32[128,1,128]{2,1,0:T(1,128)S(1)} %bitcast.35), channel_id=1, replica_groups=mesh['slab'=16,'grp'=8] {'slab','grp'}, dimensions={0} | all-to-all | bytes 131072 | tf_op jit(solution)/shard_map/all_to_all | solution.py:489
  50.6 1.7 %force_first.1 = (f32[9,128]{1,0:T(8,128)S(1)}, f32[9,128]{1,0:T(8,128)S(1)}, f32[9,128]{1,0:T(8,128)S(1)}) custom-call(f32[128,128]{1,0:T(8,128)S(1)} %bitcast.25, f32[512,512]{1,0:T(8,128)S(1)} %get-tuple-element.39.misfit_ref, f32[3,512,512]{2,1,0:T(8,128)S(1)} %get-tuple-element.40.grad_ref), custom_call_target="tpu_custom_call" | custom-call | tf_op jit(solution)/shard_map/force_first/pallas_call | solution.py:32
  52.3 1.3 %collective-permute-start = (f32[9,128]{1,0:T(8,128)S(1)}, f32[9,128]{1,0:T(8,128)S(1)}, u32[]{:S(2)}, u32[]{:S(2)}) collective-permute-start(f32[9,128]{1,0:T(8,128)S(1)} %get-tuple-element.41.near_ref), channel_id=1, source_target_pairs={{0,1},{1,0},{2,3},{3,2},{4,5},{5,4},{6,7},{7,6},{8,9},{9,8},{10,11... | collective-permute-start | bytes 13832 | tf_op jit(solution)/shard_map/ppermute | solution.py:485
  53.6 0.1 collective-permute-start.1
  53.7 0.8 collective-permute-done.below_ref
  54.4 2.2 %collective-permute-done.1.above_ref = f32[9,128]{1,0:T(8,128)S(1)} collective-permute-done((f32[9,128]{1,0:T(8,128)S(1)}, f32[9,128]{1,0:T(8,128)S(1)}, u32[]{:S(2)}, u32[]{:S(2)}) %collective-permute-start.1) | collective-permute-done | bytes 4640 | tf_op jit(solution)/shard_map/ppermute | solution.py:485
  56.7 0.4 collective-permute-start.2
  57.1 1.3 %collective-permute-start.3 = (f32[9,128]{1,0:T(8,128)S(1)}, f32[9,128]{1,0:T(8,128)S(1)}, u32[]{:S(2)}, u32[]{:S(2)}) collective-permute-start(f32[9,128]{1,0:T(8,128)S(1)} %get-tuple-element.45), channel_id=1, source_target_pairs={{8,16},{16,8},{24,32},{32,24},{40,48},{48,40},{56,64},{64,56},{72,... | collective-permute-start | bytes 13832 | tf_op jit(solution)/shard_map/ppermute | solution.py:485
  58.4 0.9 collective-permute-done.2.under_ref
  59.3 3.7 %collective-permute-done.3.over_ref = f32[9,128]{1,0:T(8,128)S(1)} collective-permute-done((f32[9,128]{1,0:T(8,128)S(1)}, f32[9,128]{1,0:T(8,128)S(1)}, u32[]{:S(2)}, u32[]{:S(2)}) %collective-permute-start.3) | collective-permute-done | bytes 4640 | tf_op jit(solution)/shard_map/ppermute | solution.py:485
  63.0 1.5 %move_first.1 = (f32[512,512]{1,0:T(8,128)S(1)}, f32[128,128]{1,0:T(8,128)S(1)}, f32[3,2,2,128]{3,2,1,0:T(2,128)S(1)}) custom-call(f32[9,128]{1,0:T(8,128)S(1)} %get-tuple-element.41.near_ref, f32[9,128]{1,0:T(8,128)S(1)} %get-tuple-element.42.mid_ref, f32[9,128]{1,0:T(8,128)S(1)} %get-tuple-element.43.far_ref, f32[9,128]{1,0:T(8,128)S(1)} %collective-permute-done.below_ref, ...), custom_call_target="tpu_custom_call" | custom-call | tf_op jit(solution)/shard_map/move_first/pallas_call | solution.py:32
  64.5 15.0 %all_to_all.58 = f32[128,1,128]{2,1,0:T(1,128)S(1)} all-to-all(f32[128,1,128]{2,1,0:T(1,128)S(1)} %bitcast.34), channel_id=1, replica_groups=mesh['slab'=16,'grp'=8] {'slab','grp'}, dimensions={0} | all-to-all | bytes 131072 | tf_op jit(solution)/shard_map/all_to_all | solution.py:489
  79.5 1.8 %force_second.1 = (f32[9,128]{1,0:T(8,128)S(1)}, f32[9,128]{1,0:T(8,128)S(1)}, f32[9,128]{1,0:T(8,128)S(1)}, f32[512,512]{1,0:T(8,128)S(1)}) custom-call(f32[128,128]{1,0:T(8,128)S(1)} %bitcast.27, f32[128,128]{1,0:T(8,128)S(1)} %bitcast.29, f32[512,512]{1,0:T(8,128)S(1)} %get-tuple-element.39.misfit_ref, f32[512,512]{1,0:T(8,128)S(1)} %get-tuple-element.47.change_ref, ...), custom_call_target="tpu_custom_call" | custom-call | tf_op jit(solution)/shard_map/force_second/pallas_call | solution.py:32
  81.2 1.3 %collective-permute-start.4 = (f32[9,128]{1,0:T(8,128)S(1)}, f32[9,128]{1,0:T(8,128)S(1)}, u32[]{:S(2)}, u32[]{:S(2)}) collective-permute-start(f32[9,128]{1,0:T(8,128)S(1)} %get-tuple-element.48.near_ref), channel_id=1, source_target_pairs={{0,1},{1,0},{2,3},{3,2},{4,5},{5,4},{6,7},{7,6},{8,9},{9,8},{10,11... | collective-permute-start | bytes 13832 | tf_op jit(solution)/shard_map/ppermute | solution.py:485
  82.6 0.1 collective-permute-start.5
  82.6 0.8 collective-permute-done.4.below_ref
  83.4 2.2 %collective-permute-done.5.above_ref = f32[9,128]{1,0:T(8,128)S(1)} collective-permute-done((f32[9,128]{1,0:T(8,128)S(1)}, f32[9,128]{1,0:T(8,128)S(1)}, u32[]{:S(2)}, u32[]{:S(2)}) %collective-permute-start.5) | collective-permute-done | bytes 4640 | tf_op jit(solution)/shard_map/ppermute | solution.py:485
  85.7 0.4 collective-permute-start.6
  86.1 1.3 %collective-permute-start.7 = (f32[9,128]{1,0:T(8,128)S(1)}, f32[9,128]{1,0:T(8,128)S(1)}, u32[]{:S(2)}, u32[]{:S(2)}) collective-permute-start(f32[9,128]{1,0:T(8,128)S(1)} %get-tuple-element.52), channel_id=1, source_target_pairs={{8,16},{16,8},{24,32},{32,24},{40,48},{48,40},{56,64},{64,56},{72,... | collective-permute-start | bytes 13832 | tf_op jit(solution)/shard_map/ppermute | solution.py:485
  87.4 0.9 collective-permute-done.6.under_ref
  88.2 3.7 %collective-permute-done.7.over_ref = f32[9,128]{1,0:T(8,128)S(1)} collective-permute-done((f32[9,128]{1,0:T(8,128)S(1)}, f32[9,128]{1,0:T(8,128)S(1)}, u32[]{:S(2)}, u32[]{:S(2)}) %collective-permute-start.7) | collective-permute-done | bytes 4640 | tf_op jit(solution)/shard_map/ppermute | solution.py:485
  91.9 1.4 %move_second.1 = (f32[512,512]{1,0:T(8,128)S(1)}, f32[128,128]{1,0:T(8,128)S(1)}, f32[3,2,2,128]{3,2,1,0:T(2,128)S(1)}) custom-call(f32[9,128]{1,0:T(8,128)S(1)} %get-tuple-element.48.near_ref, f32[9,128]{1,0:T(8,128)S(1)} %get-tuple-element.49.mid_ref, f32[9,128]{1,0:T(8,128)S(1)} %get-tuple-element.50.far_ref, ...), custom_call_target="tpu_custom_call" | custom-call | tf_op jit(solution)/shard_map/move_second/pallas_call | solution.py:32
  93.3 15.0 %all_to_all.59 = f32[128,1,128]{2,1,0:T(1,128)S(1)} all-to-all(f32[128,1,128]{2,1,0:T(1,128)S(1)} %bitcast.33), channel_id=1, replica_groups=mesh['slab'=16,'grp'=8] {'slab','grp'}, dimensions={0} | all-to-all | bytes 131072 | tf_op jit(solution)/shard_map/all_to_all | solution.py:489
  108.3 1.2 %finish.1 = (f32[3,2,2,128]{3,2,1,0:T(2,128)}, f32[512,512]{1,0:T(8,128)}) custom-call(f32[128,128]{1,0:T(8,128)S(1)} %bitcast.31, f32[128,128]{1,0:T(8,128)S(1)} %bitcast.32, f32[3,2,2,128]{3,2,1,0:T(2,128)S(1)} %get-tuple-element.55.dir0_ref, f32[3,2,2,128]{3,2,1,0:T(2,128)S(1)} %get-tuple-element.56.dir1_ref, ...), custom_call_target="tpu_custom_call" | custom-call | tf_op jit(solution)/shard_map/finish/pallas_call | solution.py:32
  (2 shorter events, 0.0 us)
Async XLA Ops:
  52.3 2.1 %collective-permute-start = (f32[9,128]{1,0:T(8,128)S(1)}, f32[9,128]{1,0:T(8,128)S(1)}, u32[]{:S(2)}, u32[]{:S(2)}) collective-permute-start(f32[9,128]{1,0:T(8,128)S(1)} %get-tuple-element.41.near_ref), channel_id=1, source_target_pairs={{0,1},{1,0},{2,3},{3,2},{4,5},{5,4},{6,7},{7,6},{8,9},{9,8},{10,11... | collective-permute-start | bytes 13832 | tf_op jit(solution)/shard_map/ppermute | solution.py:485
  53.6 3.1 %collective-permute-start.1 = (f32[9,128]{1,0:T(8,128)S(1)}, f32[9,128]{1,0:T(8,128)S(1)}, u32[]{:S(2)}, u32[]{:S(2)}) collective-permute-start(f32[9,128]{1,0:T(8,128)S(1)} %get-tuple-element.43.far_ref), channel_id=1, source_target_pairs={{1,2},{2,1},{3,4},{4,3},{5,6},{6,5},{7,0},{0,7},{9,10},{10,9},{11,... | collective-permute-start | bytes 13832 | tf_op jit(solution)/shard_map/ppermute | solution.py:485
  56.7 2.6 %collective-permute-start.2 = (f32[9,128]{1,0:T(8,128)S(1)}, f32[9,128]{1,0:T(8,128)S(1)}, u32[]{:S(2)}, u32[]{:S(2)}) collective-permute-start(f32[9,128]{1,0:T(8,128)S(1)} %get-tuple-element.44), channel_id=1, source_target_pairs={{0,8},{8,0},{16,24},{24,16},{32,40},{40,32},{48,56},{56,48},{64,72... | collective-permute-start | bytes 13832 | tf_op jit(solution)/shard_map/ppermute | solution.py:485
  57.1 5.8 %collective-permute-start.3 = (f32[9,128]{1,0:T(8,128)S(1)}, f32[9,128]{1,0:T(8,128)S(1)}, u32[]{:S(2)}, u32[]{:S(2)}) collective-permute-start(f32[9,128]{1,0:T(8,128)S(1)} %get-tuple-element.45), channel_id=1, source_target_pairs={{8,16},{16,8},{24,32},{32,24},{40,48},{48,40},{56,64},{64,56},{72,... | collective-permute-start | bytes 13832 | tf_op jit(solution)/shard_map/ppermute | solution.py:485
  81.2 2.1 %collective-permute-start.4 = (f32[9,128]{1,0:T(8,128)S(1)}, f32[9,128]{1,0:T(8,128)S(1)}, u32[]{:S(2)}, u32[]{:S(2)}) collective-permute-start(f32[9,128]{1,0:T(8,128)S(1)} %get-tuple-element.48.near_ref), channel_id=1, source_target_pairs={{0,1},{1,0},{2,3},{3,2},{4,5},{5,4},{6,7},{7,6},{8,9},{9,8},{10,11... | collective-permute-start | bytes 13832 | tf_op jit(solution)/shard_map/ppermute | solution.py:485
  82.6 3.1 %collective-permute-start.5 = (f32[9,128]{1,0:T(8,128)S(1)}, f32[9,128]{1,0:T(8,128)S(1)}, u32[]{:S(2)}, u32[]{:S(2)}) collective-permute-start(f32[9,128]{1,0:T(8,128)S(1)} %get-tuple-element.50.far_ref), channel_id=1, source_target_pairs={{1,2},{2,1},{3,4},{4,3},{5,6},{6,5},{7,0},{0,7},{9,10},{10,9},{11,... | collective-permute-start | bytes 13832 | tf_op jit(solution)/shard_map/ppermute | solution.py:485
  85.7 2.6 %collective-permute-start.6 = (f32[9,128]{1,0:T(8,128)S(1)}, f32[9,128]{1,0:T(8,128)S(1)}, u32[]{:S(2)}, u32[]{:S(2)}) collective-permute-start(f32[9,128]{1,0:T(8,128)S(1)} %get-tuple-element.51), channel_id=1, source_target_pairs={{0,8},{8,0},{16,24},{24,16},{32,40},{40,32},{48,56},{56,48},{64,72... | collective-permute-start | bytes 13832 | tf_op jit(solution)/shard_map/ppermute | solution.py:485
  86.1 5.8 %collective-permute-start.7 = (f32[9,128]{1,0:T(8,128)S(1)}, f32[9,128]{1,0:T(8,128)S(1)}, u32[]{:S(2)}, u32[]{:S(2)}) collective-permute-start(f32[9,128]{1,0:T(8,128)S(1)} %get-tuple-element.52), channel_id=1, source_target_pairs={{8,16},{16,8},{24,32},{32,24},{40,48},{48,40},{56,64},{64,56},{72,... | collective-permute-start | bytes 13832 | tf_op jit(solution)/shard_map/ppermute | solution.py:485

commit v5 on v4

--- a/solution.py
+++ b/solution.py
@@ -244,9 +244,12 @@
     sums_ref[...] = spread_sums([squares, counted])
 
 
-def high_z(j, shape):
-    vz = 2 * j + (iota(shape, 1) >> 6)
-    return (vz.astype(F32) + 0.5) * 0.125
+def base_z(lane):
+    return (((lane >> 6) & 1).astype(F32) + 0.5) * 0.125
+
+
+def round_down(value):
+    return value.astype(BF16).astype(F32)
 
 
 def plane_basis(corner, lane):
@@ -258,8 +261,6 @@
 
 
 def force_nodes(misfit_at, inverse, grad_ref, near_ref, mid_ref, far_ref, parts_ref):
-    high = [high_z(j, (1, 128)) for j in range(CHUNKS)]
-
     def block(i, carry):
         at = pl.ds(pl.multiple_of(i * ROWS, ROWS), ROWS)
         pull = []
@@ -268,24 +269,31 @@
             pull.append(misfit / (1.0 + misfit * misfit * inverse))
         for k in range(3):
             force = [pull[j] * grad_ref[k, at, columns(j)] for j in range(CHUNKS)]
-            total = (force[0] + force[1]) + (force[2] + force[3])
-            upper = (force[0] * high[0] + force[1] * high[1]) + (
-                force[2] * high[2] + force[3] * high[3]
-            )
-            for a, value in enumerate((total - upper, upper)):
+            outer = force[2] + force[3]
+            total = (force[0] + force[1]) + outer
+            rising = (force[1] + force[3]) + (outer + outer)
+            for a, value in enumerate((total, rising)):
                 coarse = value.astype(BF16)
                 parts_ref[2 * k + a, at, pl.ds(0, 128)] = coarse
                 parts_ref[2 * k + a, at, pl.ds(128, 128)] = (value - coarse.astype(F32)).astype(BF16)
         return carry
 
     lax.fori_loop(0, BLOCKS, block, 0, unroll=4)
-    corner = iota((16, 256), 0)
-    basis = jnp.where(corner < 4, plane_basis(corner, iota((16, 256), 1)), 0.0).astype(BF16)
-    first = iota((16, 128), 1) == 0
+    rank = iota((16, 256), 0)
+    lane = iota((16, 256), 1)
+    plane = plane_basis(rank & 3, lane)
+    lifted = plane * base_z(lane)
+    coarse = round_down(lifted)
+    total_basis = jnp.where(
+        rank < 4, plane, jnp.where(rank < 8, coarse, jnp.where(rank < 12, lifted - coarse, 0.0))
+    ).astype(BF16)
+    rising_basis = jnp.where(rank < 4, 0.25 * plane, 0.0).astype(BF16)
+    first = iota((4, 128), 1) == 0
     nodes = {}
     for k in range(3):
-        for a in range(2):
-            parts = dot(basis, parts_ref[2 * k + a], NT)
+        total = dot(total_basis, parts_ref[2 * k], NT)
+        upper = total[4:8] + total[8:12] + dot(rising_basis, parts_ref[2 * k + 1], NT)[0:4]
+        for a, parts in enumerate((total[0:4] - upper, upper)):
             for r in range(4):
                 own = parts[:, 128 * r : 128 * r + 128]
                 moved = jnp.where(first, 0.0, pltpu.roll(own, 1, 1))
@@ -388,26 +396,32 @@
             nodes[(z, y)] = jnp.concatenate([direction[k : k + 1] for k in range(3)], axis=1)
     end = (iota((1, 384), 1) & 127) == 127
     shifted = {key: jnp.where(end, 0.0, pltpu.roll(value, 383, 1)) for key, value in nodes.items()}
-    rank = iota((24, 256), 0)
-    lane = iota((24, 256), 1)
-    basis = jnp.where(((rank >> 2) & 1) == (lane >> 7), plane_basis(rank & 3, lane), 0.0).astype(BF16)
+    rank = iota((48, 256), 0)
+    lane = iota((48, 256), 1)
+    upper = (rank & 4) == 4
+    base = base_z(lane)
+    weight = jnp.where(
+        lane < 128, jnp.where(upper, base, 1.0 - base), jnp.where(upper, 0.25, -0.25)
+    )
+    exact = plane_basis(rank & 3, lane) * weight
+    coarse = round_down(exact)
+    basis = jnp.where(rank < 24, coarse, exact - coarse).astype(BF16)
     for r in range(4):
         rows = []
         for corner in range(8):
             key = (r // 2 + corner // 4, r % 2 + corner // 2 % 2)
             rows.append(shifted[key] if corner % 2 else nodes[key])
         full = jnp.concatenate(rows, axis=0)
-        coarse = full.astype(BF16).astype(F32)
+        coarse = round_down(full)
         rest = full - coarse
-        middle = rest.astype(BF16).astype(F32)
-        split = jnp.concatenate([coarse, middle, rest - middle], axis=0)
+        middle = round_down(rest)
+        split = jnp.concatenate([coarse, middle, rest - middle] * 2, axis=0)
         fields_ref[r] = dot(split.astype(BF16), basis, TN)
     if second:
         _, inverse = second_spread(sums_ref, steps_ref)
     else:
         square_sum, counted = gathered_sums(sums_ref, 2)
         inverse = 1.0 / (square_sum / counted + 1e-06)
-    high = [high_z(j, (1, 128)) for j in range(CHUNKS)]
 
     def block(i, carry):
         curve, cross, moved_sum = carry
@@ -417,10 +431,12 @@
         change = [None] * CHUNKS
         for k in range(3):
             cells = pl.ds(pl.multiple_of(128 * k + x, ROWS), ROWS)
-            lower = fields_ref[r, cells, pl.ds(0, 128)]
-            slope = fields_ref[r, cells, pl.ds(128, 128)] - lower
+            field = fields_ref[r, cells, pl.ds(0, 128)]
+            rise = fields_ref[r, cells, pl.ds(128, 128)]
             for j in range(CHUNKS):
-                term = grad_ref[k, at, columns(j)] * (lower + high[j] * slope)
+                if j:
+                    field = field + rise
+                term = grad_ref[k, at, columns(j)] * field
                 change[j] = term if k == 0 else change[j] + term
         for j in range(CHUNKS):
             misfit = misfit_ref[at, columns(j)]

time: 110 us -> 109 us (level)
  no operation moved by 1% of the time
where the time goes in v5:
time: 109 us
  blocking collectives  74.6 us (68%)
  waiting for transfers between devices  15.1 us (14%)
  Pallas kernels  12.2 us (11%)
  starting transfers between devices  6.17 us (6%)
    all_to_all x3, blocking collectives, to_all(): return lax.all_to_all(sums, EVERY, 0, 0, tiled=True)  48.9 us
    ppermute x8, waiting for transfers between devices, swap(): return lax.ppermute(block, axis, route)  15.1 us
    all_to_all x1, blocking collectives, shards(): asked = lax.all_to_all(want, 'slab', 0, 0, tiled=True)  13.8 us
    pallas_call x10, Pallas kernels, call(): pl.pallas_call(body, out_shape=[jax.ShapeDtypeStruct(s, d) for s, d in ou...  12.2 us
    all_to_all x1, blocking collectives, shards(): recv = lax.all_to_all(sent, 'slab', 0, 0, tiled=True)  11.9 us
    ppermute x8, starting transfers between devices, swap(): return lax.ppermute(block, axis, route)  6.17 us
  transfers between devices with their start and end apart: 8, of which 8 were waited for; matrix products, arithmetic and copies ran while one was open for 0% of the time, Pallas kernels for 0%

profile of v5, /device:TPU:1, one launch (start us, length us, event | category | flops | bytes accessed | tf_op | source)
XLA Modules:
  0.0 108.8 jit_solution(4910933417268851065)
XLA Ops:
  0.6 1.3 %wanted.1 = (f32[512,128]{1,0:T(8,128)S(1)}, s32[16,128]{1,0:T(8,128)S(1)}, bf16[512,512]{1,0:T(8,128)(2,1)S(1)}, bf16[128,384]{1,0:T(8,128)(2,1)S(1)}, bf16[256...) custom-call(s32[2,2,128]{2,1,0:T(2,128)} %src_hbm.1, bf16[512,512]{1,0:T(8,128)(2,1)} %bitcast.41), custom_call_target="tpu_custom_call" | custom-call | tf_op jit(solution)/shard_map/wanted/pallas_call | solution.py:32
  1.9 13.8 %all_to_all.55 = s32[16,1,128]{2,1,0:T(1,128)S(1)} all-to-all(s32[16,1,128]{2,1,0:T(1,128)S(1)} %bitcast.37), channel_id=1, replica_groups=mesh['slab'=16,'grp'=8] {'slab'}, dimensions={0} | all-to-all | bytes 16384 | tf_op jit(solution)/shard_map/all_to_all | solution.py:545
  15.7 0.5 pick.1
  16.2 11.9 %all_to_all.56 = bf16[16,32,512]{2,1,0:T(8,128)(2,1)S(1)} all-to-all(bf16[16,32,512]{2,1,0:T(8,128)(2,1)S(1)} %bitcast.24), channel_id=1, replica_groups=mesh['slab'=16,'grp'=8] {'slab'}, dimensions={0} | all-to-all | bytes 1048576 | tf_op jit(solution)/shard_map/all_to_all | solution.py:547
  28.1 3.6 %warp.1 = (f32[3,512,512]{2,1,0:T(8,128)S(1)}, f32[512,512]{1,0:T(8,128)S(1)}, f32[128,128]{1,0:T(8,128)S(1)}) custom-call(f32[512,128]{1,0:T(8,128)S(1)} %get-tuple-element.31.pos_ref, bf16[512,512]{1,0:T(8,128)(2,1)S(1)} %bitcast.23, bf16[128,384]{1,0:T(8,128)(2,1)S(1)} %get-tuple-element.34.level_ref, bf16[256,512]{1,0:T(8,128)(2,1)S(1)} %get-tuple-element.35.inner_ref, ...), custom_call_target="tpu_custom_call" | custom-call | tf_op jit(solution)/shard_map/warp/pallas_call | solution.py:32
  31.8 18.9 %all_to_all.57 = f32[128,1,128]{2,1,0:T(1,128)S(1)} all-to-all(f32[128,1,128]{2,1,0:T(1,128)S(1)} %bitcast.35), channel_id=1, replica_groups=mesh['slab'=16,'grp'=8] {'slab','grp'}, dimensions={0} | all-to-all | bytes 131072 | tf_op jit(solution)/shard_map/all_to_all | solution.py:505
  50.6 1.5 %force_first.1 = (f32[9,128]{1,0:T(8,128)S(1)}, f32[9,128]{1,0:T(8,128)S(1)}, f32[9,128]{1,0:T(8,128)S(1)}) custom-call(f32[128,128]{1,0:T(8,128)S(1)} %bitcast.25, f32[512,512]{1,0:T(8,128)S(1)} %get-tuple-element.39.misfit_ref, f32[3,512,512]{2,1,0:T(8,128)S(1)} %get-tuple-element.40.grad_ref), custom_call_target="tpu_custom_call" | custom-call | tf_op jit(solution)/shard_map/force_first/pallas_call | solution.py:32
  52.2 1.3 %collective-permute-start = (f32[9,128]{1,0:T(8,128)S(1)}, f32[9,128]{1,0:T(8,128)S(1)}, u32[]{:S(2)}, u32[]{:S(2)}) collective-permute-start(f32[9,128]{1,0:T(8,128)S(1)} %get-tuple-element.41.near_ref), channel_id=1, source_target_pairs={{0,1},{1,0},{2,3},{3,2},{4,5},{5,4},{6,7},{7,6},{8,9},{9,8},{10,11... | collective-permute-start | bytes 13832 | tf_op jit(solution)/shard_map/ppermute | solution.py:501
  53.5 0.1 collective-permute-start.1
  53.5 0.8 collective-permute-done.below_ref
  54.3 2.2 %collective-permute-done.1.above_ref = f32[9,128]{1,0:T(8,128)S(1)} collective-permute-done((f32[9,128]{1,0:T(8,128)S(1)}, f32[9,128]{1,0:T(8,128)S(1)}, u32[]{:S(2)}, u32[]{:S(2)}) %collective-permute-start.1) | collective-permute-done | bytes 4640 | tf_op jit(solution)/shard_map/ppermute | solution.py:501
  56.6 0.4 collective-permute-start.2
  57.0 1.3 %collective-permute-start.3 = (f32[9,128]{1,0:T(8,128)S(1)}, f32[9,128]{1,0:T(8,128)S(1)}, u32[]{:S(2)}, u32[]{:S(2)}) collective-permute-start(f32[9,128]{1,0:T(8,128)S(1)} %get-tuple-element.45), channel_id=1, source_target_pairs={{8,16},{16,8},{24,32},{32,24},{40,48},{48,40},{56,64},{64,56},{72,... | collective-permute-start | bytes 13832 | tf_op jit(solution)/shard_map/ppermute | solution.py:501
  58.3 0.9 collective-permute-done.2.under_ref
  59.1 3.7 %collective-permute-done.3.over_ref = f32[9,128]{1,0:T(8,128)S(1)} collective-permute-done((f32[9,128]{1,0:T(8,128)S(1)}, f32[9,128]{1,0:T(8,128)S(1)}, u32[]{:S(2)}, u32[]{:S(2)}) %collective-permute-start.3) | collective-permute-done | bytes 4640 | tf_op jit(solution)/shard_map/ppermute | solution.py:501
  62.8 1.3 %move_first.1 = (f32[512,512]{1,0:T(8,128)S(1)}, f32[128,128]{1,0:T(8,128)S(1)}, f32[3,2,2,128]{3,2,1,0:T(2,128)S(1)}) custom-call(f32[9,128]{1,0:T(8,128)S(1)} %get-tuple-element.41.near_ref, f32[9,128]{1,0:T(8,128)S(1)} %get-tuple-element.42.mid_ref, f32[9,128]{1,0:T(8,128)S(1)} %get-tuple-element.43.far_ref, f32[9,128]{1,0:T(8,128)S(1)} %collective-permute-done.below_ref, ...), custom_call_target="tpu_custom_call" | custom-call | tf_op jit(solution)/shard_map/move_first/pallas_call | solution.py:32
  64.1 15.0 %all_to_all.58 = f32[128,1,128]{2,1,0:T(1,128)S(1)} all-to-all(f32[128,1,128]{2,1,0:T(1,128)S(1)} %bitcast.34), channel_id=1, replica_groups=mesh['slab'=16,'grp'=8] {'slab','grp'}, dimensions={0} | all-to-all | bytes 131072 | tf_op jit(solution)/shard_map/all_to_all | solution.py:505
  79.2 1.6 %force_second.1 = (f32[9,128]{1,0:T(8,128)S(1)}, f32[9,128]{1,0:T(8,128)S(1)}, f32[9,128]{1,0:T(8,128)S(1)}, f32[512,512]{1,0:T(8,128)S(1)}) custom-call(f32[128,128]{1,0:T(8,128)S(1)} %bitcast.27, f32[128,128]{1,0:T(8,128)S(1)} %bitcast.29, f32[512,512]{1,0:T(8,128)S(1)} %get-tuple-element.39.misfit_ref, f32[512,512]{1,0:T(8,128)S(1)} %get-tuple-element.47.change_ref, ...), custom_call_target="tpu_custom_call" | custom-call | tf_op jit(solution)/shard_map/force_second/pallas_call | solution.py:32
  80.8 1.3 %collective-permute-start.4 = (f32[9,128]{1,0:T(8,128)S(1)}, f32[9,128]{1,0:T(8,128)S(1)}, u32[]{:S(2)}, u32[]{:S(2)}) collective-permute-start(f32[9,128]{1,0:T(8,128)S(1)} %get-tuple-element.48.near_ref), channel_id=1, source_target_pairs={{0,1},{1,0},{2,3},{3,2},{4,5},{5,4},{6,7},{7,6},{8,9},{9,8},{10,11... | collective-permute-start | bytes 13832 | tf_op jit(solution)/shard_map/ppermute | solution.py:501
  82.1 0.1 collective-permute-start.5
  82.1 0.8 collective-permute-done.4.below_ref
  82.9 2.2 %collective-permute-done.5.above_ref = f32[9,128]{1,0:T(8,128)S(1)} collective-permute-done((f32[9,128]{1,0:T(8,128)S(1)}, f32[9,128]{1,0:T(8,128)S(1)}, u32[]{:S(2)}, u32[]{:S(2)}) %collective-permute-start.5) | collective-permute-done | bytes 4640 | tf_op jit(solution)/shard_map/ppermute | solution.py:501
  85.2 0.4 collective-permute-start.6
  85.6 1.3 %collective-permute-start.7 = (f32[9,128]{1,0:T(8,128)S(1)}, f32[9,128]{1,0:T(8,128)S(1)}, u32[]{:S(2)}, u32[]{:S(2)}) collective-permute-start(f32[9,128]{1,0:T(8,128)S(1)} %get-tuple-element.52), channel_id=1, source_target_pairs={{8,16},{16,8},{24,32},{32,24},{40,48},{48,40},{56,64},{64,56},{72,... | collective-permute-start | bytes 13832 | tf_op jit(solution)/shard_map/ppermute | solution.py:501
  86.9 0.9 collective-permute-done.6.under_ref
  87.8 3.7 %collective-permute-done.7.over_ref = f32[9,128]{1,0:T(8,128)S(1)} collective-permute-done((f32[9,128]{1,0:T(8,128)S(1)}, f32[9,128]{1,0:T(8,128)S(1)}, u32[]{:S(2)}, u32[]{:S(2)}) %collective-permute-start.7) | collective-permute-done | bytes 4640 | tf_op jit(solution)/shard_map/ppermute | solution.py:501
  91.4 1.2 %move_second.1 = (f32[512,512]{1,0:T(8,128)S(1)}, f32[128,128]{1,0:T(8,128)S(1)}, f32[3,2,2,128]{3,2,1,0:T(2,128)S(1)}) custom-call(f32[9,128]{1,0:T(8,128)S(1)} %get-tuple-element.48.near_ref, f32[9,128]{1,0:T(8,128)S(1)} %get-tuple-element.49.mid_ref, f32[9,128]{1,0:T(8,128)S(1)} %get-tuple-element.50.far_ref, ...), custom_call_target="tpu_custom_call" | custom-call | tf_op jit(solution)/shard_map/move_second/pallas_call | solution.py:32
  92.6 15.0 %all_to_all.59 = f32[128,1,128]{2,1,0:T(1,128)S(1)} all-to-all(f32[128,1,128]{2,1,0:T(1,128)S(1)} %bitcast.33), channel_id=1, replica_groups=mesh['slab'=16,'grp'=8] {'slab','grp'}, dimensions={0} | all-to-all | bytes 131072 | tf_op jit(solution)/shard_map/all_to_all | solution.py:505
  107.7 1.2 %finish.1 = (f32[3,2,2,128]{3,2,1,0:T(2,128)}, f32[512,512]{1,0:T(8,128)}) custom-call(f32[128,128]{1,0:T(8,128)S(1)} %bitcast.31, f32[128,128]{1,0:T(8,128)S(1)} %bitcast.32, f32[3,2,2,128]{3,2,1,0:T(2,128)S(1)} %get-tuple-element.55.dir0_ref, f32[3,2,2,128]{3,2,1,0:T(2,128)S(1)} %get-tuple-element.56.dir1_ref, ...), custom_call_target="tpu_custom_call" | custom-call | tf_op jit(solution)/shard_map/finish/pallas_call | solution.py:32
  (2 shorter events, 0.0 us)
Async XLA Ops:
  52.2 2.1 %collective-permute-start = (f32[9,128]{1,0:T(8,128)S(1)}, f32[9,128]{1,0:T(8,128)S(1)}, u32[]{:S(2)}, u32[]{:S(2)}) collective-permute-start(f32[9,128]{1,0:T(8,128)S(1)} %get-tuple-element.41.near_ref), channel_id=1, source_target_pairs={{0,1},{1,0},{2,3},{3,2},{4,5},{5,4},{6,7},{7,6},{8,9},{9,8},{10,11... | collective-permute-start | bytes 13832 | tf_op jit(solution)/shard_map/ppermute | solution.py:501
  53.5 3.1 %collective-permute-start.1 = (f32[9,128]{1,0:T(8,128)S(1)}, f32[9,128]{1,0:T(8,128)S(1)}, u32[]{:S(2)}, u32[]{:S(2)}) collective-permute-start(f32[9,128]{1,0:T(8,128)S(1)} %get-tuple-element.43.far_ref), channel_id=1, source_target_pairs={{1,2},{2,1},{3,4},{4,3},{5,6},{6,5},{7,0},{0,7},{9,10},{10,9},{11,... | collective-permute-start | bytes 13832 | tf_op jit(solution)/shard_map/ppermute | solution.py:501
  56.6 2.6 %collective-permute-start.2 = (f32[9,128]{1,0:T(8,128)S(1)}, f32[9,128]{1,0:T(8,128)S(1)}, u32[]{:S(2)}, u32[]{:S(2)}) collective-permute-start(f32[9,128]{1,0:T(8,128)S(1)} %get-tuple-element.44), channel_id=1, source_target_pairs={{0,8},{8,0},{16,24},{24,16},{32,40},{40,32},{48,56},{56,48},{64,72... | collective-permute-start | bytes 13832 | tf_op jit(solution)/shard_map/ppermute | solution.py:501
  57.0 5.8 %collective-permute-start.3 = (f32[9,128]{1,0:T(8,128)S(1)}, f32[9,128]{1,0:T(8,128)S(1)}, u32[]{:S(2)}, u32[]{:S(2)}) collective-permute-start(f32[9,128]{1,0:T(8,128)S(1)} %get-tuple-element.45), channel_id=1, source_target_pairs={{8,16},{16,8},{24,32},{32,24},{40,48},{48,40},{56,64},{64,56},{72,... | collective-permute-start | bytes 13832 | tf_op jit(solution)/shard_map/ppermute | solution.py:501
  80.8 2.1 %collective-permute-start.4 = (f32[9,128]{1,0:T(8,128)S(1)}, f32[9,128]{1,0:T(8,128)S(1)}, u32[]{:S(2)}, u32[]{:S(2)}) collective-permute-start(f32[9,128]{1,0:T(8,128)S(1)} %get-tuple-element.48.near_ref), channel_id=1, source_target_pairs={{0,1},{1,0},{2,3},{3,2},{4,5},{5,4},{6,7},{7,6},{8,9},{9,8},{10,11... | collective-permute-start | bytes 13832 | tf_op jit(solution)/shard_map/ppermute | solution.py:501
  82.1 3.1 %collective-permute-start.5 = (f32[9,128]{1,0:T(8,128)S(1)}, f32[9,128]{1,0:T(8,128)S(1)}, u32[]{:S(2)}, u32[]{:S(2)}) collective-permute-start(f32[9,128]{1,0:T(8,128)S(1)} %get-tuple-element.50.far_ref), channel_id=1, source_target_pairs={{1,2},{2,1},{3,4},{4,3},{5,6},{6,5},{7,0},{0,7},{9,10},{10,9},{11,... | collective-permute-start | bytes 13832 | tf_op jit(solution)/shard_map/ppermute | solution.py:501
  85.2 2.6 %collective-permute-start.6 = (f32[9,128]{1,0:T(8,128)S(1)}, f32[9,128]{1,0:T(8,128)S(1)}, u32[]{:S(2)}, u32[]{:S(2)}) collective-permute-start(f32[9,128]{1,0:T(8,128)S(1)} %get-tuple-element.51), channel_id=1, source_target_pairs={{0,8},{8,0},{16,24},{24,16},{32,40},{40,32},{48,56},{56,48},{64,72... | collective-permute-start | bytes 13832 | tf_op jit(solution)/shard_map/ppermute | solution.py:501
  85.6 5.8 %collective-permute-start.7 = (f32[9,128]{1,0:T(8,128)S(1)}, f32[9,128]{1,0:T(8,128)S(1)}, u32[]{:S(2)}, u32[]{:S(2)}) collective-permute-start(f32[9,128]{1,0:T(8,128)S(1)} %get-tuple-element.52), channel_id=1, source_target_pairs={{8,16},{16,8},{24,32},{32,24},{40,48},{48,40},{56,64},{64,56},{72,... | collective-permute-start | bytes 13832 | tf_op jit(solution)/shard_map/ppermute | solution.py:501

commit v6 on v5

--- a/solution.py
+++ b/solution.py
@@ -370,7 +370,7 @@
 
 def move_body(
     near_ref, mid_ref, far_ref, below_ref, above_ref, under_ref, over_ref,
-    sums_ref, steps_ref, misfit_ref, grad_ref, change_ref, out_ref, dir_ref, fields_ref, second,
+    robust_ref, misfit_ref, grad_ref, change_ref, out_ref, dir_ref, fields_ref, second,
 ):
     slab = lax.axis_index("slab")
     last = lax.axis_size("slab") - 1
@@ -417,12 +417,6 @@
         middle = round_down(rest)
         split = jnp.concatenate([coarse, middle, rest - middle] * 2, axis=0)
         fields_ref[r] = dot(split.astype(BF16), basis, TN)
-    if second:
-        _, inverse = second_spread(sums_ref, steps_ref)
-    else:
-        square_sum, counted = gathered_sums(sums_ref, 2)
-        inverse = 1.0 / (square_sum / counted + 1e-06)
-
     def block(i, carry):
         curve, cross, moved_sum = carry
         at = pl.ds(pl.multiple_of(i * ROWS, ROWS), ROWS)
@@ -439,10 +433,10 @@
                 term = grad_ref[k, at, columns(j)] * field
                 change[j] = term if k == 0 else change[j] + term
         for j in range(CHUNKS):
-            misfit = misfit_ref[at, columns(j)]
+            misfit = None if second else misfit_ref[at, columns(j)]
             change_ref[at, columns(j)] = change[j]
             square = change[j] * change[j]
-            curve = curve + square / (1.0 + misfit * misfit * inverse)
+            curve = curve + square * robust_ref[at, columns(j)]
             if not second:
                 cross = cross + misfit * change[j]
                 moved_sum = moved_sum + square
@@ -455,22 +449,42 @@
 
 def first_move_body(
     near_ref, mid_ref, far_ref, below_ref, above_ref, under_ref, over_ref,
-    sums_ref, misfit_ref, grad_ref, change_ref, out_ref, dir_ref, fields_ref,
+    robust_ref, misfit_ref, grad_ref, change_ref, out_ref, dir_ref, fields_ref,
 ):
     move_body(
         near_ref, mid_ref, far_ref, below_ref, above_ref, under_ref, over_ref,
-        sums_ref, None, misfit_ref, grad_ref, change_ref, out_ref, dir_ref, fields_ref, False,
+        robust_ref, misfit_ref, grad_ref, change_ref, out_ref, dir_ref, fields_ref, False,
     )
 
 
 def second_move_body(
     near_ref, mid_ref, far_ref, below_ref, above_ref, under_ref, over_ref,
-    sums_ref, steps_ref, misfit_ref, grad_ref, change_ref, out_ref, dir_ref, fields_ref,
+    robust_ref, grad_ref, change_ref, out_ref, dir_ref, fields_ref,
 ):
     move_body(
         near_ref, mid_ref, far_ref, below_ref, above_ref, under_ref, over_ref,
-        sums_ref, steps_ref, misfit_ref, grad_ref, change_ref, out_ref, dir_ref, fields_ref, True,
-    )
+        robust_ref, None, grad_ref, change_ref, out_ref, dir_ref, fields_ref, True,
+    )
+
+
+def weigh(misfit_ref, inverse, out_ref):
+    def block(i, carry):
+        at = pl.ds(pl.multiple_of(i * ROWS, ROWS), ROWS)
+        misfit = misfit_ref[at, :]
+        out_ref[at, :] = 1.0 / (1.0 + misfit * misfit * inverse)
+        return carry
+
+    lax.fori_loop(0, BLOCKS, block, 0, unroll=4)
+
+
+def first_weigh_body(after_ref, sums_ref, misfit_ref, out_ref):
+    square_sum, counted = gathered_sums(sums_ref, 2)
+    weigh(misfit_ref, 1.0 / (square_sum / counted + 1e-06), out_ref)
+
+
+def second_weigh_body(after_ref, sums_ref, steps_ref, misfit_ref, out_ref):
+    _, inverse = second_spread(sums_ref, steps_ref)
+    weigh(misfit_ref, inverse, out_ref)
 
 
 def finish_body(
@@ -511,7 +525,7 @@
     pair, cross = call(edge_body, [((9, 128), F32)] * 2, (near, mid, far, below, above), "edges")
     under = swap(pair, "slab", 0)
     over = swap(cross, "slab", 1)
-    return below, above, under, over
+    return below, above, under, over, pair
 
 
 def shards(reference_bricks, deformed, tap_weights, valid_voxels, sources):
@@ -564,11 +578,12 @@
     )
     sums = to_all(sums)
     near, mid, far = call(first_force_body, nodes_shape, (sums, misfit, grads), "force_first", parts)
-    below, above, under, over = halo(near, mid, far)
+    below, above, under, over, pair = halo(near, mid, far)
+    (robust,) = call(first_weigh_body, [big], (pair, sums, misfit), "weigh_first")
     change, steps, dir0 = call(
         first_move_body,
         [big, sums_shape, dir_shape],
-        (near, mid, far, below, above, under, over, sums, misfit, grads),
+        (near, mid, far, below, above, under, over, robust, misfit, grads),
         "move_first",
         fields,
     )
@@ -580,11 +595,12 @@
         "force_second",
         parts,
     )
-    below, above, under, over = halo(near, mid, far)
+    below, above, under, over, pair = halo(near, mid, far)
+    (robust,) = call(second_weigh_body, [big], (pair, sums, first, misfit), "weigh_second")
     change, steps, dir1 = call(
         second_move_body,
         [big, sums_shape, dir_shape],
-        (near, mid, far, below, above, under, over, sums, first, misfit, grads),
+        (near, mid, far, below, above, under, over, robust, grads),
         "move_second",
         fields,
     )

time: 109 us -> 108 us (level)
    pallas_call x10 -> x12, Pallas kernels: 12.2 us -> 12.8 us  [call(): pl.pallas_call(body, out_shape=[jax.ShapeDtypeStruct(s, d) for s, d in ou...]
  transfers between devices with their start and end apart: 8 -> 8, of which waited for: 8 -> 6; matrix products, arithmetic and copies ran while one was open for 0% -> 0% of each run, Pallas kernels for 0% -> 1%
where the time goes in v6:
time: 108 us; the launch traced here: 107 us
  blocking collectives  74.1 us (69%)
  waiting for transfers between devices  14.7 us (14%)
  Pallas kernels  12.8 us (12%)
  starting transfers between devices  5.12 us (5%)
    all_to_all x3, blocking collectives, to_all(): return lax.all_to_all(sums, EVERY, 0, 0, tiled=True)  48.3 us
    ppermute x8, waiting for transfers between devices, swap(): return lax.ppermute(block, axis, route)  14.7 us
    all_to_all x1, blocking collectives, shards(): asked = lax.all_to_all(want, 'slab', 0, 0, tiled=True)  13.8 us
    pallas_call x12, Pallas kernels, call(): pl.pallas_call(body, out_shape=[jax.ShapeDtypeStruct(s, d) for s, d in ou...  12.8 us
    all_to_all x1, blocking collectives, shards(): recv = lax.all_to_all(sent, 'slab', 0, 0, tiled=True)  11.9 us
    ppermute x8, starting transfers between devices, swap(): return lax.ppermute(block, axis, route)  5.12 us
  transfers between devices with their start and end apart: 8, of which 6 were waited for; matrix products, arithmetic and copies ran while one was open for 0% of the time, Pallas kernels for 1%

profile of v6, /device:TPU:1, one launch (start us, length us, event | category | flops | bytes accessed | tf_op | source)
XLA Modules:
  0.0 107.3 jit_solution(14650398746018557824)
XLA Ops:
  0.6 1.3 %wanted.1 = (f32[512,128]{1,0:T(8,128)S(1)}, s32[16,128]{1,0:T(8,128)S(1)}, bf16[512,512]{1,0:T(8,128)(2,1)S(1)}, bf16[128,384]{1,0:T(8,128)(2,1)S(1)}, bf16[256...) custom-call(s32[2,2,128]{2,1,0:T(2,128)} %src_hbm.1, bf16[512,512]{1,0:T(8,128)(2,1)} %bitcast.41), custom_call_target="tpu_custom_call" | custom-call | tf_op jit(solution)/shard_map/wanted/pallas_call | solution.py:32
  1.9 13.8 %all_to_all.55 = s32[16,1,128]{2,1,0:T(1,128)S(1)} all-to-all(s32[16,1,128]{2,1,0:T(1,128)S(1)} %bitcast.37), channel_id=1, replica_groups=mesh['slab'=16,'grp'=8] {'slab'}, dimensions={0} | all-to-all | bytes 16384 | tf_op jit(solution)/shard_map/all_to_all | solution.py:559
  15.7 0.5 pick.1
  16.2 11.9 %all_to_all.56 = bf16[16,32,512]{2,1,0:T(8,128)(2,1)S(1)} all-to-all(bf16[16,32,512]{2,1,0:T(8,128)(2,1)S(1)} %bitcast.24), channel_id=1, replica_groups=mesh['slab'=16,'grp'=8] {'slab'}, dimensions={0} | all-to-all | bytes 1048576 | tf_op jit(solution)/shard_map/all_to_all | solution.py:561
  28.1 3.6 %warp.1 = (f32[3,512,512]{2,1,0:T(8,128)S(1)}, f32[512,512]{1,0:T(8,128)S(1)}, f32[128,128]{1,0:T(8,128)S(1)}) custom-call(f32[512,128]{1,0:T(8,128)S(1)} %get-tuple-element.31.pos_ref, bf16[512,512]{1,0:T(8,128)(2,1)S(1)} %bitcast.23, bf16[128,384]{1,0:T(8,128)(2,1)S(1)} %get-tuple-element.34.level_ref, bf16[256,512]{1,0:T(8,128)(2,1)S(1)} %get-tuple-element.35.inner_ref, ...), custom_call_target="tpu_custom_call" | custom-call | tf_op jit(solution)/shard_map/warp/pallas_call | solution.py:32
  31.8 18.9 %all_to_all.57 = f32[128,1,128]{2,1,0:T(1,128)S(1)} all-to-all(f32[128,1,128]{2,1,0:T(1,128)S(1)} %bitcast.35), channel_id=1, replica_groups=mesh['slab'=16,'grp'=8] {'slab','grp'}, dimensions={0} | all-to-all | bytes 131072 | tf_op jit(solution)/shard_map/all_to_all | solution.py:519
  50.6 1.5 %force_first.1 = (f32[9,128]{1,0:T(8,128)S(1)}, f32[9,128]{1,0:T(8,128)S(1)}, f32[9,128]{1,0:T(8,128)S(1)}) custom-call(f32[128,128]{1,0:T(8,128)S(1)} %bitcast.25, f32[512,512]{1,0:T(8,128)S(1)} %get-tuple-element.39.misfit_ref, f32[3,512,512]{2,1,0:T(8,128)S(1)} %get-tuple-element.40.grad_ref), custom_call_target="tpu_custom_call" | custom-call | tf_op jit(solution)/shard_map/force_first/pallas_call | solution.py:32
  52.2 1.3 %collective-permute-start = (f32[9,128]{1,0:T(8,128)S(1)}, f32[9,128]{1,0:T(8,128)S(1)}, u32[]{:S(2)}, u32[]{:S(2)}) collective-permute-start(f32[9,128]{1,0:T(8,128)S(1)} %get-tuple-element.41.near_ref), channel_id=1, source_target_pairs={{0,1},{1,0},{2,3},{3,2},{4,5},{5,4},{6,7},{7,6},{8,9},{9,8},{10,11... | collective-permute-start | bytes 13832 | tf_op jit(solution)/shard_map/ppermute | solution.py:515
  53.5 0.1 collective-permute-start.1
  53.5 0.8 collective-permute-done.below_ref
  54.3 2.2 %collective-permute-done.1.above_ref = f32[9,128]{1,0:T(8,128)S(1)} collective-permute-done((f32[9,128]{1,0:T(8,128)S(1)}, f32[9,128]{1,0:T(8,128)S(1)}, u32[]{:S(2)}, u32[]{:S(2)}) %collective-permute-start.1) | collective-permute-done | bytes 4640 | tf_op jit(solution)/shard_map/ppermute | solution.py:515
  56.6 1.2 %collective-permute-start.3 = (f32[9,128]{1,0:T(8,128)S(1)}, f32[9,128]{1,0:T(8,128)S(1)}, u32[]{:S(2)}, u32[]{:S(2)}) collective-permute-start(f32[9,128]{1,0:T(8,128)S(1)} %get-tuple-element.45), channel_id=1, source_target_pairs={{8,16},{16,8},{24,32},{32,24},{40,48},{48,40},{56,64},{64,56},{72,... | collective-permute-start | bytes 13832 | tf_op jit(solution)/shard_map/ppermute | solution.py:515
  57.7 0.0 collective-permute-start.2
  57.7 0.4 weigh_first.1.robust_ref
  58.1 4.3 %collective-permute-done.3.over_ref = f32[9,128]{1,0:T(8,128)S(1)} collective-permute-done((f32[9,128]{1,0:T(8,128)S(1)}, f32[9,128]{1,0:T(8,128)S(1)}, u32[]{:S(2)}, u32[]{:S(2)}) %collective-permute-start.3) | collective-permute-done | bytes 4640 | tf_op jit(solution)/shard_map/ppermute | solution.py:515
  62.5 0.0 collective-permute-done.2.under_ref
  62.5 1.2 %move_first.1 = (f32[512,512]{1,0:T(8,128)S(1)}, f32[128,128]{1,0:T(8,128)S(1)}, f32[3,2,2,128]{3,2,1,0:T(2,128)S(1)}) custom-call(f32[9,128]{1,0:T(8,128)S(1)} %get-tuple-element.41.near_ref, f32[9,128]{1,0:T(8,128)S(1)} %get-tuple-element.42.mid_ref, f32[9,128]{1,0:T(8,128)S(1)} %get-tuple-element.43.far_ref, f32[9,128]{1,0:T(8,128)S(1)} %collective-permute-done.below_ref, ...), custom_call_target="tpu_custom_call" | custom-call | tf_op jit(solution)/shard_map/move_first/pallas_call | solution.py:32
  63.7 14.7 %all_to_all.58 = f32[128,1,128]{2,1,0:T(1,128)S(1)} all-to-all(f32[128,1,128]{2,1,0:T(1,128)S(1)} %bitcast.34), channel_id=1, replica_groups=mesh['slab'=16,'grp'=8] {'slab','grp'}, dimensions={0} | all-to-all | bytes 131072 | tf_op jit(solution)/shard_map/all_to_all | solution.py:519
  78.4 1.6 %force_second.1 = (f32[9,128]{1,0:T(8,128)S(1)}, f32[9,128]{1,0:T(8,128)S(1)}, f32[9,128]{1,0:T(8,128)S(1)}, f32[512,512]{1,0:T(8,128)S(1)}) custom-call(f32[128,128]{1,0:T(8,128)S(1)} %bitcast.27, f32[128,128]{1,0:T(8,128)S(1)} %bitcast.29, f32[512,512]{1,0:T(8,128)S(1)} %get-tuple-element.39.misfit_ref, f32[512,512]{1,0:T(8,128)S(1)} %get-tuple-element.47.change_ref, ...), custom_call_target="tpu_custom_call" | custom-call | tf_op jit(solution)/shard_map/force_second/pallas_call | solution.py:32
  80.0 1.3 %collective-permute-start.4 = (f32[9,128]{1,0:T(8,128)S(1)}, f32[9,128]{1,0:T(8,128)S(1)}, u32[]{:S(2)}, u32[]{:S(2)}) collective-permute-start(f32[9,128]{1,0:T(8,128)S(1)} %get-tuple-element.48.near_ref), channel_id=1, source_target_pairs={{0,1},{1,0},{2,3},{3,2},{4,5},{5,4},{6,7},{7,6},{8,9},{9,8},{10,11... | collective-permute-start | bytes 13832 | tf_op jit(solution)/shard_map/ppermute | solution.py:515
  81.3 0.1 collective-permute-start.5
  81.4 0.8 collective-permute-done.4.below_ref
  82.1 2.2 %collective-permute-done.5.above_ref = f32[9,128]{1,0:T(8,128)S(1)} collective-permute-done((f32[9,128]{1,0:T(8,128)S(1)}, f32[9,128]{1,0:T(8,128)S(1)}, u32[]{:S(2)}, u32[]{:S(2)}) %collective-permute-start.5) | collective-permute-done | bytes 4640 | tf_op jit(solution)/shard_map/ppermute | solution.py:515
  84.4 1.2 %collective-permute-start.7 = (f32[9,128]{1,0:T(8,128)S(1)}, f32[9,128]{1,0:T(8,128)S(1)}, u32[]{:S(2)}, u32[]{:S(2)}) collective-permute-start(f32[9,128]{1,0:T(8,128)S(1)} %get-tuple-element.52), channel_id=1, source_target_pairs={{8,16},{16,8},{24,32},{32,24},{40,48},{48,40},{56,64},{64,56},{72,... | collective-permute-start | bytes 13832 | tf_op jit(solution)/shard_map/ppermute | solution.py:515
  85.6 0.0 collective-permute-start.6
  85.6 0.4 weigh_second.1.robust_ref
  86.0 4.3 %collective-permute-done.7.over_ref = f32[9,128]{1,0:T(8,128)S(1)} collective-permute-done((f32[9,128]{1,0:T(8,128)S(1)}, f32[9,128]{1,0:T(8,128)S(1)}, u32[]{:S(2)}, u32[]{:S(2)}) %collective-permute-start.7) | collective-permute-done | bytes 4640 | tf_op jit(solution)/shard_map/ppermute | solution.py:515
  90.3 0.0 collective-permute-done.6.under_ref
  90.3 1.1 %move_second.1 = (f32[512,512]{1,0:T(8,128)S(1)}, f32[128,128]{1,0:T(8,128)S(1)}, f32[3,2,2,128]{3,2,1,0:T(2,128)S(1)}) custom-call(f32[9,128]{1,0:T(8,128)S(1)} %get-tuple-element.48.near_ref, f32[9,128]{1,0:T(8,128)S(1)} %get-tuple-element.49.mid_ref, f32[9,128]{1,0:T(8,128)S(1)} %get-tuple-element.50.far_ref, ...), custom_call_target="tpu_custom_call" | custom-call | tf_op jit(solution)/shard_map/move_second/pallas_call | solution.py:32
  91.4 14.7 %all_to_all.59 = f32[128,1,128]{2,1,0:T(1,128)S(1)} all-to-all(f32[128,1,128]{2,1,0:T(1,128)S(1)} %bitcast.33), channel_id=1, replica_groups=mesh['slab'=16,'grp'=8] {'slab','grp'}, dimensions={0} | all-to-all | bytes 131072 | tf_op jit(solution)/shard_map/all_to_all | solution.py:519
  106.2 1.2 %finish.1 = (f32[3,2,2,128]{3,2,1,0:T(2,128)}, f32[512,512]{1,0:T(8,128)}) custom-call(f32[128,128]{1,0:T(8,128)S(1)} %bitcast.31, f32[128,128]{1,0:T(8,128)S(1)} %bitcast.32, f32[3,2,2,128]{3,2,1,0:T(2,128)S(1)} %get-tuple-element.55.dir0_ref, f32[3,2,2,128]{3,2,1,0:T(2,128)S(1)} %get-tuple-element.56.dir1_ref, ...), custom_call_target="tpu_custom_call" | custom-call | tf_op jit(solution)/shard_map/finish/pallas_call | solution.py:32
  (2 shorter events, 0.0 us)
Async XLA Ops:
  52.2 2.1 %collective-permute-start = (f32[9,128]{1,0:T(8,128)S(1)}, f32[9,128]{1,0:T(8,128)S(1)}, u32[]{:S(2)}, u32[]{:S(2)}) collective-permute-start(f32[9,128]{1,0:T(8,128)S(1)} %get-tuple-element.41.near_ref), channel_id=1, source_target_pairs={{0,1},{1,0},{2,3},{3,2},{4,5},{5,4},{6,7},{7,6},{8,9},{9,8},{10,11... | collective-permute-start | bytes 13832 | tf_op jit(solution)/shard_map/ppermute | solution.py:515
  53.5 3.1 %collective-permute-start.1 = (f32[9,128]{1,0:T(8,128)S(1)}, f32[9,128]{1,0:T(8,128)S(1)}, u32[]{:S(2)}, u32[]{:S(2)}) collective-permute-start(f32[9,128]{1,0:T(8,128)S(1)} %get-tuple-element.43.far_ref), channel_id=1, source_target_pairs={{1,2},{2,1},{3,4},{4,3},{5,6},{6,5},{7,0},{0,7},{9,10},{10,9},{11,... | collective-permute-start | bytes 13832 | tf_op jit(solution)/shard_map/ppermute | solution.py:515
  56.6 5.9 %collective-permute-start.3 = (f32[9,128]{1,0:T(8,128)S(1)}, f32[9,128]{1,0:T(8,128)S(1)}, u32[]{:S(2)}, u32[]{:S(2)}) collective-permute-start(f32[9,128]{1,0:T(8,128)S(1)} %get-tuple-element.45), channel_id=1, source_target_pairs={{8,16},{16,8},{24,32},{32,24},{40,48},{48,40},{56,64},{64,56},{72,... | collective-permute-start | bytes 13832 | tf_op jit(solution)/shard_map/ppermute | solution.py:515
  57.7 4.7 %collective-permute-start.2 = (f32[9,128]{1,0:T(8,128)S(1)}, f32[9,128]{1,0:T(8,128)S(1)}, u32[]{:S(2)}, u32[]{:S(2)}) collective-permute-start(f32[9,128]{1,0:T(8,128)S(1)} %get-tuple-element.44.after_ref), channel_id=1, source_target_pairs={{0,8},{8,0},{16,24},{24,16},{32,40},{40,32},{48,56},{56,48},{64,72... | collective-permute-start | bytes 13832 | tf_op jit(solution)/shard_map/ppermute | solution.py:515
  80.0 2.1 %collective-permute-start.4 = (f32[9,128]{1,0:T(8,128)S(1)}, f32[9,128]{1,0:T(8,128)S(1)}, u32[]{:S(2)}, u32[]{:S(2)}) collective-permute-start(f32[9,128]{1,0:T(8,128)S(1)} %get-tuple-element.48.near_ref), channel_id=1, source_target_pairs={{0,1},{1,0},{2,3},{3,2},{4,5},{5,4},{6,7},{7,6},{8,9},{9,8},{10,11... | collective-permute-start | bytes 13832 | tf_op jit(solution)/shard_map/ppermute | solution.py:515
  81.3 3.1 %collective-permute-start.5 = (f32[9,128]{1,0:T(8,128)S(1)}, f32[9,128]{1,0:T(8,128)S(1)}, u32[]{:S(2)}, u32[]{:S(2)}) collective-permute-start(f32[9,128]{1,0:T(8,128)S(1)} %get-tuple-element.50.far_ref), channel_id=1, source_target_pairs={{1,2},{2,1},{3,4},{4,3},{5,6},{6,5},{7,0},{0,7},{9,10},{10,9},{11,... | collective-permute-start | bytes 13832 | tf_op jit(solution)/shard_map/ppermute | solution.py:515
  84.4 5.9 %collective-permute-start.7 = (f32[9,128]{1,0:T(8,128)S(1)}, f32[9,128]{1,0:T(8,128)S(1)}, u32[]{:S(2)}, u32[]{:S(2)}) collective-permute-start(f32[9,128]{1,0:T(8,128)S(1)} %get-tuple-element.52), channel_id=1, source_target_pairs={{8,16},{16,8},{24,32},{32,24},{40,48},{48,40},{56,64},{64,56},{72,... | collective-permute-start | bytes 13832 | tf_op jit(solution)/shard_map/ppermute | solution.py:515
  85.6 4.7 %collective-permute-start.6 = (f32[9,128]{1,0:T(8,128)S(1)}, f32[9,128]{1,0:T(8,128)S(1)}, u32[]{:S(2)}, u32[]{:S(2)}) collective-permute-start(f32[9,128]{1,0:T(8,128)S(1)} %get-tuple-element.51.after_ref), channel_id=1, source_target_pairs={{0,8},{8,0},{16,24},{24,16},{32,40},{40,32},{48,56},{56,48},{64,72... | collective-permute-start | bytes 13832 | tf_op jit(solution)/shard_map/ppermute | solution.py:515

commit v7 on v6

--- a/solution.py
+++ b/solution.py
@@ -477,14 +477,17 @@
     lax.fori_loop(0, BLOCKS, block, 0, unroll=4)
 
 
-def first_weigh_body(after_ref, sums_ref, misfit_ref, out_ref):
+def first_scale_body(after_ref, sums_ref, out_ref):
     square_sum, counted = gathered_sums(sums_ref, 2)
-    weigh(misfit_ref, 1.0 / (square_sum / counted + 1e-06), out_ref)
-
-
-def second_weigh_body(after_ref, sums_ref, steps_ref, misfit_ref, out_ref):
-    _, inverse = second_spread(sums_ref, steps_ref)
-    weigh(misfit_ref, inverse, out_ref)
+    out_ref[...] = jnp.broadcast_to(1.0 / (square_sum / counted + 1e-06), (1, 128))
+
+
+def second_scale_body(after_ref, sums_ref, steps_ref, out_ref):
+    out_ref[...] = jnp.broadcast_to(second_spread(sums_ref, steps_ref)[1], (1, 128))
+
+
+def weigh_body(after_ref, inverse_ref, misfit_ref, out_ref):
+    weigh(misfit_ref, inverse_ref[:, 0:1], out_ref)
 
 
 def finish_body(
@@ -579,7 +582,8 @@
     sums = to_all(sums)
     near, mid, far = call(first_force_body, nodes_shape, (sums, misfit, grads), "force_first", parts)
     below, above, under, over, pair = halo(near, mid, far)
-    (robust,) = call(first_weigh_body, [big], (pair, sums, misfit), "weigh_first")
+    (inverse,) = call(first_scale_body, [((1, 128), F32)], (near, sums), "scale_first")
+    (robust,) = call(weigh_body, [big], (pair, inverse, misfit), "weigh_first")
     change, steps, dir0 = call(
         first_move_body,
         [big, sums_shape, dir_shape],
@@ -596,7 +600,8 @@
         parts,
     )
     below, above, under, over, pair = halo(near, mid, far)
-    (robust,) = call(second_weigh_body, [big], (pair, sums, first, misfit), "weigh_second")
+    (inverse,) = call(second_scale_body, [((1, 128), F32)], (near, sums, first), "scale_second")
+    (robust,) = call(weigh_body, [big], (pair, inverse, misfit), "weigh_second")
     change, steps, dir1 = call(
         second_move_body,
         [big, sums_shape, dir_shape],

time: 108 us -> 107 us (level)
  waiting for transfers between devices: 14.7 us -> 9.67 us
  blocking collectives: 74.1 us -> 76.3 us
  starting transfers between devices: 5.12 us -> 6.66 us
    ppermute x8, waiting for transfers between devices: 14.7 us -> 9.67 us  [swap(): return lax.ppermute(block, axis, route)]
    all_to_all x3, blocking collectives: 48.3 us -> 50.6 us  [to_all(): return lax.all_to_all(sums, EVERY, 0, 0, tiled=True)]
    ppermute x8, starting transfers between devices: 5.12 us -> 6.66 us  [swap(): return lax.ppermute(block, axis, route)]
    pallas_call x12 -> x14, Pallas kernels: 12.8 us -> 13.8 us  [call(): pl.pallas_call(body, out_shape=[jax.ShapeDtypeStruct(s, d) for s, d in ou...]
  transfers between devices with their start and end apart: 8 -> 8, of which waited for: 6 -> 4; matrix products, arithmetic and copies ran while one was open for 0% -> 0% of each run, Pallas kernels for 1% -> 2%
where the time goes in v7:
time: 107 us
  blocking collectives  76.3 us (71%)
  Pallas kernels  13.8 us (13%)
  waiting for transfers between devices  9.67 us (9%)
  starting transfers between devices  6.66 us (6%)
    all_to_all x3, blocking collectives, to_all(): return lax.all_to_all(sums, EVERY, 0, 0, tiled=True)  50.6 us
    all_to_all x1, blocking collectives, shards(): asked = lax.all_to_all(want, 'slab', 0, 0, tiled=True)  13.8 us
    pallas_call x14, Pallas kernels, call(): pl.pallas_call(body, out_shape=[jax.ShapeDtypeStruct(s, d) for s, d in ou...  13.8 us
    all_to_all x1, blocking collectives, shards(): recv = lax.all_to_all(sent, 'slab', 0, 0, tiled=True)  11.9 us
    ppermute x8, waiting for transfers between devices, swap(): return lax.ppermute(block, axis, route)  9.67 us
    ppermute x8, starting transfers between devices, swap(): return lax.ppermute(block, axis, route)  6.66 us
  transfers between devices with their start and end apart: 8, of which 4 were waited for; matrix products, arithmetic and copies ran while one was open for 0% of the time, Pallas kernels for 2%

profile of v7, /device:TPU:1, one launch (start us, length us, event | category | flops | bytes accessed | tf_op | source)
XLA Modules:
  0.0 107.1 jit_solution(11223591380668842730)
XLA Ops:
  0.6 1.3 %wanted.1 = (f32[512,128]{1,0:T(8,128)S(1)}, s32[16,128]{1,0:T(8,128)S(1)}, bf16[512,512]{1,0:T(8,128)(2,1)S(1)}, bf16[128,384]{1,0:T(8,128)(2,1)S(1)}, bf16[256...) custom-call(s32[2,2,128]{2,1,0:T(2,128)} %src_hbm.1, bf16[512,512]{1,0:T(8,128)(2,1)} %bitcast.41), custom_call_target="tpu_custom_call" | custom-call | tf_op jit(solution)/shard_map/wanted/pallas_call | solution.py:32
  1.9 13.8 %all_to_all.55 = s32[16,1,128]{2,1,0:T(1,128)S(1)} all-to-all(s32[16,1,128]{2,1,0:T(1,128)S(1)} %bitcast.37), channel_id=1, replica_groups=mesh['slab'=16,'grp'=8] {'slab'}, dimensions={0} | all-to-all | bytes 16384 | tf_op jit(solution)/shard_map/all_to_all | solution.py:562
  15.7 0.5 pick.1
  16.2 11.9 %all_to_all.56 = bf16[16,32,512]{2,1,0:T(8,128)(2,1)S(1)} all-to-all(bf16[16,32,512]{2,1,0:T(8,128)(2,1)S(1)} %bitcast.24), channel_id=1, replica_groups=mesh['slab'=16,'grp'=8] {'slab'}, dimensions={0} | all-to-all | bytes 1048576 | tf_op jit(solution)/shard_map/all_to_all | solution.py:564
  28.1 3.6 %warp.1 = (f32[3,512,512]{2,1,0:T(8,128)S(1)}, f32[512,512]{1,0:T(8,128)S(1)}, f32[128,128]{1,0:T(8,128)S(1)}) custom-call(f32[512,128]{1,0:T(8,128)S(1)} %get-tuple-element.31.pos_ref, bf16[512,512]{1,0:T(8,128)(2,1)S(1)} %bitcast.23, bf16[128,384]{1,0:T(8,128)(2,1)S(1)} %get-tuple-element.34.level_ref, bf16[256,512]{1,0:T(8,128)(2,1)S(1)} %get-tuple-element.35.inner_ref, ...), custom_call_target="tpu_custom_call" | custom-call | tf_op jit(solution)/shard_map/warp/pallas_call | solution.py:32
  31.8 18.9 %all_to_all.57 = f32[128,1,128]{2,1,0:T(1,128)S(1)} all-to-all(f32[128,1,128]{2,1,0:T(1,128)S(1)} %bitcast.35), channel_id=1, replica_groups=mesh['slab'=16,'grp'=8] {'slab','grp'}, dimensions={0} | all-to-all | bytes 131072 | tf_op jit(solution)/shard_map/all_to_all | solution.py:522
  50.6 1.5 %force_first.1 = (f32[9,128]{1,0:T(8,128)S(1)}, f32[9,128]{1,0:T(8,128)S(1)}, f32[9,128]{1,0:T(8,128)S(1)}) custom-call(f32[128,128]{1,0:T(8,128)S(1)} %bitcast.25, f32[512,512]{1,0:T(8,128)S(1)} %get-tuple-element.39.misfit_ref, f32[3,512,512]{2,1,0:T(8,128)S(1)} %get-tuple-element.40.grad_ref), custom_call_target="tpu_custom_call" | custom-call | tf_op jit(solution)/shard_map/force_first/pallas_call | solution.py:32
  52.2 1.3 %collective-permute-start.1 = (f32[9,128]{1,0:T(8,128)S(1)}, f32[9,128]{1,0:T(8,128)S(1)}, u32[]{:S(2)}, u32[]{:S(2)}) collective-permute-start(f32[9,128]{1,0:T(8,128)S(1)} %get-tuple-element.43.far_ref), channel_id=1, source_target_pairs={{1,2},{2,1},{3,4},{4,3},{5,6},{6,5},{7,0},{0,7},{9,10},{10,9},{11,... | collective-permute-start | bytes 13832 | tf_op jit(solution)/shard_map/ppermute | solution.py:518
  53.4 0.2 collective-permute-start
  53.7 1.6 %collective-permute-done.1.above_ref = f32[9,128]{1,0:T(8,128)S(1)} collective-permute-done((f32[9,128]{1,0:T(8,128)S(1)}, f32[9,128]{1,0:T(8,128)S(1)}, u32[]{:S(2)}, u32[]{:S(2)}) %collective-permute-start.1) | collective-permute-done | bytes 4640 | tf_op jit(solution)/shard_map/ppermute | solution.py:518
  55.3 0.0 collective-permute-done.below_ref
  55.3 1.8 %collective-permute-start.3 = (f32[9,128]{1,0:T(8,128)S(1)}, f32[9,128]{1,0:T(8,128)S(1)}, u32[]{:S(2)}, u32[]{:S(2)}) collective-permute-start(f32[9,128]{1,0:T(8,128)S(1)} %get-tuple-element.45), channel_id=1, source_target_pairs={{8,16},{16,8},{24,32},{32,24},{40,48},{48,40},{56,64},{64,56},{72,... | collective-permute-start | bytes 13832 | tf_op jit(solution)/shard_map/ppermute | solution.py:518
  57.1 0.0 collective-permute-start.2
  57.1 0.1 scale_first.1.inverse_ref
  57.2 0.8 weigh_first.1.robust_ref
  58.0 3.2 %collective-permute-done.3.over_ref = f32[9,128]{1,0:T(8,128)S(1)} collective-permute-done((f32[9,128]{1,0:T(8,128)S(1)}, f32[9,128]{1,0:T(8,128)S(1)}, u32[]{:S(2)}, u32[]{:S(2)}) %collective-permute-start.3) | collective-permute-done | bytes 4640 | tf_op jit(solution)/shard_map/ppermute | solution.py:518
  61.2 0.0 collective-permute-done.2.under_ref
  61.2 1.2 %move_first.1 = (f32[512,512]{1,0:T(8,128)S(1)}, f32[128,128]{1,0:T(8,128)S(1)}, f32[3,2,2,128]{3,2,1,0:T(2,128)S(1)}) custom-call(f32[9,128]{1,0:T(8,128)S(1)} %get-tuple-element.41.near_ref.after_ref, f32[9,128]{1,0:T(8,128)S(1)} %get-tuple-element.42.mid_ref, f32[9,128]{1,0:T(8,128)S(1)} %get-tuple-element.43.far_ref, ...), custom_call_target="tpu_custom_call" | custom-call | tf_op jit(solution)/shard_map/move_first/pallas_call | solution.py:32
  62.4 15.9 %all_to_all.58 = f32[128,1,128]{2,1,0:T(1,128)S(1)} all-to-all(f32[128,1,128]{2,1,0:T(1,128)S(1)} %bitcast.34), channel_id=1, replica_groups=mesh['slab'=16,'grp'=8] {'slab','grp'}, dimensions={0} | all-to-all | bytes 131072 | tf_op jit(solution)/shard_map/all_to_all | solution.py:522
  78.3 1.6 %force_second.1 = (f32[9,128]{1,0:T(8,128)S(1)}, f32[9,128]{1,0:T(8,128)S(1)}, f32[9,128]{1,0:T(8,128)S(1)}, f32[512,512]{1,0:T(8,128)S(1)}) custom-call(f32[128,128]{1,0:T(8,128)S(1)} %bitcast.27, f32[128,128]{1,0:T(8,128)S(1)} %bitcast.29, f32[512,512]{1,0:T(8,128)S(1)} %get-tuple-element.39.misfit_ref, f32[512,512]{1,0:T(8,128)S(1)} %get-tuple-element.47.change_ref, ...), custom_call_target="tpu_custom_call" | custom-call | tf_op jit(solution)/shard_map/force_second/pallas_call | solution.py:32
  79.9 1.3 %collective-permute-start.5 = (f32[9,128]{1,0:T(8,128)S(1)}, f32[9,128]{1,0:T(8,128)S(1)}, u32[]{:S(2)}, u32[]{:S(2)}) collective-permute-start(f32[9,128]{1,0:T(8,128)S(1)} %get-tuple-element.50.far_ref), channel_id=1, source_target_pairs={{1,2},{2,1},{3,4},{4,3},{5,6},{6,5},{7,0},{0,7},{9,10},{10,9},{11,... | collective-permute-start | bytes 13832 | tf_op jit(solution)/shard_map/ppermute | solution.py:518
  81.2 0.2 collective-permute-start.4
  81.4 1.6 %collective-permute-done.5.above_ref = f32[9,128]{1,0:T(8,128)S(1)} collective-permute-done((f32[9,128]{1,0:T(8,128)S(1)}, f32[9,128]{1,0:T(8,128)S(1)}, u32[]{:S(2)}, u32[]{:S(2)}) %collective-permute-start.5) | collective-permute-done | bytes 4640 | tf_op jit(solution)/shard_map/ppermute | solution.py:518
  83.1 0.0 collective-permute-done.4.below_ref
  83.1 1.8 %collective-permute-start.7 = (f32[9,128]{1,0:T(8,128)S(1)}, f32[9,128]{1,0:T(8,128)S(1)}, u32[]{:S(2)}, u32[]{:S(2)}) collective-permute-start(f32[9,128]{1,0:T(8,128)S(1)} %get-tuple-element.52), channel_id=1, source_target_pairs={{8,16},{16,8},{24,32},{32,24},{40,48},{48,40},{56,64},{64,56},{72,... | collective-permute-start | bytes 13832 | tf_op jit(solution)/shard_map/ppermute | solution.py:518
  84.9 0.0 collective-permute-start.6
  84.9 0.1 scale_second.1.inverse_ref
  85.0 0.8 weigh_second.1.robust_ref
  85.8 3.2 %collective-permute-done.7.over_ref = f32[9,128]{1,0:T(8,128)S(1)} collective-permute-done((f32[9,128]{1,0:T(8,128)S(1)}, f32[9,128]{1,0:T(8,128)S(1)}, u32[]{:S(2)}, u32[]{:S(2)}) %collective-permute-start.7) | collective-permute-done | bytes 4640 | tf_op jit(solution)/shard_map/ppermute | solution.py:518
  89.0 1.1 %move_second.1 = (f32[512,512]{1,0:T(8,128)S(1)}, f32[128,128]{1,0:T(8,128)S(1)}, f32[3,2,2,128]{3,2,1,0:T(2,128)S(1)}) custom-call(f32[9,128]{1,0:T(8,128)S(1)} %get-tuple-element.48.near_ref.after_ref, f32[9,128]{1,0:T(8,128)S(1)} %get-tuple-element.49.mid_ref, f32[9,128]{1,0:T(8,128)S(1)} %get-tuple-element.50.far_ref, ...), custom_call_target="tpu_custom_call" | custom-call | tf_op jit(solution)/shard_map/move_second/pallas_call | solution.py:32
  90.1 15.9 %all_to_all.59 = f32[128,1,128]{2,1,0:T(1,128)S(1)} all-to-all(f32[128,1,128]{2,1,0:T(1,128)S(1)} %bitcast.33), channel_id=1, replica_groups=mesh['slab'=16,'grp'=8] {'slab','grp'}, dimensions={0} | all-to-all | bytes 131072 | tf_op jit(solution)/shard_map/all_to_all | solution.py:522
  106.0 1.2 %finish.1 = (f32[3,2,2,128]{3,2,1,0:T(2,128)}, f32[512,512]{1,0:T(8,128)}) custom-call(f32[128,128]{1,0:T(8,128)S(1)} %bitcast.31, f32[128,128]{1,0:T(8,128)S(1)} %bitcast.32, f32[3,2,2,128]{3,2,1,0:T(2,128)S(1)} %get-tuple-element.55.dir0_ref, f32[3,2,2,128]{3,2,1,0:T(2,128)S(1)} %get-tuple-element.56.dir1_ref, ...), custom_call_target="tpu_custom_call" | custom-call | tf_op jit(solution)/shard_map/finish/pallas_call | solution.py:32
  (3 shorter events, 0.0 us)
Async XLA Ops:
  52.2 3.2 %collective-permute-start.1 = (f32[9,128]{1,0:T(8,128)S(1)}, f32[9,128]{1,0:T(8,128)S(1)}, u32[]{:S(2)}, u32[]{:S(2)}) collective-permute-start(f32[9,128]{1,0:T(8,128)S(1)} %get-tuple-element.43.far_ref), channel_id=1, source_target_pairs={{1,2},{2,1},{3,4},{4,3},{5,6},{6,5},{7,0},{0,7},{9,10},{10,9},{11,... | collective-permute-start | bytes 13832 | tf_op jit(solution)/shard_map/ppermute | solution.py:518
  53.4 1.9 %collective-permute-start = (f32[9,128]{1,0:T(8,128)S(1)}, f32[9,128]{1,0:T(8,128)S(1)}, u32[]{:S(2)}, u32[]{:S(2)}) collective-permute-start(f32[9,128]{1,0:T(8,128)S(1)} %get-tuple-element.41.near_ref.after_ref), channel_id=1, source_target_pairs={{0,1},{1,0},{2,3},{3,2},{4,5},{5,4},{6,7},{7,6},{8,9},{9,8},{10,11... | collective-permute-start | bytes 13832 | tf_op jit(solution)/shard_map/ppermute | solution.py:518
  55.3 5.9 %collective-permute-start.3 = (f32[9,128]{1,0:T(8,128)S(1)}, f32[9,128]{1,0:T(8,128)S(1)}, u32[]{:S(2)}, u32[]{:S(2)}) collective-permute-start(f32[9,128]{1,0:T(8,128)S(1)} %get-tuple-element.45), channel_id=1, source_target_pairs={{8,16},{16,8},{24,32},{32,24},{40,48},{48,40},{56,64},{64,56},{72,... | collective-permute-start | bytes 13832 | tf_op jit(solution)/shard_map/ppermute | solution.py:518
  57.1 4.1 %collective-permute-start.2 = (f32[9,128]{1,0:T(8,128)S(1)}, f32[9,128]{1,0:T(8,128)S(1)}, u32[]{:S(2)}, u32[]{:S(2)}) collective-permute-start(f32[9,128]{1,0:T(8,128)S(1)} %get-tuple-element.44.after_ref), channel_id=1, source_target_pairs={{0,8},{8,0},{16,24},{24,16},{32,40},{40,32},{48,56},{56,48},{64,72... | collective-permute-start | bytes 13832 | tf_op jit(solution)/shard_map/ppermute | solution.py:518
  79.9 3.2 %collective-permute-start.5 = (f32[9,128]{1,0:T(8,128)S(1)}, f32[9,128]{1,0:T(8,128)S(1)}, u32[]{:S(2)}, u32[]{:S(2)}) collective-permute-start(f32[9,128]{1,0:T(8,128)S(1)} %get-tuple-element.50.far_ref), channel_id=1, source_target_pairs={{1,2},{2,1},{3,4},{4,3},{5,6},{6,5},{7,0},{0,7},{9,10},{10,9},{11,... | collective-permute-start | bytes 13832 | tf_op jit(solution)/shard_map/ppermute | solution.py:518
  81.2 1.9 %collective-permute-start.4 = (f32[9,128]{1,0:T(8,128)S(1)}, f32[9,128]{1,0:T(8,128)S(1)}, u32[]{:S(2)}, u32[]{:S(2)}) collective-permute-start(f32[9,128]{1,0:T(8,128)S(1)} %get-tuple-element.48.near_ref.after_ref), channel_id=1, source_target_pairs={{0,1},{1,0},{2,3},{3,2},{4,5},{5,4},{6,7},{7,6},{8,9},{9,8},{10,11... | collective-permute-start | bytes 13832 | tf_op jit(solution)/shard_map/ppermute | solution.py:518
  83.1 5.9 %collective-permute-start.7 = (f32[9,128]{1,0:T(8,128)S(1)}, f32[9,128]{1,0:T(8,128)S(1)}, u32[]{:S(2)}, u32[]{:S(2)}) collective-permute-start(f32[9,128]{1,0:T(8,128)S(1)} %get-tuple-element.52), channel_id=1, source_target_pairs={{8,16},{16,8},{24,32},{32,24},{40,48},{48,40},{56,64},{64,56},{72,... | collective-permute-start | bytes 13832 | tf_op jit(solution)/shard_map/ppermute | solution.py:518
  84.9 4.1 %collective-permute-start.6 = (f32[9,128]{1,0:T(8,128)S(1)}, f32[9,128]{1,0:T(8,128)S(1)}, u32[]{:S(2)}, u32[]{:S(2)}) collective-permute-start(f32[9,128]{1,0:T(8,128)S(1)} %get-tuple-element.51.after_ref), channel_id=1, source_target_pairs={{0,8},{8,0},{16,24},{24,16},{32,40},{40,32},{48,56},{56,48},{64,72... | collective-permute-start | bytes 13832 | tf_op jit(solution)/shard_map/ppermute | solution.py:518

commit v8 on v6

--- a/solution.py
+++ b/solution.py
@@ -86,10 +86,11 @@
 def pick_body(want_ref, bricks_ref, out_ref):
     bricks = bricks_ref[...]
     rows = iota((CELLS, 128), 0)
+    picks = []
     for r in range(4):
         index = jnp.sum(want_ref[pl.ds(4 * r, 4), :], axis=0, keepdims=True)
-        chosen = jnp.where(rows == index, 1.0, 0.0).astype(BF16)
-        out_ref[pl.ds(128 * r, 128), :] = dot(chosen, bricks, TN).astype(BF16)
+        picks.append(jnp.where(rows == index, 1.0, 0.0).astype(BF16))
+    out_ref[...] = dot(jnp.concatenate(picks, axis=1), bricks, TN).astype(BF16)
 
 
 def columns(j):

time: 108 us -> 108 us (level)
  no operation moved by 1% of the time
where the time goes in v8:
time: 108 us; the launch traced here: 107 us
  blocking collectives  74.1 us (69%)
  waiting for transfers between devices  14.7 us (14%)
  Pallas kernels  12.8 us (12%)
  starting transfers between devices  5.12 us (5%)
    all_to_all x3, blocking collectives, to_all(): return lax.all_to_all(sums, EVERY, 0, 0, tiled=True)  48.3 us
    ppermute x8, waiting for transfers between devices, swap(): return lax.ppermute(block, axis, route)  14.7 us
    all_to_all x1, blocking collectives, shards(): asked = lax.all_to_all(want, 'slab', 0, 0, tiled=True)  13.8 us
    pallas_call x12, Pallas kernels, call(): pl.pallas_call(body, out_shape=[jax.ShapeDtypeStruct(s, d) for s, d in ou...  12.8 us
    all_to_all x1, blocking collectives, shards(): recv = lax.all_to_all(sent, 'slab', 0, 0, tiled=True)  11.9 us
    ppermute x8, starting transfers between devices, swap(): return lax.ppermute(block, axis, route)  5.12 us
  transfers between devices with their start and end apart: 8, of which 6 were waited for; matrix products, arithmetic and copies ran while one was open for 0% of the time, Pallas kernels for 1%

profile of v8, /device:TPU:1, one launch (start us, length us, event | category | flops | bytes accessed | tf_op | source)
XLA Modules:
  0.0 107.3 jit_solution(14018679970460070406)
XLA Ops:
  0.6 1.3 %wanted.1 = (f32[512,128]{1,0:T(8,128)S(1)}, s32[16,128]{1,0:T(8,128)S(1)}, bf16[512,512]{1,0:T(8,128)(2,1)S(1)}, bf16[128,384]{1,0:T(8,128)(2,1)S(1)}, bf16[256...) custom-call(s32[2,2,128]{2,1,0:T(2,128)} %src_hbm.1, bf16[512,512]{1,0:T(8,128)(2,1)} %bitcast.41), custom_call_target="tpu_custom_call" | custom-call | tf_op jit(solution)/shard_map/wanted/pallas_call | solution.py:32
  1.9 13.8 %all_to_all.55 = s32[16,1,128]{2,1,0:T(1,128)S(1)} all-to-all(s32[16,1,128]{2,1,0:T(1,128)S(1)} %bitcast.37), channel_id=1, replica_groups=mesh['slab'=16,'grp'=8] {'slab'}, dimensions={0} | all-to-all | bytes 16384 | tf_op jit(solution)/shard_map/all_to_all | solution.py:560
  15.7 0.5 pick.1
  16.2 11.9 %all_to_all.56 = bf16[16,32,512]{2,1,0:T(8,128)(2,1)S(1)} all-to-all(bf16[16,32,512]{2,1,0:T(8,128)(2,1)S(1)} %bitcast.24), channel_id=1, replica_groups=mesh['slab'=16,'grp'=8] {'slab'}, dimensions={0} | all-to-all | bytes 1048576 | tf_op jit(solution)/shard_map/all_to_all | solution.py:562
  28.1 3.6 %warp.1 = (f32[3,512,512]{2,1,0:T(8,128)S(1)}, f32[512,512]{1,0:T(8,128)S(1)}, f32[128,128]{1,0:T(8,128)S(1)}) custom-call(f32[512,128]{1,0:T(8,128)S(1)} %get-tuple-element.31.pos_ref, bf16[512,512]{1,0:T(8,128)(2,1)S(1)} %bitcast.23, bf16[128,384]{1,0:T(8,128)(2,1)S(1)} %get-tuple-element.34.level_ref, bf16[256,512]{1,0:T(8,128)(2,1)S(1)} %get-tuple-element.35.inner_ref, ...), custom_call_target="tpu_custom_call" | custom-call | tf_op jit(solution)/shard_map/warp/pallas_call | solution.py:32
  31.8 18.9 %all_to_all.57 = f32[128,1,128]{2,1,0:T(1,128)S(1)} all-to-all(f32[128,1,128]{2,1,0:T(1,128)S(1)} %bitcast.35), channel_id=1, replica_groups=mesh['slab'=16,'grp'=8] {'slab','grp'}, dimensions={0} | all-to-all | bytes 131072 | tf_op jit(solution)/shard_map/all_to_all | solution.py:520
  50.6 1.5 %force_first.1 = (f32[9,128]{1,0:T(8,128)S(1)}, f32[9,128]{1,0:T(8,128)S(1)}, f32[9,128]{1,0:T(8,128)S(1)}) custom-call(f32[128,128]{1,0:T(8,128)S(1)} %bitcast.25, f32[512,512]{1,0:T(8,128)S(1)} %get-tuple-element.39.misfit_ref, f32[3,512,512]{2,1,0:T(8,128)S(1)} %get-tuple-element.40.grad_ref), custom_call_target="tpu_custom_call" | custom-call | tf_op jit(solution)/shard_map/force_first/pallas_call | solution.py:32
  52.2 1.3 %collective-permute-start = (f32[9,128]{1,0:T(8,128)S(1)}, f32[9,128]{1,0:T(8,128)S(1)}, u32[]{:S(2)}, u32[]{:S(2)}) collective-permute-start(f32[9,128]{1,0:T(8,128)S(1)} %get-tuple-element.41.near_ref), channel_id=1, source_target_pairs={{0,1},{1,0},{2,3},{3,2},{4,5},{5,4},{6,7},{7,6},{8,9},{9,8},{10,11... | collective-permute-start | bytes 13832 | tf_op jit(solution)/shard_map/ppermute | solution.py:516
  53.5 0.1 collective-permute-start.1
  53.5 0.8 collective-permute-done.below_ref
  54.3 2.2 %collective-permute-done.1.above_ref = f32[9,128]{1,0:T(8,128)S(1)} collective-permute-done((f32[9,128]{1,0:T(8,128)S(1)}, f32[9,128]{1,0:T(8,128)S(1)}, u32[]{:S(2)}, u32[]{:S(2)}) %collective-permute-start.1) | collective-permute-done | bytes 4640 | tf_op jit(solution)/shard_map/ppermute | solution.py:516
  56.6 1.2 %collective-permute-start.3 = (f32[9,128]{1,0:T(8,128)S(1)}, f32[9,128]{1,0:T(8,128)S(1)}, u32[]{:S(2)}, u32[]{:S(2)}) collective-permute-start(f32[9,128]{1,0:T(8,128)S(1)} %get-tuple-element.45), channel_id=1, source_target_pairs={{8,16},{16,8},{24,32},{32,24},{40,48},{48,40},{56,64},{64,56},{72,... | collective-permute-start | bytes 13832 | tf_op jit(solution)/shard_map/ppermute | solution.py:516
  57.7 0.0 collective-permute-start.2
  57.7 0.4 weigh_first.1.robust_ref
  58.1 4.3 %collective-permute-done.3.over_ref = f32[9,128]{1,0:T(8,128)S(1)} collective-permute-done((f32[9,128]{1,0:T(8,128)S(1)}, f32[9,128]{1,0:T(8,128)S(1)}, u32[]{:S(2)}, u32[]{:S(2)}) %collective-permute-start.3) | collective-permute-done | bytes 4640 | tf_op jit(solution)/shard_map/ppermute | solution.py:516
  62.5 0.0 collective-permute-done.2.under_ref
  62.5 1.2 %move_first.1 = (f32[512,512]{1,0:T(8,128)S(1)}, f32[128,128]{1,0:T(8,128)S(1)}, f32[3,2,2,128]{3,2,1,0:T(2,128)S(1)}) custom-call(f32[9,128]{1,0:T(8,128)S(1)} %get-tuple-element.41.near_ref, f32[9,128]{1,0:T(8,128)S(1)} %get-tuple-element.42.mid_ref, f32[9,128]{1,0:T(8,128)S(1)} %get-tuple-element.43.far_ref, f32[9,128]{1,0:T(8,128)S(1)} %collective-permute-done.below_ref, ...), custom_call_target="tpu_custom_call" | custom-call | tf_op jit(solution)/shard_map/move_first/pallas_call | solution.py:32
  63.7 14.7 %all_to_all.58 = f32[128,1,128]{2,1,0:T(1,128)S(1)} all-to-all(f32[128,1,128]{2,1,0:T(1,128)S(1)} %bitcast.34), channel_id=1, replica_groups=mesh['slab'=16,'grp'=8] {'slab','grp'}, dimensions={0} | all-to-all | bytes 131072 | tf_op jit(solution)/shard_map/all_to_all | solution.py:520
  78.4 1.6 %force_second.1 = (f32[9,128]{1,0:T(8,128)S(1)}, f32[9,128]{1,0:T(8,128)S(1)}, f32[9,128]{1,0:T(8,128)S(1)}, f32[512,512]{1,0:T(8,128)S(1)}) custom-call(f32[128,128]{1,0:T(8,128)S(1)} %bitcast.27, f32[128,128]{1,0:T(8,128)S(1)} %bitcast.29, f32[512,512]{1,0:T(8,128)S(1)} %get-tuple-element.39.misfit_ref, f32[512,512]{1,0:T(8,128)S(1)} %get-tuple-element.47.change_ref, ...), custom_call_target="tpu_custom_call" | custom-call | tf_op jit(solution)/shard_map/force_second/pallas_call | solution.py:32
  80.0 1.3 %collective-permute-start.4 = (f32[9,128]{1,0:T(8,128)S(1)}, f32[9,128]{1,0:T(8,128)S(1)}, u32[]{:S(2)}, u32[]{:S(2)}) collective-permute-start(f32[9,128]{1,0:T(8,128)S(1)} %get-tuple-element.48.near_ref), channel_id=1, source_target_pairs={{0,1},{1,0},{2,3},{3,2},{4,5},{5,4},{6,7},{7,6},{8,9},{9,8},{10,11... | collective-permute-start | bytes 13832 | tf_op jit(solution)/shard_map/ppermute | solution.py:516
  81.3 0.1 collective-permute-start.5
  81.4 0.8 collective-permute-done.4.below_ref
  82.1 2.2 %collective-permute-done.5.above_ref = f32[9,128]{1,0:T(8,128)S(1)} collective-permute-done((f32[9,128]{1,0:T(8,128)S(1)}, f32[9,128]{1,0:T(8,128)S(1)}, u32[]{:S(2)}, u32[]{:S(2)}) %collective-permute-start.5) | collective-permute-done | bytes 4640 | tf_op jit(solution)/shard_map/ppermute | solution.py:516
  84.4 1.2 %collective-permute-start.7 = (f32[9,128]{1,0:T(8,128)S(1)}, f32[9,128]{1,0:T(8,128)S(1)}, u32[]{:S(2)}, u32[]{:S(2)}) collective-permute-start(f32[9,128]{1,0:T(8,128)S(1)} %get-tuple-element.52), channel_id=1, source_target_pairs={{8,16},{16,8},{24,32},{32,24},{40,48},{48,40},{56,64},{64,56},{72,... | collective-permute-start | bytes 13832 | tf_op jit(solution)/shard_map/ppermute | solution.py:516
  85.6 0.0 collective-permute-start.6
  85.6 0.4 weigh_second.1.robust_ref
  86.0 4.3 %collective-permute-done.7.over_ref = f32[9,128]{1,0:T(8,128)S(1)} collective-permute-done((f32[9,128]{1,0:T(8,128)S(1)}, f32[9,128]{1,0:T(8,128)S(1)}, u32[]{:S(2)}, u32[]{:S(2)}) %collective-permute-start.7) | collective-permute-done | bytes 4640 | tf_op jit(solution)/shard_map/ppermute | solution.py:516
  90.3 0.0 collective-permute-done.6.under_ref
  90.3 1.1 %move_second.1 = (f32[512,512]{1,0:T(8,128)S(1)}, f32[128,128]{1,0:T(8,128)S(1)}, f32[3,2,2,128]{3,2,1,0:T(2,128)S(1)}) custom-call(f32[9,128]{1,0:T(8,128)S(1)} %get-tuple-element.48.near_ref, f32[9,128]{1,0:T(8,128)S(1)} %get-tuple-element.49.mid_ref, f32[9,128]{1,0:T(8,128)S(1)} %get-tuple-element.50.far_ref, ...), custom_call_target="tpu_custom_call" | custom-call | tf_op jit(solution)/shard_map/move_second/pallas_call | solution.py:32
  91.4 14.7 %all_to_all.59 = f32[128,1,128]{2,1,0:T(1,128)S(1)} all-to-all(f32[128,1,128]{2,1,0:T(1,128)S(1)} %bitcast.33), channel_id=1, replica_groups=mesh['slab'=16,'grp'=8] {'slab','grp'}, dimensions={0} | all-to-all | bytes 131072 | tf_op jit(solution)/shard_map/all_to_all | solution.py:520
  106.2 1.2 %finish.1 = (f32[3,2,2,128]{3,2,1,0:T(2,128)}, f32[512,512]{1,0:T(8,128)}) custom-call(f32[128,128]{1,0:T(8,128)S(1)} %bitcast.31, f32[128,128]{1,0:T(8,128)S(1)} %bitcast.32, f32[3,2,2,128]{3,2,1,0:T(2,128)S(1)} %get-tuple-element.55.dir0_ref, f32[3,2,2,128]{3,2,1,0:T(2,128)S(1)} %get-tuple-element.56.dir1_ref, ...), custom_call_target="tpu_custom_call" | custom-call | tf_op jit(solution)/shard_map/finish/pallas_call | solution.py:32
  (2 shorter events, 0.0 us)
Async XLA Ops:
  52.2 2.1 %collective-permute-start = (f32[9,128]{1,0:T(8,128)S(1)}, f32[9,128]{1,0:T(8,128)S(1)}, u32[]{:S(2)}, u32[]{:S(2)}) collective-permute-start(f32[9,128]{1,0:T(8,128)S(1)} %get-tuple-element.41.near_ref), channel_id=1, source_target_pairs={{0,1},{1,0},{2,3},{3,2},{4,5},{5,4},{6,7},{7,6},{8,9},{9,8},{10,11... | collective-permute-start | bytes 13832 | tf_op jit(solution)/shard_map/ppermute | solution.py:516
  53.5 3.1 %collective-permute-start.1 = (f32[9,128]{1,0:T(8,128)S(1)}, f32[9,128]{1,0:T(8,128)S(1)}, u32[]{:S(2)}, u32[]{:S(2)}) collective-permute-start(f32[9,128]{1,0:T(8,128)S(1)} %get-tuple-element.43.far_ref), channel_id=1, source_target_pairs={{1,2},{2,1},{3,4},{4,3},{5,6},{6,5},{7,0},{0,7},{9,10},{10,9},{11,... | collective-permute-start | bytes 13832 | tf_op jit(solution)/shard_map/ppermute | solution.py:516
  56.6 5.9 %collective-permute-start.3 = (f32[9,128]{1,0:T(8,128)S(1)}, f32[9,128]{1,0:T(8,128)S(1)}, u32[]{:S(2)}, u32[]{:S(2)}) collective-permute-start(f32[9,128]{1,0:T(8,128)S(1)} %get-tuple-element.45), channel_id=1, source_target_pairs={{8,16},{16,8},{24,32},{32,24},{40,48},{48,40},{56,64},{64,56},{72,... | collective-permute-start | bytes 13832 | tf_op jit(solution)/shard_map/ppermute | solution.py:516
  57.7 4.7 %collective-permute-start.2 = (f32[9,128]{1,0:T(8,128)S(1)}, f32[9,128]{1,0:T(8,128)S(1)}, u32[]{:S(2)}, u32[]{:S(2)}) collective-permute-start(f32[9,128]{1,0:T(8,128)S(1)} %get-tuple-element.44.after_ref), channel_id=1, source_target_pairs={{0,8},{8,0},{16,24},{24,16},{32,40},{40,32},{48,56},{56,48},{64,72... | collective-permute-start | bytes 13832 | tf_op jit(solution)/shard_map/ppermute | solution.py:516
  80.0 2.1 %collective-permute-start.4 = (f32[9,128]{1,0:T(8,128)S(1)}, f32[9,128]{1,0:T(8,128)S(1)}, u32[]{:S(2)}, u32[]{:S(2)}) collective-permute-start(f32[9,128]{1,0:T(8,128)S(1)} %get-tuple-element.48.near_ref), channel_id=1, source_target_pairs={{0,1},{1,0},{2,3},{3,2},{4,5},{5,4},{6,7},{7,6},{8,9},{9,8},{10,11... | collective-permute-start | bytes 13832 | tf_op jit(solution)/shard_map/ppermute | solution.py:516
  81.3 3.1 %collective-permute-start.5 = (f32[9,128]{1,0:T(8,128)S(1)}, f32[9,128]{1,0:T(8,128)S(1)}, u32[]{:S(2)}, u32[]{:S(2)}) collective-permute-start(f32[9,128]{1,0:T(8,128)S(1)} %get-tuple-element.50.far_ref), channel_id=1, source_target_pairs={{1,2},{2,1},{3,4},{4,3},{5,6},{6,5},{7,0},{0,7},{9,10},{10,9},{11,... | collective-permute-start | bytes 13832 | tf_op jit(solution)/shard_map/ppermute | solution.py:516
  84.4 5.9 %collective-permute-start.7 = (f32[9,128]{1,0:T(8,128)S(1)}, f32[9,128]{1,0:T(8,128)S(1)}, u32[]{:S(2)}, u32[]{:S(2)}) collective-permute-start(f32[9,128]{1,0:T(8,128)S(1)} %get-tuple-element.52), channel_id=1, source_target_pairs={{8,16},{16,8},{24,32},{32,24},{40,48},{48,40},{56,64},{64,56},{72,... | collective-permute-start | bytes 13832 | tf_op jit(solution)/shard_map/ppermute | solution.py:516
  85.6 4.7 %collective-permute-start.6 = (f32[9,128]{1,0:T(8,128)S(1)}, f32[9,128]{1,0:T(8,128)S(1)}, u32[]{:S(2)}, u32[]{:S(2)}) collective-permute-start(f32[9,128]{1,0:T(8,128)S(1)} %get-tuple-element.51.after_ref), channel_id=1, source_target_pairs={{0,8},{8,0},{16,24},{24,16},{32,40},{40,32},{48,56},{56,48},{64,72... | collective-permute-start | bytes 13832 | tf_op jit(solution)/shard_map/ppermute | solution.py:516
